TPU v7x, 32 devices: a whole 2x2x4 slice. The times are simulated.
32 devices in a mesh: tm: 4 (over x, core), vox: 8 (over z, y).
Axes of the slice: x: 2, y: 2, z: 4, core: 2. Of those that a mesh axis runs over, the one named last changes fastest.
Arguments:
- clip_features: bfloat16 [1024, 1024], P('tm'), may hold values from -6 to 6
- depth_kernel: float32 [3, 1024], replicated, may hold values from -3.5 to 3.5
- point_weight: bfloat16 [1024, 1024], replicated, may hold values from -0.1875 to 0.1875
- session_lengths: int32 [8], replicated, may hold values from 1 to 256, 1024 in all
- subject_feature_gains: float32 [16, 1024], replicated, may hold values from 0.25 to 1.75
- readout_weight: bfloat16 [1024, 5120], P(None, 'vox'), may hold values from -0.1875 to 0.1875
- hrf_kernel: float32 [16, 5120], P(None, 'vox'), may hold values from -1.5 to 1.5
- block_subject: int32 [40], P('vox'), may hold values from 0 to 15, as said below
- block_live: int32 [40], P('vox'), may hold values from 0 to 128, as said below
- bold_target: bfloat16 [1024, 5120], P('tm', 'vox'), may hold values from -6 to 6
Outputs:
- loss_total: float32 [], replicated
- grad_readout: float32 [1024, 5120], P('tm', 'vox')
- grad_point: float32 [1024, 1024], P(None, 'vox')
Inputs may be any that keep to these rules, and one draw needn't show every extreme that they name: `session_lengths`: the lengths sum to 1024; one session has exactly 256 TRs. `block_subject`: ids never fall along the blocks; every subject owns one or two consecutive blocks, subject 0 two; the blocks after the last subject's live ones carry id 16 - 1 and no live voxels. `block_live`: the live voxels of a block are its first slots; a subject's blocks are full except its last, which holds at least one live voxel; blocks after the subjects' blocks are empty.
All inputs are finite; a program needn't handle non-finite values.
Results may differ from a plain program's by a relative error of at most 0.0044.
Values may be sent and summed in bfloat16 or wider, within the bound.
No kernel may reach another device: no remote copies, remote signals or barrier semaphores. Data moves between devices by JAX's collectives and lax.ppermute only.
A program may use at most 64 MiB of HBM per device.

v0:
```python
import jax
import jax.numpy as jnp
from jax import lax
from jax.sharding import PartitionSpec as P

BLOCK_VOX = 128
KERNEL_TAPS = 3
TAP_SPACING = 8
HRF = 16


def from_behind(value, axis, steps):
    count = lax.axis_size(axis)
    first, last = (max(0, -steps), min(count, count - steps))
    return lax.ppermute(value, axis, [(source, source + steps) for source in range(first, last)])


def session_of(session_ends, position):
    return jnp.sum((session_ends[None, :] <= position[:, None]).astype(jnp.int32), axis=1)


def live_block(operands):
    return jnp.dot(operands[0], operands[1], preferred_element_type=jnp.float32).astype(
        jnp.bfloat16
    )


def dead_block(operands):
    return jnp.zeros((operands[0].shape[0], operands[1].shape[1]), jnp.bfloat16)


def shards(
    clip_features,
    depth_kernel,
    point_weight,
    session_lengths,
    subject_feature_gains,
    readout_weight,
    hrf_kernel,
    block_subject,
    block_live,
    bold_target,
):
    local_rows = clip_features.shape[0]
    feature_count = clip_features.shape[1]
    slot_count = readout_weight.shape[1]
    block_count = slot_count // BLOCK_VOX
    subjects = subject_feature_gains.shape[0]
    total_rows = local_rows * lax.axis_size("tm")
    first_row = lax.axis_index("tm") * local_rows
    core_margin_rows = (KERNEL_TAPS - 1) * TAP_SPACING
    filter_rim = HRF - 1
    session_ends = jnp.cumsum(session_lengths)
    earlier = from_behind(clip_features[local_rows - core_margin_rows :], "tm", 1)
    extended = jnp.concatenate([earlier, clip_features], axis=0)
    ext_position = (
        first_row - core_margin_rows + jnp.arange(core_margin_rows + local_rows, dtype=jnp.int32)
    )
    ext_session = session_of(session_ends, ext_position)
    out_rows = core_margin_rows + local_rows - core_margin_rows
    out_session = ext_session[core_margin_rows:]
    depth_sum = jnp.zeros((out_rows, feature_count), jnp.float32)
    for kernel_tap_index in range(KERNEL_TAPS):
        shift_amount = core_margin_rows - kernel_tap_index * TAP_SPACING
        source = extended[shift_amount : shift_amount + out_rows].astype(jnp.float32)
        valid_tap = (ext_position[shift_amount : shift_amount + out_rows] >= 0) & (
            ext_session[shift_amount : shift_amount + out_rows] == out_session
        )
        depth_sum = depth_sum + depth_kernel[kernel_tap_index][None, :] * jnp.where(
            valid_tap[:, None], source, 0.0
        )
    depth_half = depth_sum.astype(jnp.bfloat16)
    pre_act = jnp.dot(depth_half, point_weight, preferred_element_type=jnp.float32)
    core_out = (extended[core_margin_rows:].astype(jnp.float32) + jax.nn.gelu(pre_act)).astype(
        jnp.bfloat16
    )
    one_hot = (block_subject[:, None] == jnp.arange(subjects, dtype=jnp.int32)[None, :]).astype(
        jnp.float32
    )
    gain_rows = jnp.dot(one_hot, subject_feature_gains, precision=lax.Precision.HIGHEST)
    scale_cols = jnp.transpose(gain_rows)[:, :, None]
    effective = (
        (
            readout_weight.astype(jnp.float32).reshape(feature_count, block_count, BLOCK_VOX)
            * scale_cols
        )
        .reshape(feature_count, slot_count)
        .astype(jnp.bfloat16)
    )
    pieces = []
    for block_index in range(block_count):
        weight_cols = effective[:, block_index * BLOCK_VOX : (block_index + 1) * BLOCK_VOX]
        pieces.append(
            lax.cond(block_live[block_index] > 0, live_block, dead_block, (core_out, weight_cols))
        )
    response = jnp.concatenate(pieces, axis=1)
    response_before = from_behind(response[local_rows - filter_rim :], "tm", 1)
    response_ext = jnp.concatenate([response_before, response], axis=0)
    filter_position = first_row - filter_rim + jnp.arange(filter_rim + local_rows, dtype=jnp.int32)
    filter_session = session_of(session_ends, filter_position)
    own_session = filter_session[filter_rim:]
    predicted = jnp.zeros((local_rows, slot_count), jnp.float32)
    for kernel_tap_index in range(HRF):
        shift_amount = filter_rim - kernel_tap_index
        source = response_ext[shift_amount : shift_amount + local_rows].astype(jnp.float32)
        valid_tap = (filter_position[shift_amount : shift_amount + local_rows] >= 0) & (
            filter_session[shift_amount : shift_amount + local_rows] == own_session
        )
        predicted = predicted + hrf_kernel[kernel_tap_index][None, :] * jnp.where(
            valid_tap[:, None], source, 0.0
        )
    local_counts = jnp.dot(block_live.astype(jnp.float32), one_hot, precision=lax.Precision.HIGHEST)
    subject_voxels = lax.psum(local_counts, "vox")
    block_voxels = jnp.dot(one_hot, subject_voxels, precision=lax.Precision.HIGHEST)
    live_mask = (
        (jnp.arange(BLOCK_VOX, dtype=jnp.int32)[None, :] < block_live[:, None])
        .astype(jnp.float32)
        .reshape(slot_count)
    )
    voxel_weight = live_mask / jnp.repeat(block_voxels, BLOCK_VOX)
    misfit = predicted - bold_target.astype(jnp.float32)
    partial_loss = jnp.sum(voxel_weight[None, :] * misfit * misfit)
    loss_total = lax.psum(partial_loss, ("tm", "vox")) / (subjects * total_rows)
    pred_grad = 2.0 * voxel_weight[None, :] * misfit
    later = from_behind(pred_grad[:filter_rim], "tm", -1)
    grad_ext = jnp.concatenate([pred_grad, later], axis=0)
    later_position = first_row + jnp.arange(local_rows + filter_rim, dtype=jnp.int32)
    later_session = session_of(session_ends, later_position)
    response_grad = jnp.zeros((local_rows, slot_count), jnp.float32)
    for kernel_tap_index in range(HRF):
        source = grad_ext[kernel_tap_index : kernel_tap_index + local_rows]
        valid_tap = (
            later_position[kernel_tap_index : kernel_tap_index + local_rows] < total_rows
        ) & (later_session[kernel_tap_index : kernel_tap_index + local_rows] == own_session)
        response_grad = response_grad + hrf_kernel[kernel_tap_index][None, :] * jnp.where(
            valid_tap[:, None], source, 0.0
        )
    response_half = response_grad.astype(jnp.bfloat16)
    raw_rows = lax.dot_general(
        core_out, response_half, (((0,), (0,)), ((), ())), preferred_element_type=jnp.float32
    )
    grad_readout = lax.psum_scatter(
        (
            raw_rows.reshape(
                lax.axis_size("tm") * (feature_count // lax.axis_size("tm")), block_count, BLOCK_VOX
            )
            * jnp.transpose(gain_rows)[:, :, None]
        ).reshape(lax.axis_size("tm") * (feature_count // lax.axis_size("tm")), slot_count),
        "tm",
        scatter_dimension=0,
        tiled=True,
    )
    share_width = feature_count // lax.axis_size("vox")
    col_start = lax.axis_index("vox") * share_width
    pre_cols = lax.dynamic_slice_in_dim(pre_act, col_start, share_width, 1)
    full_grad = lax.dot_general(
        response_half, effective, (((1,), (1,)), ((), ())), preferred_element_type=jnp.float32
    )
    summed_grad = lax.psum(full_grad, "vox")
    grad_cols = lax.dynamic_slice_in_dim(summed_grad, col_start, share_width, 1)
    pre_grad = jax.vjp(jax.nn.gelu, pre_cols)[1](grad_cols)[0].astype(jnp.bfloat16)
    point_part = lax.dot_general(
        depth_half, pre_grad, (((0,), (0,)), ((), ())), preferred_element_type=jnp.float32
    )
    grad_point = lax.psum(point_part, "tm")
    return (loss_total, grad_readout, grad_point)


def solution(mesh):
    placed = (
        P("tm", None),
        P(),
        P(),
        P(),
        P(),
        P(None, "vox"),
        P(None, "vox"),
        P("vox"),
        P("vox"),
        P("tm", "vox"),
    )
    return jax.shard_map(
        shards,
        mesh=mesh,
        in_specs=placed,
        out_specs=(P(), P("tm", "vox"), P(None, "vox")),
        check_vma=False,
    )
```

profile of v0, /device:TPU:0, one launch (start us, length us, event | category | flops | bytes accessed | tf_op | source)
XLA Modules:
  0.0 259.4 jit_solution(6205240970641587257)
XLA Ops:
  8.1 2.3 collective-permute-start
  15.5 22.5 %psum.28 = f32[16]{0:T(128)S(1)} all-reduce(f32[16]{0:T(128)S(1)} %convolution_bitcast_fusion.2), channel_id=1, replica_groups=mesh['tm'=4,'vox'=8] {'vox'}, use_global_device_ids=true, to_apply=%region_0.0 | all-reduce | flops 16 | bytes 128 | tf_op jit(solution)/shard_map/psum | solution.py:113
  42.3 1.5 fusion.119
  47.1 2.5 copy.21
  49.7 1.7 multiply_convert_fusion
  52.0 2.0 fusion.9
  54.0 2.8 %conditional.5 = (bf16[256,128]{1,0:T(8,128)(2,1)S(1)}) conditional(s32[]{:T(128)} %bitcast.5, () %tuple.38, (bf16[1024,640]{0,1:T(8,128)(2,1)S(1)}, bf16[256,1024]{1,0:T(8,128)(2,1)}) %tuple.45), branch_computations={%region_3.4_spmd, %region_4.5_spmd} | conditional | flops 67141632 | bytes 3473416 | solution.py:94
  54.0 1.5 copy.22
  57.5 2.8 %conditional.9 = (bf16[256,128]{1,0:T(8,128)(2,1)S(1)}) conditional(s32[]{:T(128)} %bitcast.16, () %tuple.43, (bf16[1024,640]{0,1:T(8,128)(2,1)S(1)}, bf16[256,1024]{1,0:T(8,128)(2,1)}) %tuple.45), branch_computations={%region_11.12_spmd, %region_12.13_spmd} | conditional | flops 67141632 | bytes 3473416 | solution.py:94
  57.5 1.5 copy.26
  60.4 3.5 %conditional.8 = (bf16[256,128]{1,0:T(8,128)(2,1)}) conditional(s32[]{:T(128)} %bitcast.15, () %tuple.42, (bf16[1024,640]{0,1:T(8,128)(2,1)S(1)}, bf16[256,1024]{1,0:T(8,128)(2,1)}) %tuple.45), branch_computations={%region_9.10_spmd, %region_10.11_spmd} | conditional | flops 67141632 | bytes 3473416 | solution.py:94
  60.4 1.5 copy.25
  61.9 2.0 convolution_convert_fusion.3
  63.9 3.5 %conditional.7 = (bf16[256,128]{1,0:T(8,128)(2,1)}) conditional(s32[]{:T(128)} %bitcast.14, () %tuple.41, (bf16[1024,640]{0,1:T(8,128)(2,1)S(1)}, bf16[256,1024]{1,0:T(8,128)(2,1)}) %tuple.45), branch_computations={%region_7.8_spmd, %region_8.9_spmd} | conditional | flops 67141632 | bytes 3473416 | solution.py:94
  65.3 2.0 convolution_convert_fusion.2
  67.4 3.5 %conditional.6 = (bf16[256,128]{1,0:T(8,128)(2,1)}) conditional(s32[]{:T(128)} %bitcast.13, () %tuple.40, (bf16[1024,640]{0,1:T(8,128)(2,1)S(1)}, bf16[256,1024]{1,0:T(8,128)(2,1)}) %tuple.45), branch_computations={%region_5.6_spmd, %region_6.7_spmd} | conditional | flops 67141632 | bytes 3473416 | solution.py:94
  68.8 2.0 convolution_convert_fusion.1
  70.8 1.5 constant_dynamic-update-slice_fusion.5
  72.3 1.5 constant_dynamic-update-slice_fusion.4
  73.8 1.5 constant_dynamic-update-slice_fusion.3
  79.3 9.5 %broadcast_multiply_fusion = (f32[256,640]{1,0:T(8,128)S(1)}, f32[256,640]{1,0:T(8,128)}) fusion(f32[640]{0:T(1024)S(1)} %broadcast_multiply_fusion.1, bf16[256,640]{1,0:T(8,128)(2,1)} %param.29, bf16[256,640]{1,0:T(8,128)(2,1)} %constant_dynamic-update-slice_fusion.2, bf16[15,640]{1,0:T(8,128)(2,1)S(1)} %collective-permute-done.1, ...), kind=kLoop, calls=%fused_computation.154 | loop fusion | flops 18186240 | bytes 2032896 | tf_op jit(solution)/shard_map/mul | solution.py:124
  90.3 3.6 %collective-permute-done.2 = f32[15,640]{1,0:T(8,128)S(1)} collective-permute-done((f32[15,640]{1,0:T(8,128)S(1)}, f32[15,640]{1,0:T(8,128)S(1)}, u32[]{:S(2)}, u32[]{:S(2)}) %collective-permute-start.2) | collective-permute-done | bytes 38432 | tf_op jit(solution)/shard_map/ppermute | solution.py:15
  94.0 3.4 %fusion.23 = bf16[256,640]{1,0:T(8,128)(2,1)S(1)} fusion(f32[15,640]{1,0:T(8,128)S(1)} %collective-permute-done.2, f32[256,640]{1,0:T(8,128)S(1)} %get-tuple-element.91, f32[640]{0:T(1024)S(1)} %get-tuple-element.87, f32[640]{0:T(1024)S(1)} %get-tuple-element.88, f32[640]{0:T(1024)S(1)} %get-tuple-element.74, f32[640]{0:T(1024)S(1)} %get-tuple-element.75, ...), kind=kLoop, calls=%fused_computation.65 | loop fusion | flops 10321920 | bytes 1066496 | tf_op jit(solution)/shard_map/convert_element_type | solution.py:138
  98.2 1.6 fusion.120
  99.8 1.9 mul.406
  101.7 3.3 %copy.27 = f32[1024,640]{1,0:T(8,128)} copy(f32[1024,640]{0,1:T(8,128)} %bitcast.41) | data formatting | bytes 5242880 | tf_op jit(solution)/shard_map/mul | solution.py:84
  104.9 71.6 %all-reduce.3.cloned.1.call-done = f32[256,1024]{1,0:T(8,128)} async-done(((f32[256,1024]{1,0:T(8,128)}), f32[256,1024]{1,0:T(8,128)}) %all-reduce.3.cloned.1.call-update) | async-done | bytes 1048592 | tf_op jit(solution)/shard_map/psum | solution.py:159
  176.5 2.1 fusion.99
  178.8 4.0 %convolution_multiply_fusion = f32[1024,640]{1,0:T(8,128)} fusion(f32[1024,640]{1,0:T(8,128)} %copy.27, bf16[256,1024]{1,0:T(8,128)(2,1)} %get-tuple-element.136, bf16[256,640]{1,0:T(8,128)(2,1)S(1)} %copy-done.2), kind=kOutput, calls=%fused_computation.39 | convolution fusion | flops 336199680 | bytes 6094848 | tf_op jit(solution)/shard_map/dot_general | solution.py:139
  184.7 39.8 %psum.29 = f32[]{:T(128)} all-reduce(f32[]{:T(128)} %fusion.17), channel_id=1, replica_groups=mesh['tm'=4,'vox'=8] {'tm','vox'}, use_global_device_ids=true, to_apply=%region_15.16 | all-reduce | flops 1 | bytes 8 | tf_op jit(solution)/shard_map/psum | solution.py:123
  225.2 24.7 %reduce-scatter.2.cloned.1.call-done = f32[256,640]{1,0:T(8,128)} async-done(((f32[1024,640]{1,0:T(8,128)}), f32[256,640]{1,0:T(8,128)}) %reduce-scatter.2.cloned.1.call-update) | async-done | bytes 655376 | tf_op jit(solution)/shard_map/reduce_scatter | solution.py:142
  249.9 1.9 copy.45
  (83 shorter events, 25.3 us)
Async XLA Ops:
  7.2 44.8 %copy-start = (bf16[1024,1024]{1,0:T(8,128)(2,1)S(1)}, bf16[1024,1024]{1,0:T(8,128)(2,1)}, u32[]{:S(2)}) copy-start(bf16[1024,1024]{1,0:T(8,128)(2,1)} %param.22) | copy-start | bytes 6291460
  7.2 169.4 %all-reduce.3.cloned.1.call-start = ((), (), s32[]{:S(2)}) async-start(), calls=%async_computation.2 | async-start | bytes 2097152 | tf_op jit(solution)/shard_map/psum | solution.py:159
  8.1 43.2 %collective-permute-start = (bf16[16,1024]{1,0:T(8,128)(2,1)S(1)}, bf16[16,1024]{1,0:T(8,128)(2,1)S(1)}, u32[]{:S(2)}, u32[]{:S(2)}) collective-permute-start(bf16[16,1024]{1,0:T(8,128)(2,1)S(1)} %slice.434), channel_id=1, source_target_pairs={{0,8},{8,16},{16,24},{1,9},{9,17},{17,25},{2,10},{10,18},{18,26},{... | collective-permute-start | bytes 98312 | tf_op jit(solution)/shard_map/ppermute | solution.py:15
  38.9 0.8 copy-start.18
  49.6 1.7 copy-start.4
  49.6 1.8 copy-start.15
  49.6 1.8 copy-start.16
  49.7 1.8 copy-start.17
  52.0 2.1 copy-start.5
  73.8 20.1 %copy-start.8 = (pred[256]{0:T(512)(128)(4,1)S(1)}, pred[256]{0:T(512)(128)(4,1)}, u32[]{:S(2)}) copy-start(pred[256]{0:T(512)(128)(4,1)} %get-tuple-element.107) | copy-start | bytes 772
  73.8 20.1 %copy-start.9 = (pred[256]{0:T(512)(128)(4,1)S(1)}, pred[256]{0:T(512)(128)(4,1)}, u32[]{:S(2)}) copy-start(pred[256]{0:T(512)(128)(4,1)} %get-tuple-element.96) | copy-start | bytes 772
  73.8 20.1 %copy-start.10 = (pred[256]{0:T(512)(128)(4,1)S(1)}, pred[256]{0:T(512)(128)(4,1)}, u32[]{:S(2)}) copy-start(pred[256]{0:T(512)(128)(4,1)} %get-tuple-element.97) | copy-start | bytes 772
  73.8 20.1 %copy-start.11 = (pred[256]{0:T(512)(128)(4,1)S(1)}, pred[256]{0:T(512)(128)(4,1)}, u32[]{:S(2)}) copy-start(pred[256]{0:T(512)(128)(4,1)} %get-tuple-element.98) | copy-start | bytes 772
  73.8 20.1 %copy-start.12 = (pred[256]{0:T(512)(128)(4,1)S(1)}, pred[256]{0:T(512)(128)(4,1)}, u32[]{:S(2)}) copy-start(pred[256]{0:T(512)(128)(4,1)} %get-tuple-element.99) | copy-start | bytes 772
  73.8 20.1 %copy-start.13 = (pred[256]{0:T(512)(128)(4,1)S(1)}, pred[256]{0:T(512)(128)(4,1)}, u32[]{:S(2)}) copy-start(pred[256]{0:T(512)(128)(4,1)} %get-tuple-element.100) | copy-start | bytes 772
  73.8 20.1 %copy-start.14 = (pred[256]{0:T(512)(128)(4,1)S(1)}, pred[256]{0:T(512)(128)(4,1)}, u32[]{:S(2)}) copy-start(pred[256]{0:T(512)(128)(4,1)} %get-tuple-element.101) | copy-start | bytes 772
  76.7 2.6 %collective-permute-start.1 = (bf16[15,640]{1,0:T(8,128)(2,1)S(1)}, bf16[15,640]{1,0:T(8,128)(2,1)S(1)}, u32[]{:S(2)}, u32[]{:S(2)}) collective-permute-start(bf16[15,640]{1,0:T(8,128)(2,1)S(1)} %slice.561), channel_id=1, source_target_pairs={{0,8},{8,16},{16,24},{1,9},{9,17},{17,25},{2,10},{10,18},{18,26},{... | collective-permute-start | bytes 57608 | tf_op jit(solution)/shard_map/ppermute | solution.py:15
  88.9 5.0 %collective-permute-start.2 = (f32[15,640]{1,0:T(8,128)S(1)}, f32[15,640]{1,0:T(8,128)S(1)}, u32[]{:S(2)}, u32[]{:S(2)}) collective-permute-start(f32[15,640]{1,0:T(8,128)S(1)} %slice.590), channel_id=1, source_target_pairs={{8,0},{16,8},{24,16},{9,1},{17,9},{25,17},{10,2},{18,10},{26,18},{... | collective-permute-start | bytes 115208 | tf_op jit(solution)/shard_map/ppermute | solution.py:15
  97.4 0.8 copy-start.1
  99.7 125.5 %all-reduce.5.cloned.1.call-start = ((), (), s32[]{:S(2)}) async-start(), calls=%async_computation.3 | async-start | bytes 1048576 | tf_op jit(solution)/shard_map/psum | solution.py:165
  101.7 74.9 %copy-start.6 = (bf16[256,1024]{1,0:T(8,128)(2,1)S(1)}, bf16[256,1024]{1,0:T(8,128)(2,1)}, u32[]{:S(2)}) copy-start(bf16[256,1024]{1,0:T(8,128)(2,1)} %copy-done.5) | copy-start | bytes 1572868
  104.9 73.8 %copy-start.2 = (bf16[256,640]{1,0:T(8,128)(2,1)S(1)}, bf16[256,640]{1,0:T(8,128)(2,1)}, u32[]{:S(2)}) copy-start(bf16[256,640]{1,0:T(8,128)(2,1)} %copy-done.1) | copy-start | bytes 983044
  178.7 71.2 %reduce-scatter.2.cloned.1.call-start = ((), (), s32[]{:S(2)}) async-start(), calls=%async_computation.1 | async-start | bytes 3276800 | tf_op jit(solution)/shard_map/reduce_scatter | solution.py:142
  182.8 0.7 copy-start.7
  182.8 0.7 copy-start.19
  182.8 1.1 copy-start.3
Sparse Core Ops, SparseCore 0:
  99.9 76.6 all-reduce.2
  179.0 32.8 all-reduce.4
  215.2 34.6 reduce-scatter.1
where the time goes:
time: 261 us; the launch traced here: 259 us
  waiting for transfers between devices  100 us (38%)
  blocking collectives  62.3 us (24%)
  local copies, waits for them, and re-layouts  29.8 us (11%)
  other arithmetic  21.8 us (8%)
  matrix products  21.4 us (8%)
  between operations  19.2 us (7%)
  starting transfers between devices  5.04 us (2%)
    psum x1, waiting for transfers between devices, shards(): summed_grad = lax.psum(full_grad, 'vox')  71.6 us
    psum x1, blocking collectives, shards(): loss_total = lax.psum(partial_loss, ('tm', 'vox')) / (subjects * total_rows)  39.8 us
    reduce_scatter x1, waiting for transfers between devices, shards(): lax.psum_scatter((raw_rows.reshape(lax.axis_size('tm') * (feature_count /...  24.7 us
    psum x1, blocking collectives, shards(): subject_voxels = lax.psum(local_counts, 'vox')  22.5 us
    unnamed x47, local copies, waits for them, and re-layouts  11.3 us
    mul x2, other arithmetic, shards(): pred_grad = 2.0 * voxel_weight[None, :] * misfit  10.3 us
    dot_general x5, matrix products, live_block(): jnp.dot(operands[0], operands[1], preferred_element_type=jnp.float32)  8.82 us
    another operation x5, local copies, waits for them, and re-layouts  7.27 us
  transfers between devices with their start and end apart: 6, of which 3 were waited for; matrix products, arithmetic and copies ran while one was open for 10% of the time, Pallas kernels for 0%

commit v1 on v0

v1 whole, which is shorter than its diff:
```python
import functools
import jax
import jax.numpy as jnp
from jax import lax
from jax.experimental import pallas as pl
from jax.experimental.pallas import tpu as pltpu
from jax.sharding import PartitionSpec as P

BLOCK_VOX = 128
KERNEL_TAPS = 3
TAP_SPACING = 8
HRF = 16
MARGIN = (KERNEL_TAPS - 1) * TAP_SPACING
F32 = jnp.float32
BF16 = jnp.bfloat16
NT = (((1,), (1,)), ((), ()))
VMEM = pl.BlockSpec(memory_space=pltpu.VMEM)
SMEM = pl.BlockSpec(memory_space=pltpu.SMEM)


def call(body, outs, ins, flops, moved, scratch=()):
    return pl.pallas_call(
        body,
        out_shape=outs,
        in_specs=[spec for spec, _ in ins],
        out_specs=jax.tree.map(lambda _: VMEM, outs),
        scratch_shapes=scratch,
        compiler_params=pltpu.CompilerParams(vmem_limit_bytes=40 << 20),
        cost_estimate=pl.CostEstimate(flops=flops, bytes_accessed=moved, transcendentals=0),
    )(*[value for _, value in ins])


def session_starts(lengths_ref, time):
    start = jnp.zeros_like(time)
    end = jnp.int32(0)
    for at in range(lengths_ref.shape[0]):
        end = end + lengths_ref[at]
        start = jnp.where(time >= end, end, start)
    return start


def session_stops(lengths_ref, time):
    stop = jnp.zeros_like(time)
    ends = []
    end = jnp.int32(0)
    for at in range(lengths_ref.shape[0]):
        end = end + lengths_ref[at]
        ends.append(end)
    for end in reversed(ends):
        stop = jnp.where(time < end, end, stop)
    return stop


def gain_kernel(blocks, subject_ref, gains_ref, weight_ref, effective_ref):
    rows = [gains_ref[pl.ds(subject_ref[b], 1), :] for b in range(blocks)]
    rows += [rows[-1]] * (-blocks % 8)
    cols = jnp.transpose(jnp.concatenate(rows, axis=0))
    for b in range(blocks):
        lanes = slice(b * BLOCK_VOX, (b + 1) * BLOCK_VOX)
        effective_ref[:, lanes] = (
            weight_ref[:, lanes].astype(F32) * cols[:, b : b + 1]
        ).astype(BF16)


def core_kernel(
    rows, lengths_ref, clip_ref, near_ref, far_ref, taps_ref, point_ref, depth_ref, core_ref, ext, deep
):
    feats = clip_ref.shape[1]
    odd = lax.axis_index("tm") % 2
    ext[2 * MARGIN : 2 * MARGIN + rows, :] = clip_ref[...]

    @pl.when(odd == 0)
    def _():
        ext[: 2 * MARGIN, :] = far_ref[: 2 * MARGIN, :]
        ext[2 * MARGIN + rows :, :] = near_ref[2 * MARGIN : 3 * MARGIN, :]

    @pl.when(odd == 1)
    def _():
        ext[: 2 * MARGIN, :] = near_ref[: 2 * MARGIN, :]
        ext[2 * MARGIN + rows :, :] = far_ref[2 * MARGIN : 3 * MARGIN, :]

    first = lax.axis_index("tm") * rows - MARGIN
    taps = [taps_ref[k : k + 1, :] for k in range(KERNEL_TAPS)]
    for at in range(0, rows + 2 * MARGIN, 16):
        time = first + at + lax.broadcasted_iota(jnp.int32, (16, 128), 0)
        since = time - session_starts(lengths_ref, time)
        values = ext[at : at + 32, :].astype(F32)
        total = taps[0] * values[16:32]
        for k in range(1, KERNEL_TAPS):
            valid = (since >= k * TAP_SPACING).astype(F32)
            shift = MARGIN - k * TAP_SPACING
            moved = values[shift : shift + 16] * jnp.tile(valid, (1, feats // 128))
            total = total + taps[k] * moved
        deep[at : at + 16, :] = total.astype(BF16)
    depth_ref[...] = deep[MARGIN : MARGIN + rows, :]
    for col in range(0, feats, 256):
        lanes = slice(col, col + 256)
        act = jnp.dot(deep[...], point_ref[:, lanes], preferred_element_type=F32)
        core_ref[:, lanes] = (
            ext[MARGIN : MARGIN + rows + 2 * MARGIN, lanes].astype(F32) + jax.nn.gelu(act)
        ).astype(BF16)


def block_at(position, bits):
    return sum(
        ((position >> (len(bits) - 1 - s)) & 1) << bits[s] for s in range(len(bits))
    )


def picked(position, orders):
    even, odd = (block_at(position, bits) for bits in orders)
    mask = jnp.where(lax.axis_index("tm") % 2 == 0, even, odd)
    return lax.axis_index("vox") ^ mask


def voxel_kernel(
    rows,
    blocks,
    orders,
    width,
    lengths_ref,
    own_ref,
    mine_ref,
    twin_ref,
    core_ref,
    effective_ref,
    hrf_ref,
    bold_ref,
    near_ref,
    far_ref,
    half_ref,
    send_ref,
    loss_ref,
    response,
    grads,
    bold,
    since,
    left,
    scale,
):
    ext_rows = rows + 2 * MARGIN
    lead_rows = rows + MARGIN
    slots = blocks * BLOCK_VOX
    odd = lax.axis_index("tm") % 2
    bold[:rows, :] = bold_ref[...]

    @pl.when(odd == 0)
    def _():
        bold[rows:, :] = near_ref[3 * MARGIN :, :slots]

    @pl.when(odd == 1)
    def _():
        bold[rows:, :] = far_ref[3 * MARGIN :, :slots]

    first = lax.axis_index("tm") * rows
    time = first + lax.broadcasted_iota(jnp.int32, (lead_rows, 128), 0)
    since[...] = time - session_starts(lengths_ref, time)
    left[...] = session_stops(lengths_ref, time) - 1 - time

    even_vox = lax.axis_index("vox") % 2 == 0
    zero_odd = odd == 0

    def neighbour(at):
        low = jnp.where(zero_odd, mine_ref[at], twin_ref[at])
        high = jnp.where(zero_odd, twin_ref[at], mine_ref[at])
        return low, high

    last_pair = [neighbour(blocks - 1), neighbour(2 * blocks - 1)]
    next_pair = [neighbour(0), neighbour(blocks)]
    before = [jnp.where(even_vox, high, low) for low, high in last_pair]
    after = [jnp.where(even_vox, low, high) for low, high in next_pair]
    subjects = [before[0]] + [own_ref[b] for b in range(blocks)] + [after[0]]
    lives = [before[1]] + [own_ref[blocks + b] for b in range(blocks)] + [after[1]]
    lane = lax.broadcasted_iota(jnp.int32, (16, BLOCK_VOX), 1)
    for b in range(blocks):
        count = lives[b + 1]
        count = count + jnp.where(subjects[b] == subjects[b + 1], lives[b], 0)
        count = count + jnp.where(subjects[b + 2] == subjects[b + 1], lives[b + 2], 0)
        counts = jnp.full((16, BLOCK_VOX), jnp.maximum(count, 1), jnp.int32).astype(F32)
        scale[b] = jnp.where(lane < lives[b + 1], 1.0 / counts, 0.0)

    for b in range(0, blocks, 2):
        many = min(2, blocks - b)
        lanes = slice(b * BLOCK_VOX, (b + many) * BLOCK_VOX)
        part = jnp.dot(core_ref[...], effective_ref[:, lanes], preferred_element_type=F32)
        part = part.astype(BF16).astype(F32)
        for c in range(many):
            response[b + c] = part[:, c * BLOCK_VOX : (c + 1) * BLOCK_VOX]

    def one_block(b, lost):
        lanes = pl.ds(pl.multiple_of(b * BLOCK_VOX, BLOCK_VOX), BLOCK_VOX)
        taps = [jnp.broadcast_to(hrf_ref[k : k + 1, lanes], (16, BLOCK_VOX)) for k in range(HRF)]
        weight = scale[b]
        double = 2.0 * weight
        for at in range(0, lead_rows, 16):
            depth = since[at : at + 16, :]
            total = taps[0] * response[b, MARGIN + at : MARGIN + at + 16, :]
            for k in range(1, HRF):
                moved = response[b, MARGIN + at - k : MARGIN + at - k + 16, :]
                total = total + taps[k] * jnp.where(depth >= k, moved, 0.0)
            misfit = total - bold[at : at + 16, lanes].astype(F32)
            grads[b, at : at + 16, :] = double * misfit
            if at < rows:
                cost = weight * misfit * misfit
                lost = lost + cost[:8] + cost[8:]
        for at in range(0, rows, 16):
            depth = left[at : at + 16, :]
            total = taps[0] * grads[b, at : at + 16, :]
            for k in range(1, HRF):
                moved = grads[b, at + k : at + k + 16, :]
                total = total + taps[k] * jnp.where(depth >= k, moved, 0.0)
            half_ref[at : at + 16, lanes] = total.astype(BF16)
        return lost

    lost = lax.fori_loop(0, blocks, one_block, jnp.zeros((8, BLOCK_VOX), F32))
    loss_ref[...] = lost
    high = lost.astype(BF16).astype(F32)
    pair = jnp.concatenate([high, lost - high], axis=0)
    pad = jnp.zeros((16, rows - BLOCK_VOX), F32)
    pieces = 1 << len(orders[0])
    halves = pieces // 2
    send_ref[halves * width :, :] = jnp.concatenate([pair, pad], axis=1).astype(BF16)
    for p in range(halves):
        at = pl.multiple_of(picked(halves + p, orders) * width, width)
        send_ref[p * width : (p + 1) * width, :] = lax.dot_general(
            effective_ref[pl.ds(at, width), :], half_ref[...], NT, preferred_element_type=F32
        ).astype(BF16)


def rest_kernel(
    rows, orders, width, tm_bits, share, core_ref, effective_ref, half_ref, keep_ref, out_ref, own_ref, flipped
):
    halves = 1 << (len(orders[0]) - 1)
    flipped[...] = jnp.transpose(core_ref[MARGIN : MARGIN + rows, :])
    pieces = 1 << len(tm_bits)
    for q in reversed(range(pieces)):
        at = pl.multiple_of((lax.axis_index("tm") ^ block_at(q, tm_bits)) * share, share)
        part = jnp.dot(flipped[pl.ds(at, share), :], half_ref[...], preferred_element_type=F32)
        if q >= pieces // 2:
            slot = q - pieces // 2
            out_ref[slot * share : (slot + 1) * share, :] = part.astype(BF16)
        else:
            own_ref[q * share : (q + 1) * share, :] = part
    for p in range(halves):
        at = pl.multiple_of(picked(p, orders) * width, width)
        keep_ref[p * width : (p + 1) * width, :] = lax.dot_general(
            effective_ref[pl.ds(at, width), :], half_ref[...], NT, preferred_element_type=F32
        )


def last_kernel(parts, width, grads_ref, *refs):
    depth_refs, (point_ref,) = refs[:parts], refs[parts:]
    feats = point_ref.shape[0]
    for col in range(0, feats, 256):
        lanes = slice(col, col + 256)
        total = None
        for r in range(parts):
            part = jnp.dot(
                grads_ref[r, :width, :], depth_refs[r][:, lanes], preferred_element_type=F32
            )
            total = part if total is None else total + part
        point_ref[lanes, :] = jnp.transpose(total)


def shards(
    tm_count,
    vox_count,
    clip_features,
    depth_kernel,
    point_weight,
    session_lengths,
    subject_feature_gains,
    readout_weight,
    hrf_kernel,
    block_subject,
    block_live,
    bold_target,
):
    rows, feats = clip_features.shape
    slots = readout_weight.shape[1]
    blocks = slots // BLOCK_VOX
    subjects = subject_feature_gains.shape[0]
    width = feats // vox_count
    share = feats // tm_count
    vox_bits = list(range(vox_count.bit_length() - 1))
    orders = (vox_bits, [vox_bits[1], vox_bits[0]] + vox_bits[2:])
    tm_bits = list(range(tm_count.bit_length() - 1))

    def swap_tm(value, bit):
        return lax.ppermute(value, "tm", [(i, i ^ (1 << bit)) for i in range(tm_count)])

    def across(value, partner):
        pairs = []
        for t in range(tm_count):
            for v in range(vox_count):
                to = partner(t, v)
                if to is not None:
                    pairs.append((t * vox_count + v, to[0] * vox_count + to[1]))
        return lax.ppermute(value, ("tm", "vox"), pairs)

    def next_tm(t, v):
        other = t + 1 if t % 2 else t - 1
        return (other, v) if 0 <= other < tm_count else None

    def next_vox(t, v):
        if t % 2 == 0:
            return (t, v ^ 1)
        other = v + 1 if v % 2 else v - 1
        return (t, other) if 0 <= other < vox_count else None

    payload = jnp.concatenate(
        [
            clip_features[rows - 2 * MARGIN :],
            clip_features[:MARGIN],
            jnp.pad(bold_target[:MARGIN], ((0, 0), (0, feats - slots))),
        ],
        axis=0,
    )
    far = across(payload, next_tm)
    own_blocks = jnp.concatenate([block_subject, block_live])
    mine = across(own_blocks, next_vox)
    near = swap_tm(payload, 0)
    twin = swap_tm(mine, 0)

    effective = call(
        functools.partial(gain_kernel, blocks),
        jax.ShapeDtypeStruct((feats, slots), BF16),
        [(SMEM, block_subject), (VMEM, subject_feature_gains), (VMEM, readout_weight)],
        feats * slots,
        4 * feats * slots,
    )
    depth_half, core_out = call(
        functools.partial(core_kernel, rows),
        (
            jax.ShapeDtypeStruct((rows, feats), BF16),
            jax.ShapeDtypeStruct((rows + 2 * MARGIN, feats), BF16),
        ),
        [
            (SMEM, session_lengths),
            (VMEM, clip_features),
            (VMEM, near),
            (VMEM, far),
            (VMEM, depth_kernel),
            (VMEM, point_weight),
        ],
        2 * rows * feats * feats,
        2 * feats * feats,
        [
            pltpu.VMEM((rows + 3 * MARGIN, feats), BF16),
            pltpu.VMEM((rows + 2 * MARGIN, feats), BF16),
        ],
    )
    half, send, lost = call(
        functools.partial(voxel_kernel, rows, blocks, orders, width),
        (
            jax.ShapeDtypeStruct((rows, slots), BF16),
            jax.ShapeDtypeStruct((feats // 2 + 16, rows), BF16),
            jax.ShapeDtypeStruct((8, BLOCK_VOX), F32),
        ),
        [
            (SMEM, session_lengths),
            (SMEM, own_blocks),
            (SMEM, mine),
            (SMEM, twin),
            (VMEM, core_out),
            (VMEM, effective),
            (VMEM, hrf_kernel),
            (VMEM, bold_target),
            (VMEM, near),
            (VMEM, far),
        ],
        4 * rows * feats * slots,
        8 * rows * slots,
        [
            pltpu.VMEM((blocks, rows + 2 * MARGIN, BLOCK_VOX), F32),
            pltpu.VMEM((blocks, rows + MARGIN, BLOCK_VOX), F32),
            pltpu.VMEM((rows + MARGIN, slots), BF16),
            pltpu.VMEM((rows + MARGIN, BLOCK_VOX), jnp.int32),
            pltpu.VMEM((rows + MARGIN, BLOCK_VOX), jnp.int32),
            pltpu.VMEM((blocks, 16, BLOCK_VOX), F32),
        ],
    )
    keep, raw_send, raw_keep = call(
        functools.partial(rest_kernel, rows, orders, width, tm_bits, share),
        (
            jax.ShapeDtypeStruct((feats // 2, rows), F32),
            jax.ShapeDtypeStruct((feats // 2, slots), BF16),
            jax.ShapeDtypeStruct((feats // 2, slots), F32),
        ),
        [(VMEM, core_out), (VMEM, effective), (VMEM, half)],
        4 * rows * feats * slots,
        8 * feats * slots,
        [pltpu.VMEM((feats, rows), BF16)],
    )

    def loss_rows(value):
        high = lax.reduce_precision(value, 8, 7)
        pair = jnp.concatenate([high, value - high], axis=0)
        return jnp.pad(pair, ((0, 0), (0, rows - BLOCK_VOX))).astype(BF16)

    def loss_of(arrived):
        pair = arrived[:, :BLOCK_VOX].astype(F32)
        return pair[:8] + pair[8:]

    for stage in range(len(vox_bits)):
        arrived = across(send, lambda t, v: (t, v ^ (1 << orders[t % 2][stage])))
        size = keep.shape[0]
        keep = keep + arrived[:size].astype(F32)
        lost = lost + loss_of(arrived[size:])
        if stage + 1 < len(vox_bits):
            send = jnp.concatenate([keep[size // 2 :].astype(BF16), loss_rows(lost)], axis=0)
            keep = keep[: size // 2]

    col = lax.axis_index("vox") * width
    point_cols = lax.dynamic_slice_in_dim(point_weight, col, width, 1)
    pre_act = lax.dot_general(
        point_cols, depth_half, (((0,), (1,)), ((), ())), preferred_element_type=F32
    )
    pre_grad = jax.vjp(jax.nn.gelu, pre_act)[1](keep)[0].astype(BF16)
    gathered = jnp.concatenate([pre_grad, loss_rows(lost)], axis=0)[None]
    depths = [depth_half]
    for bit in reversed(tm_bits):
        depths = depths + [swap_tm(value, bit) for value in depths]
        gathered = jnp.concatenate([gathered, swap_tm(gathered, bit)], axis=0)
    loss_sum = jnp.sum(gathered[:, width:, :BLOCK_VOX].astype(F32))
    loss_total = loss_sum / (subjects * rows * tm_count)
    grad_point = call(
        functools.partial(last_kernel, tm_count, width),
        jax.ShapeDtypeStruct((feats, width), F32),
        [(VMEM, gathered)] + [(VMEM, value) for value in depths],
        2 * rows * tm_count * feats * width,
        2 * rows * tm_count * feats,
    )

    for bit in tm_bits:
        arrived = swap_tm(raw_send, bit)
        raw_keep = raw_keep + arrived.astype(F32)
        if bit + 1 < len(tm_bits):
            size = raw_keep.shape[0] // 2
            raw_send = raw_keep[size:].astype(BF16)
            raw_keep = raw_keep[:size]
    own_gains = lax.dynamic_slice_in_dim(
        subject_feature_gains, lax.axis_index("tm") * share, share, 1
    )
    gain_cols = jnp.transpose(own_gains[block_subject])
    grad_readout = raw_keep * jnp.repeat(gain_cols, BLOCK_VOX, axis=1)
    return (loss_total, grad_readout, grad_point)


def solution(mesh):
    placed = (
        P("tm", None),
        P(),
        P(),
        P(),
        P(),
        P(None, "vox"),
        P(None, "vox"),
        P("vox"),
        P("vox"),
        P("tm", "vox"),
    )
    return jax.shard_map(
        functools.partial(shards, mesh.shape["tm"], mesh.shape["vox"]),
        mesh=mesh,
        in_specs=placed,
        out_specs=(P(), P("tm", "vox"), P(None, "vox")),
        check_vma=False,
    )
```

time: 261 us -> 71 us (0.27)
  waiting for transfers between devices: 100 us -> 19.5 us
  blocking collectives: 62.3 us -> 0 us
  local copies, waits for them, and re-layouts: 29.8 us -> 9.45 us
  matrix products: 21.4 us -> 1.52 us
  between operations: 19.2 us -> 2.68 us
  other arithmetic: 21.8 us -> 6.14 us
  starting transfers between devices: 5.04 us -> 19 us
  Pallas kernels: 0 us -> 12.1 us
    psum x2 -> x0, waiting for transfers between devices: 71.6 us -> none  [the longest x1 71.6 us: shards(): summed_grad = lax.psum(full_grad, 'vox')]
    psum x2 -> x0, blocking collectives: 62.3 us -> none  [the longest x1 39.8 us: shards(): loss_total = lax.psum(partial_loss, ('tm', 'vox')) / (subjects * total_rows)]
    reduce_scatter x1 -> x0, waiting for transfers between devices: 24.7 us -> none  [shards(): lax.psum_scatter((raw_rows.reshape(lax.axis_size('tm') * (feature_count /...]
    dot_general x12 -> x1, matrix products: 21.4 us -> 1.52 us  [shards(): lax.dot_general(point_cols, depth_half, (((0,), (1,)), ((), ())), preferr...]
    ppermute x3 -> x14, waiting for transfers between devices: 3.64 us -> 19.5 us  [the longest x9 11.5 us: swap_tm(): lax.ppermute(value, 'tm', [(i, i ^ 1 << bit) for i in range(tm_count)])]
    ppermute x3 -> x14, starting transfers between devices: 4.92 us -> 19 us  [the longest x5 14.4 us: across(): return lax.ppermute(value, ('tm', 'vox'), pairs)]
    pallas_call x0 -> x5, Pallas kernels: none -> 12.1 us  [call(): pl.pallas_call(body, out_shape=outs, in_specs=[spec for spec, _ in ins],...]
    mul x2 -> x1, other arithmetic: 10.3 us -> 2.13 us  [shards(): grad_readout = raw_keep * jnp.repeat(gain_cols, BLOCK_VOX, axis=1)]
  transfers between devices with their start and end apart: 6 -> 14, of which waited for: 3 -> 6; matrix products, arithmetic and copies ran while one was open for 10% -> 15% of each run, Pallas kernels for 0% -> 6%
where the time goes in v1:
time: 71 us; the launch traced here: 70.4 us
  waiting for transfers between devices  19.5 us (27%)
  starting transfers between devices  19 us (27%)
  Pallas kernels  12.1 us (17%)
  local copies, waits for them, and re-layouts  9.45 us (13%)
  other arithmetic  6.14 us (9%)
  between operations  2.68 us (4%)
  matrix products  1.52 us (2%)
    ppermute x5, starting transfers between devices, across(): return lax.ppermute(value, ('tm', 'vox'), pairs)  14.4 us
    pallas_call x5, Pallas kernels, call(): pl.pallas_call(body, out_shape=outs, in_specs=[spec for spec, _ in ins],...  12.1 us
    ppermute x9, waiting for transfers between devices, swap_tm(): lax.ppermute(value, 'tm', [(i, i ^ 1 << bit) for i in range(tm_count)])  11.5 us
    ppermute x5, waiting for transfers between devices, across(): return lax.ppermute(value, ('tm', 'vox'), pairs)  7.94 us
    ppermute x9, starting transfers between devices, swap_tm(): lax.ppermute(value, 'tm', [(i, i ^ 1 << bit) for i in range(tm_count)])  4.59 us
    unnamed x26, local copies, waits for them, and re-layouts  3.93 us
    mul x1, other arithmetic, shards(): grad_readout = raw_keep * jnp.repeat(gain_cols, BLOCK_VOX, axis=1)  2.13 us
    concatenate x2, other arithmetic, shards(): gathered = jnp.concatenate([gathered, swap_tm(gathered, bit)], axis=0)  1.62 us
  transfers between devices with their start and end apart: 14, of which 6 were waited for; matrix products, arithmetic and copies ran while one was open for 15% of the time, Pallas kernels for 6%

profile of v1, /device:TPU:0, one launch (start us, length us, event | category | flops | bytes accessed | tf_op | source)
XLA Modules:
  0.0 70.4 jit_solution(15396744825608315138)
XLA Ops:
  0.6 0.8 %slice.75 = bf16[32,1024]{1,0:T(8,128)(2,1)S(1)} slice(bf16[256,1024]{1,0:T(8,128)(2,1)} %clip_ref.1), slice={[224:256], [0:1024]} | slice | bytes 131072 | tf_op jit(solution)/shard_map/slice | solution.py:313
  1.5 0.8 %slice.76 = bf16[16,1024]{1,0:T(8,128)(2,1)S(1)} slice(bf16[256,1024]{1,0:T(8,128)(2,1)} %clip_ref.1), slice={[0:16], [0:1024]} | slice | bytes 65536 | tf_op jit(solution)/shard_map/slice | solution.py:314
  2.2 0.7 %slice.77 = bf16[16,640]{1,0:T(8,128)(2,1)S(1)} slice(bf16[256,640]{1,0:T(8,128)(2,1)} %bold_ref.1), slice={[0:16], [0:640]} | slice | bytes 40960 | tf_op jit(solution)/shard_map/slice | solution.py:315
  4.2 0.7 %pad_add_fusion.own_ref = s32[10]{0:T(128)S(1)} fusion(s32[5]{0:T(128)} %param.18, s32[5]{0:T(128)} %subject_ref.1), kind=kLoop, calls=%fused_computation.60 | loop fusion | flops 10 | bytes 80 | tf_op jit(solution)/shard_map/concatenate | solution.py:320
  4.9 4.6 %collective-permute-start.2 = (s32[10]{0:T(128)S(1)}, s32[10]{0:T(128)S(1)}, u32[]{:S(2)}, u32[]{:S(2)}) collective-permute-start(s32[10]{0:T(128)S(1)} %pad_add_fusion.own_ref), channel_id=1, source_target_pairs={{0,1},{1,0},{2,3},{3,2},{4,5},{5,4},{6,7},{7,6},{9,10},{10,9},{11,... | collective-permute-start | bytes 128 | tf_op jit(solution)/shard_map/ppermute | solution.py:299
  9.5 1.3 %copy-done.1 = bf16[1024,640]{1,0:T(8,128)(2,1)S(1)} copy-done((bf16[1024,640]{1,0:T(8,128)(2,1)S(1)}, bf16[1024,640]{1,0:T(8,128)(2,1)}, u32[]{:S(2)}) %copy-start.1) | copy-done | bytes 1310744
  10.8 0.8 %copy-done.4 = f32[16,1024]{1,0:T(8,128)S(1)} copy-done((f32[16,1024]{1,0:T(8,128)S(1)}, f32[16,1024]{1,0:T(8,128)}, u32[]{:S(2)}) %copy-start.4) | copy-done | bytes 65560
  12.3 1.5 %shard_map.122.effective_ref = bf16[1024,640]{1,0:T(8,128)(2,1)S(1)} custom-call(s32[5]{0:T(128)S(1)} %copy-done.8, f32[16,1024]{1,0:T(8,128)S(1)} %copy-done.4, bf16[1024,640]{1,0:T(8,128)(2,1)S(1)} %copy-done.1), custom_call_target="tpu_custom_call" | custom-call | flops 655360 | bytes 2621440 | tf_op jit(solution)/shard_map/pallas_call | solution.py:22
  14.0 1.9 %shard_map.121 = (bf16[256,1024]{1,0:T(8,128)(2,1)}, bf16[288,1024]{1,0:T(8,128)(2,1)S(1)}) custom-call(s32[8]{0:T(128)S(1)} %copy-done.7, bf16[256,1024]{1,0:T(8,128)(2,1)S(1)} %copy-done.2, bf16[64,1024]{1,0:T(8,128)(2,1)S(1)} %collective-permute-done.near_ref, bf16[64,1024]{1,0:T(8,128)(2,1)S(1)} %collective-permute-done.1.far_ref, ...), custom_call_target="tpu_custom_call" | custom-call | flops 536870912 | bytes 2097152 | tf_op jit(solution)/shard_map/pallas_call | solution.py:22
  16.0 5.1 %shard_map.123 = (bf16[256,640]{1,0:T(8,128)(2,1)S(1)}, bf16[528,256]{1,0:T(8,128)(2,1)S(1)}, f32[8,128]{1,0:T(8,128)S(1)}) custom-call(s32[8]{0:T(128)S(1)} %copy-done.7, s32[10]{0:T(128)S(1)} %pad_add_fusion.own_ref, s32[10]{0:T(128)S(1)} %collective-permute-done.2.mine_ref, s32[10]{0:T(128)S(1)} %collective-permute-done.3.twin_ref, ...), custom_call_target="tpu_custom_call" | custom-call | flops 671088640 | bytes 1310720 | tf_op jit(solution)/shard_map/pallas_call | solution.py:22
  21.0 4.1 %collective-permute-start.4 = (bf16[528,256]{1,0:T(8,128)(2,1)S(1)}, bf16[528,256]{1,0:T(8,128)(2,1)S(1)}, u32[]{:S(2)}, u32[]{:S(2)}) collective-permute-start(bf16[528,256]{1,0:T(8,128)(2,1)S(1)} %get-tuple-element.14), channel_id=1, source_target_pairs={{0,1},{1,0},{2,3},{3,2},{4,5},{5,4},{6,7},{7,6},{8,10},{9,11},{10,... | collective-permute-start | bytes 811016 | tf_op jit(solution)/shard_map/ppermute | solution.py:299
  25.1 1.1 %shard_map.124 = (f32[512,256]{1,0:T(8,128)S(1)}, bf16[512,640]{1,0:T(8,128)(2,1)S(1)}, f32[512,640]{1,0:T(8,128)S(1)}) custom-call(bf16[288,1024]{1,0:T(8,128)(2,1)S(1)} %get-tuple-element.11.core_ref, bf16[1024,640]{1,0:T(8,128)(2,1)S(1)} %shard_map.122.effective_ref, bf16[256,640]{1,0:T(8,128)(2,1)S(1)} %get-tuple-element.12.half_ref), custom_call_target="tpu_custom_call" | custom-call | flops 671088640 | bytes 5242880 | tf_op jit(solution)/shard_map/pallas_call | solution.py:22
  26.2 3.3 %collective-permute-done.4 = bf16[528,256]{1,0:T(8,128)(2,1)S(1)} collective-permute-done((bf16[528,256]{1,0:T(8,128)(2,1)S(1)}, bf16[528,256]{1,0:T(8,128)(2,1)S(1)}, u32[]{:S(2)}, u32[]{:S(2)}) %collective-permute-start.4) | collective-permute-done | bytes 270368 | tf_op jit(solution)/shard_map/ppermute | solution.py:299
  29.7 2.0 %collective-permute-start.5 = (bf16[272,256]{1,0:T(8,128)(2,1)S(1)}, bf16[272,256]{1,0:T(8,128)(2,1)S(1)}, u32[]{:S(2)}, u32[]{:S(2)}) collective-permute-start(bf16[272,256]{1,0:T(8,128)(2,1)S(1)} %pad_maximum_fusion.2), channel_id=1, source_target_pairs={{0,2},{1,3},{2,0},{3,1},{4,6},{5,7},{6,4},{7,5},{8,9},{9,8},{10,11... | collective-permute-start | bytes 417800 | tf_op jit(solution)/shard_map/ppermute | solution.py:299
  31.7 3.1 %collective-permute-done.5 = bf16[272,256]{1,0:T(8,128)(2,1)S(1)} collective-permute-done((bf16[272,256]{1,0:T(8,128)(2,1)S(1)}, bf16[272,256]{1,0:T(8,128)(2,1)S(1)}, u32[]{:S(2)}, u32[]{:S(2)}) %collective-permute-start.5) | collective-permute-done | bytes 139296 | tf_op jit(solution)/shard_map/ppermute | solution.py:299
  35.0 3.0 %collective-permute-start.6 = (bf16[144,256]{1,0:T(8,128)(2,1)S(1)}, bf16[144,256]{1,0:T(8,128)(2,1)}, u32[]{:S(2)}, u32[]{:S(2)}) collective-permute-start(bf16[144,256]{1,0:T(8,128)(2,1)S(1)} %pad_maximum_fusion.3), channel_id=1, source_target_pairs={{0,4},{1,5},{2,6},{3,7},{4,0},{5,1},{6,2},{7,3},{8,12},{9,13},{10,... | collective-permute-start | bytes 221192 | tf_op jit(solution)/shard_map/ppermute | solution.py:299
  38.0 0.9 %collective-permute-start.11 = (bf16[256,1024]{1,0:T(8,128)(2,1)}, bf16[256,1024]{1,0:T(8,128)(2,1)}, u32[]{:S(2)}, u32[]{:S(2)}) collective-permute-start(bf16[256,1024]{1,0:T(8,128)(2,1)} %get-tuple-element.16.refs_0_), channel_id=1, source_target_pairs={{0,16},{8,24},{16,0},{24,8},{1,17},{9,25},{17,1},{25,9},{2,18},{10... | collective-permute-start | bytes 1572872 | tf_op jit(solution)/shard_map/ppermute | solution.py:290
  39.0 1.5 %collective-permute-done.6 = bf16[144,256]{1,0:T(8,128)(2,1)} collective-permute-done((bf16[144,256]{1,0:T(8,128)(2,1)S(1)}, bf16[144,256]{1,0:T(8,128)(2,1)}, u32[]{:S(2)}, u32[]{:S(2)}) %collective-permute-start.6) | collective-permute-done | bytes 73760 | tf_op jit(solution)/shard_map/ppermute | solution.py:299
  40.5 0.7 slice_convert_fusion.3
  41.1 1.5 %fusion.10 = bf16[128,256]{1,0:T(8,128)(2,1)S(1)} fusion(f32[256,256]{1,0:T(8,128)} %copy-done.12, bf16[256,1024]{1,0:T(8,128)(2,1)} %get-tuple-element.16.refs_0_, bf16[1024,1024]{1,0:T(8,128)(2,1)S(1)} %copy-done, s32[]{:T(128)S(6)} %select_n.9, bf16[144,256]{1,0:T(8,128)(2,1)} %collective-permute-done.6), kind=kOutput, calls=%fused_computation.23 | convolution fusion | flops 67829760 | bytes 1048580 | tf_op jit(solution)/shard_map/dot_general | solution.py:416
  42.7 1.3 %collective-permute-start.7 = (bf16[1,144,256]{2,1,0:T(8,128)(2,1)S(1)}, bf16[1,144,256]{2,1,0:T(8,128)(2,1)S(1)}, u32[]{:S(2)}, u32[]{:S(2)}) collective-permute-start(bf16[1,144,256]{2,1,0:T(8,128)(2,1)S(1)} %maximum_bitcast_fusion), channel_id=1, source_target_pairs={{0,16},{8,24},{16,0},{24,8},{1,17},{9,25},{17,1},{25,9},{2,18},{10... | collective-permute-start | bytes 221192 | tf_op jit(solution)/shard_map/ppermute | solution.py:290
  44.0 0.7 %constant_dynamic-slice_fusion = f32[16,256]{1,0:T(8,128)S(1)} fusion(f32[16,1024]{1,0:T(8,128)} %gains_ref.1, s32[]{:T(128)S(6)} %select_n.10), kind=kLoop, calls=%fused_computation.61 | loop fusion | bytes 32772 | tf_op jit(solution)/shard_map/dynamic_slice | solution.py:442
  44.7 6.0 %collective-permute-done.11.refs_1_ = bf16[256,1024]{1,0:T(8,128)(2,1)} collective-permute-done((bf16[256,1024]{1,0:T(8,128)(2,1)}, bf16[256,1024]{1,0:T(8,128)(2,1)}, u32[]{:S(2)}, u32[]{:S(2)}) %collective-permute-start.11) | collective-permute-done | bytes 524320 | tf_op jit(solution)/shard_map/ppermute | solution.py:290
  50.7 0.7 collective-permute-done.7
  52.2 1.1 %copy-done.10 = f32[512,640]{1,0:T(8,128)} copy-done((f32[512,640]{1,0:T(8,128)}, f32[512,640]{1,0:T(8,128)S(1)}, u32[]{:S(2)}) %copy-start.10) | copy-done | bytes 1310744
  53.3 0.8 %slice.155 = bf16[256,640]{1,0:T(8,128)(2,1)} slice(f32[512,640]{1,0:T(8,128)S(1)} %convert_add_fusion), slice={[256:512], [0:640]} | slice | bytes 655360 | tf_op jit(solution)/shard_map/slice | solution.py:440
  54.1 1.7 %collective-permute-start.10 = (bf16[256,640]{1,0:T(8,128)(2,1)}, bf16[256,640]{1,0:T(8,128)(2,1)}, u32[]{:S(2)}, u32[]{:S(2)}) collective-permute-start(bf16[256,640]{1,0:T(8,128)(2,1)} %slice.155), channel_id=1, source_target_pairs={{0,16},{8,24},{16,0},{24,8},{1,17},{9,25},{17,1},{25,9},{2,18},{10... | collective-permute-start | bytes 983048 | tf_op jit(solution)/shard_map/ppermute | solution.py:290
  56.4 1.1 %copy.14 = f32[256,640]{1,0:T(8,128)} copy(f32[256,640]{0,1:T(8,128)S(1)} %bitcast.5) | data formatting | bytes 1310720 | tf_op jit(solution)/shard_map/reshape | solution.py:446
  57.5 0.9 %pad_maximum_fusion.grads_ref = bf16[4,144,256]{2,1,0:T(8,128)(2,1)S(1)} fusion(bf16[2,144,256]{2,1,0:T(8,128)(2,1)} %collective-permute-done.8, bf16[1,144,256]{2,1,0:T(8,128)(2,1)S(1)} %collective-permute-done.7, bf16[1,144,256]{2,1,0:T(8,128)(2,1)S(1)} %maximum_bitcast_fusion), kind=kLoop, calls=%fused_computation.6 | loop fusion | flops 294912 | bytes 589824 | tf_op jit(solution)/shard_map/concatenate | solution.py:424
  59.7 4.9 %collective-permute-done.10 = bf16[256,640]{1,0:T(8,128)(2,1)} collective-permute-done((bf16[256,640]{1,0:T(8,128)(2,1)}, bf16[256,640]{1,0:T(8,128)(2,1)}, u32[]{:S(2)}, u32[]{:S(2)}) %collective-permute-start.10) | collective-permute-done | bytes 327712 | tf_op jit(solution)/shard_map/ppermute | solution.py:290
  64.5 2.1 %fusion = f32[256,640]{1,0:T(8,128)} fusion(f32[256,640]{1,0:T(8,128)} %copy.14, f32[512,640]{1,0:T(8,128)S(1)} %copy-done.11, bf16[256,640]{1,0:T(8,128)(2,1)} %collective-permute-done.10), kind=kLoop, calls=%fused_computation.4 | loop fusion | flops 491520 | bytes 2293760 | tf_op jit(solution)/shard_map/mul | solution.py:446
  66.7 2.6 %shard_map.125 = f32[1024,128]{1,0:T(8,128)} custom-call(bf16[4,144,256]{2,1,0:T(8,128)(2,1)S(1)} %pad_maximum_fusion.grads_ref, bf16[256,1024]{1,0:T(8,128)(2,1)} %get-tuple-element.16.refs_0_, bf16[256,1024]{1,0:T(8,128)(2,1)} %collective-permute-done.11.refs_1_, bf16[256,1024]{1,0:T(8,128)(2,1)S(1)} %collective-permute-done.12.refs_2_, ...), custom_call_target="tpu_custom_call" | custom-call | flops 268435456 | bytes 2097152 | tf_op jit(solution)/shard_map/pallas_call | solution.py:22
  (63 shorter events, 4.3 us)
Async XLA Ops:
  3.0 11.0 %collective-permute-start = (bf16[64,1024]{1,0:T(8,128)(2,1)S(1)}, bf16[64,1024]{1,0:T(8,128)(2,1)S(1)}, u32[]{:S(2)}, u32[]{:S(2)}) collective-permute-start(bf16[64,1024]{1,0:T(8,128)(2,1)S(1)} %fusion.11), channel_id=1, source_target_pairs={{0,8},{8,0},{16,24},{24,16},{1,9},{9,1},{17,25},{25,17},{2,10},{10... | collective-permute-start | bytes 393224 | tf_op jit(solution)/shard_map/ppermute | solution.py:290
  3.5 10.5 %collective-permute-start.1 = (bf16[64,1024]{1,0:T(8,128)(2,1)S(1)}, bf16[64,1024]{1,0:T(8,128)(2,1)S(1)}, u32[]{:S(2)}, u32[]{:S(2)}) collective-permute-start(bf16[64,1024]{1,0:T(8,128)(2,1)S(1)} %fusion.11), channel_id=1, source_target_pairs={{8,16},{9,17},{10,18},{11,19},{12,20},{13,21},{14,22},{15,23},{16,... | collective-permute-start | bytes 393224 | tf_op jit(solution)/shard_map/ppermute | solution.py:299
  4.9 9.1 %copy-start = (bf16[1024,1024]{1,0:T(8,128)(2,1)S(1)}, bf16[1024,1024]{1,0:T(8,128)(2,1)}, u32[]{:S(2)}) copy-start(bf16[1024,1024]{1,0:T(8,128)(2,1)} %point_ref.1) | copy-start | bytes 6291460
  4.9 8.9 %collective-permute-start.2 = (s32[10]{0:T(128)S(1)}, s32[10]{0:T(128)S(1)}, u32[]{:S(2)}, u32[]{:S(2)}) collective-permute-start(s32[10]{0:T(128)S(1)} %pad_add_fusion.own_ref), channel_id=1, source_target_pairs={{0,1},{1,0},{2,3},{3,2},{4,5},{5,4},{6,7},{7,6},{9,10},{10,9},{11,... | collective-permute-start | bytes 128 | tf_op jit(solution)/shard_map/ppermute | solution.py:299
  9.5 1.3 %copy-start.1 = (bf16[1024,640]{1,0:T(8,128)(2,1)S(1)}, bf16[1024,640]{1,0:T(8,128)(2,1)}, u32[]{:S(2)}) copy-start(bf16[1024,640]{1,0:T(8,128)(2,1)} %weight_ref.1) | copy-start | bytes 3932164
  10.8 0.8 %copy-start.4 = (f32[16,1024]{1,0:T(8,128)S(1)}, f32[16,1024]{1,0:T(8,128)}, u32[]{:S(2)}) copy-start(f32[16,1024]{1,0:T(8,128)} %gains_ref.1) | copy-start | bytes 196612
  11.7 0.7 copy-start.8
  12.3 1.7 %copy-start.2 = (bf16[256,1024]{1,0:T(8,128)(2,1)S(1)}, bf16[256,1024]{1,0:T(8,128)(2,1)}, u32[]{:S(2)}) copy-start(bf16[256,1024]{1,0:T(8,128)(2,1)} %clip_ref.1) | copy-start | bytes 1572868
  12.3 1.7 %copy-start.6 = (f32[3,1024]{1,0:T(4,128)S(1)}, f32[3,1024]{1,0:T(4,128)}, u32[]{:S(2)}) copy-start(f32[3,1024]{1,0:T(4,128)} %taps_ref.1) | copy-start | bytes 36868
  12.3 1.7 %copy-start.7 = (s32[8]{0:T(128)S(1)}, s32[8]{0:T(128)}, u32[]{:S(2)}) copy-start(s32[8]{0:T(128)} %lengths_ref.3) | copy-start | bytes 100
  13.8 2.2 %copy-start.3 = (bf16[256,640]{1,0:T(8,128)(2,1)S(1)}, bf16[256,640]{1,0:T(8,128)(2,1)}, u32[]{:S(2)}) copy-start(bf16[256,640]{1,0:T(8,128)(2,1)} %bold_ref.1) | copy-start | bytes 983044
  13.8 2.1 %copy-start.5 = (f32[16,640]{1,0:T(8,128)S(1)}, f32[16,640]{1,0:T(8,128)}, u32[]{:S(2)}) copy-start(f32[16,640]{1,0:T(8,128)} %hrf_ref.1) | copy-start | bytes 122884
  13.8 2.1 %collective-permute-start.3 = (s32[10]{0:T(128)S(1)}, s32[10]{0:T(128)S(1)}, u32[]{:S(2)}, u32[]{:S(2)}) collective-permute-start(s32[10]{0:T(128)S(1)} %collective-permute-done.2.mine_ref), channel_id=1, source_target_pairs={{0,8},{8,0},{16,24},{24,16},{1,9},{9,1},{17,25},{25,17},{2,10},{10... | collective-permute-start | bytes 128 | tf_op jit(solution)/shard_map/ppermute | solution.py:290
  21.0 8.5 %collective-permute-start.4 = (bf16[528,256]{1,0:T(8,128)(2,1)S(1)}, bf16[528,256]{1,0:T(8,128)(2,1)S(1)}, u32[]{:S(2)}, u32[]{:S(2)}) collective-permute-start(bf16[528,256]{1,0:T(8,128)(2,1)S(1)} %get-tuple-element.14), channel_id=1, source_target_pairs={{0,1},{1,0},{2,3},{3,2},{4,5},{5,4},{6,7},{7,6},{8,10},{9,11},{10,... | collective-permute-start | bytes 811016 | tf_op jit(solution)/shard_map/ppermute | solution.py:299
  26.2 8.7 %copy-start.9 = (bf16[512,640]{1,0:T(8,128)(2,1)}, bf16[512,640]{1,0:T(8,128)(2,1)S(1)}, u32[]{:S(2)}) copy-start(bf16[512,640]{1,0:T(8,128)(2,1)S(1)} %get-tuple-element.18) | copy-start | bytes 1966084
  29.7 5.1 %collective-permute-start.5 = (bf16[272,256]{1,0:T(8,128)(2,1)S(1)}, bf16[272,256]{1,0:T(8,128)(2,1)S(1)}, u32[]{:S(2)}, u32[]{:S(2)}) collective-permute-start(bf16[272,256]{1,0:T(8,128)(2,1)S(1)} %pad_maximum_fusion.2), channel_id=1, source_target_pairs={{0,2},{1,3},{2,0},{3,1},{4,6},{5,7},{6,4},{7,5},{8,9},{9,8},{10,11... | collective-permute-start | bytes 417800 | tf_op jit(solution)/shard_map/ppermute | solution.py:299
  34.9 3.2 %copy-start.12 = (f32[256,256]{1,0:T(8,128)}, f32[256,256]{1,0:T(8,128)S(1)}, u32[]{:S(2)}) copy-start(f32[256,256]{1,0:T(8,128)S(1)} %slice_add_fusion.1) | copy-start | bytes 786436
  35.0 5.5 %collective-permute-start.6 = (bf16[144,256]{1,0:T(8,128)(2,1)S(1)}, bf16[144,256]{1,0:T(8,128)(2,1)}, u32[]{:S(2)}, u32[]{:S(2)}) collective-permute-start(bf16[144,256]{1,0:T(8,128)(2,1)S(1)} %pad_maximum_fusion.3), channel_id=1, source_target_pairs={{0,4},{1,5},{2,6},{3,7},{4,0},{5,1},{6,2},{7,3},{8,12},{9,13},{10,... | collective-permute-start | bytes 221192 | tf_op jit(solution)/shard_map/ppermute | solution.py:299
  38.0 12.7 %collective-permute-start.11 = (bf16[256,1024]{1,0:T(8,128)(2,1)}, bf16[256,1024]{1,0:T(8,128)(2,1)}, u32[]{:S(2)}, u32[]{:S(2)}) collective-permute-start(bf16[256,1024]{1,0:T(8,128)(2,1)} %get-tuple-element.16.refs_0_), channel_id=1, source_target_pairs={{0,16},{8,24},{16,0},{24,8},{1,17},{9,25},{17,1},{25,9},{2,18},{10... | collective-permute-start | bytes 1572872 | tf_op jit(solution)/shard_map/ppermute | solution.py:290
  38.9 13.1 %collective-permute-start.9 = (bf16[512,640]{1,0:T(8,128)(2,1)}, bf16[512,640]{1,0:T(8,128)(2,1)S(1)}, u32[]{:S(2)}, u32[]{:S(2)}) collective-permute-start(bf16[512,640]{1,0:T(8,128)(2,1)} %copy-done.9), channel_id=1, source_target_pairs={{0,8},{8,0},{16,24},{24,16},{1,9},{9,1},{17,25},{25,17},{2,10},{10... | collective-permute-start | bytes 1966088 | tf_op jit(solution)/shard_map/ppermute | solution.py:290
  42.7 8.7 %collective-permute-start.7 = (bf16[1,144,256]{2,1,0:T(8,128)(2,1)S(1)}, bf16[1,144,256]{2,1,0:T(8,128)(2,1)S(1)}, u32[]{:S(2)}, u32[]{:S(2)}) collective-permute-start(bf16[1,144,256]{2,1,0:T(8,128)(2,1)S(1)} %maximum_bitcast_fusion), channel_id=1, source_target_pairs={{0,16},{8,24},{16,0},{24,8},{1,17},{9,25},{17,1},{25,9},{2,18},{10... | collective-permute-start | bytes 221192 | tf_op jit(solution)/shard_map/ppermute | solution.py:290
  44.7 21.9 %collective-permute-start.12 = (bf16[256,1024]{1,0:T(8,128)(2,1)}, bf16[256,1024]{1,0:T(8,128)(2,1)S(1)}, u32[]{:S(2)}, u32[]{:S(2)}) collective-permute-start(bf16[256,1024]{1,0:T(8,128)(2,1)} %get-tuple-element.16.refs_0_), channel_id=1, source_target_pairs={{0,8},{8,0},{16,24},{24,16},{1,9},{9,1},{17,25},{25,17},{2,10},{10... | collective-permute-start | bytes 1572872 | tf_op jit(solution)/shard_map/ppermute | solution.py:290
  50.7 16.0 %collective-permute-start.13 = (bf16[256,1024]{1,0:T(8,128)(2,1)}, bf16[256,1024]{1,0:T(8,128)(2,1)S(1)}, u32[]{:S(2)}, u32[]{:S(2)}) collective-permute-start(bf16[256,1024]{1,0:T(8,128)(2,1)} %collective-permute-done.11.refs_1_), channel_id=1, source_target_pairs={{0,8},{8,0},{16,24},{24,16},{1,9},{9,1},{17,25},{25,17},{2,10},{10... | collective-permute-start | bytes 1572872 | tf_op jit(solution)/shard_map/ppermute | solution.py:290
  52.1 5.4 %collective-permute-start.8 = (bf16[2,144,256]{2,1,0:T(8,128)(2,1)}, bf16[2,144,256]{2,1,0:T(8,128)(2,1)}, u32[]{:S(2)}, u32[]{:S(2)}) collective-permute-start(bf16[2,144,256]{2,1,0:T(8,128)(2,1)} %pad_maximum_fusion.1), channel_id=1, source_target_pairs={{0,8},{8,0},{16,24},{24,16},{1,9},{9,1},{17,25},{25,17},{2,10},{10... | collective-permute-start | bytes 442376 | tf_op jit(solution)/shard_map/ppermute | solution.py:290
  52.2 1.1 %copy-start.10 = (f32[512,640]{1,0:T(8,128)}, f32[512,640]{1,0:T(8,128)S(1)}, u32[]{:S(2)}) copy-start(f32[512,640]{1,0:T(8,128)S(1)} %convert_add_fusion) | copy-start | bytes 3932164
  54.1 10.4 %collective-permute-start.10 = (bf16[256,640]{1,0:T(8,128)(2,1)}, bf16[256,640]{1,0:T(8,128)(2,1)}, u32[]{:S(2)}, u32[]{:S(2)}) collective-permute-start(bf16[256,640]{1,0:T(8,128)(2,1)} %slice.155), channel_id=1, source_target_pairs={{0,16},{8,24},{16,0},{24,8},{1,17},{9,25},{17,1},{25,9},{2,18},{10... | collective-permute-start | bytes 983048 | tf_op jit(solution)/shard_map/ppermute | solution.py:290
  56.3 8.2 %copy-start.11 = (f32[512,640]{1,0:T(8,128)S(1)}, f32[512,640]{1,0:T(8,128)}, u32[]{:S(2)}) copy-start(f32[512,640]{1,0:T(8,128)} %copy-done.10) | copy-start | bytes 3932164

commit v2 on v1

--- a/solution.py
+++ b/solution.py
@@ -16,17 +16,20 @@
 NT = (((1,), (1,)), ((), ()))
 VMEM = pl.BlockSpec(memory_space=pltpu.VMEM)
 SMEM = pl.BlockSpec(memory_space=pltpu.SMEM)
-
-
-def call(body, outs, ins, flops, moved, scratch=()):
+HBM = pl.BlockSpec(memory_space=pltpu.HBM)
+
+
+def call(body, outs, ins, micros, scratch=()):
     return pl.pallas_call(
         body,
         out_shape=outs,
         in_specs=[spec for spec, _ in ins],
         out_specs=jax.tree.map(lambda _: VMEM, outs),
         scratch_shapes=scratch,
-        compiler_params=pltpu.CompilerParams(vmem_limit_bytes=40 << 20),
-        cost_estimate=pl.CostEstimate(flops=flops, bytes_accessed=moved, transcendentals=0),
+        compiler_params=pltpu.CompilerParams(vmem_limit_bytes=16 << 20),
+        cost_estimate=pl.CostEstimate(
+            flops=int(micros * 1.15e9), bytes_accessed=int(micros * 1e6), transcendentals=0
+        ),
     )(*[value for _, value in ins])
 
 
@@ -51,6 +54,19 @@
     return stop
 
 
+def pack_kernel(blocks, subject_ref, live_ref, tail_ref, head_ref, bold_ref, payload_ref, ends_ref):
+    slots = bold_ref.shape[1]
+    payload_ref[: 2 * MARGIN, :] = tail_ref[...]
+    payload_ref[2 * MARGIN : 3 * MARGIN, :] = head_ref[...]
+    payload_ref[3 * MARGIN :, :slots] = bold_ref[...]
+    payload_ref[3 * MARGIN :, slots:] = jnp.zeros_like(payload_ref[3 * MARGIN :, slots:])
+    row = lax.broadcasted_iota(jnp.int32, ends_ref.shape, 0)
+    last = blocks - 1
+    ends = jnp.where(row == 0, subject_ref[0], live_ref[0])
+    ends = jnp.where(row == 2, subject_ref[last], ends)
+    ends_ref[...] = jnp.where(row == 3, live_ref[last], ends)
+
+
 def gain_kernel(blocks, subject_ref, gains_ref, weight_ref, effective_ref):
     rows = [gains_ref[pl.ds(subject_ref[b], 1), :] for b in range(blocks)]
     rows += [rows[-1]] * (-blocks % 8)
@@ -63,7 +79,17 @@
 
 
 def core_kernel(
-    rows, lengths_ref, clip_ref, near_ref, far_ref, taps_ref, point_ref, depth_ref, core_ref, ext, deep
+    rows,
+    lengths_ref,
+    clip_ref,
+    near_ref,
+    far_ref,
+    taps_ref,
+    point_ref,
+    depth_ref,
+    core_ref,
+    ext,
+    deep,
 ):
     feats = clip_ref.shape[1]
     odd = lax.axis_index("tm") % 2
@@ -119,7 +145,8 @@
     orders,
     width,
     lengths_ref,
-    own_ref,
+    subject_ref,
+    live_ref,
     mine_ref,
     twin_ref,
     core_ref,
@@ -157,27 +184,21 @@
     since[...] = time - session_starts(lengths_ref, time)
     left[...] = session_stops(lengths_ref, time) - 1 - time
 
+    first_core = odd == 0
+    low = jnp.where(first_core, mine_ref[...], twin_ref[...])
+    high = jnp.where(first_core, twin_ref[...], mine_ref[...])
     even_vox = lax.axis_index("vox") % 2 == 0
-    zero_odd = odd == 0
-
-    def neighbour(at):
-        low = jnp.where(zero_odd, mine_ref[at], twin_ref[at])
-        high = jnp.where(zero_odd, twin_ref[at], mine_ref[at])
-        return low, high
-
-    last_pair = [neighbour(blocks - 1), neighbour(2 * blocks - 1)]
-    next_pair = [neighbour(0), neighbour(blocks)]
-    before = [jnp.where(even_vox, high, low) for low, high in last_pair]
-    after = [jnp.where(even_vox, low, high) for low, high in next_pair]
-    subjects = [before[0]] + [own_ref[b] for b in range(blocks)] + [after[0]]
-    lives = [before[1]] + [own_ref[blocks + b] for b in range(blocks)] + [after[1]]
+    before = jnp.where(even_vox, high, low)
+    after = jnp.where(even_vox, low, high)
+    subjects = [before[2:3]] + [subject_ref[b] for b in range(blocks)] + [after[0:1]]
+    lives = [before[3:4]] + [live_ref[b] for b in range(blocks)] + [after[1:2]]
     lane = lax.broadcasted_iota(jnp.int32, (16, BLOCK_VOX), 1)
     for b in range(blocks):
-        count = lives[b + 1]
+        count = jnp.full((1, BLOCK_VOX), lives[b + 1], jnp.int32)
         count = count + jnp.where(subjects[b] == subjects[b + 1], lives[b], 0)
         count = count + jnp.where(subjects[b + 2] == subjects[b + 1], lives[b + 2], 0)
-        counts = jnp.full((16, BLOCK_VOX), jnp.maximum(count, 1), jnp.int32).astype(F32)
-        scale[b] = jnp.where(lane < lives[b + 1], 1.0 / counts, 0.0)
+        inverse = 1.0 / jnp.maximum(count, 1).astype(F32)
+        scale[b] = jnp.where(lane < lives[b + 1], inverse, 0.0)
 
     for b in range(0, blocks, 2):
         many = min(2, blocks - b)
@@ -248,18 +269,69 @@
         )
 
 
-def last_kernel(parts, width, grads_ref, *refs):
-    depth_refs, (point_ref,) = refs[:parts], refs[parts:]
-    feats = point_ref.shape[0]
-    for col in range(0, feats, 256):
+def slope_kernel(point_ref, depth_ref, slope_ref):
+    act = lax.dot_general(
+        point_ref[...], depth_ref[...], (((0,), (1,)), ((), ())), preferred_element_type=F32
+    )
+    slope_ref[...] = jax.vjp(jax.nn.gelu, act)[1](jnp.ones_like(act))[0]
+
+
+def loss_pair(value, width):
+    high = value.astype(BF16).astype(F32)
+    pair = jnp.concatenate([high, value - high], axis=0)
+    pad = jnp.zeros((16, width - BLOCK_VOX), F32)
+    return jnp.concatenate([pair, pad], axis=1).astype(BF16)
+
+
+def grad_kernel(keep_ref, arrived_ref, lost_ref, slope_ref, out_ref):
+    width = keep_ref.shape[0]
+    total = keep_ref[...] + arrived_ref[:width, :].astype(F32)
+    out_ref[:width, :] = (total * slope_ref[...]).astype(BF16)
+    pair = arrived_ref[width:, :BLOCK_VOX].astype(F32)
+    out_ref[width:, :] = loss_pair(lost_ref[...] + pair[:8] + pair[8:], keep_ref.shape[1])
+
+
+def early_kernel(parts, width, *refs):
+    grad_refs, depth_refs, (total_ref,) = refs[:parts], refs[parts : 2 * parts], refs[2 * parts :]
+    for col in range(0, total_ref.shape[1], 256):
         lanes = slice(col, col + 256)
         total = None
-        for r in range(parts):
+        for grad_ref, depth_ref in zip(grad_refs, depth_refs):
             part = jnp.dot(
-                grads_ref[r, :width, :], depth_refs[r][:, lanes], preferred_element_type=F32
+                grad_ref[:width, :], depth_ref[:, lanes], preferred_element_type=F32
             )
             total = part if total is None else total + part
+        total_ref[:, lanes] = total
+
+
+def last_kernel(early, late, width, scale, total_ref, *refs):
+    first_refs = refs[:early]
+    grad_refs = refs[early : early + late]
+    depth_refs = refs[early + late : early + 2 * late]
+    point_ref, loss_ref = refs[early + 2 * late :]
+    for col in range(0, total_ref.shape[1], 256):
+        lanes = slice(col, col + 256)
+        total = total_ref[:, lanes]
+        for grad_ref, depth_ref in zip(grad_refs, depth_refs):
+            total = total + jnp.dot(
+                grad_ref[:width, :], depth_ref[:, lanes], preferred_element_type=F32
+            )
         point_ref[lanes, :] = jnp.transpose(total)
+    lost = None
+    for ref in first_refs + grad_refs:
+        part = ref[width:, :BLOCK_VOX].astype(F32)
+        lost = part if lost is None else lost + part
+    loss_ref[0, 0] = jnp.sum(lost) * scale
+
+
+def readout_kernel(blocks, subject_ref, keep_ref, arrived_ref, gains_ref, out_ref):
+    rows = [gains_ref[pl.ds(subject_ref[b], 1), :] for b in range(blocks)]
+    rows += [rows[-1]] * (-blocks % 8)
+    cols = jnp.transpose(jnp.concatenate(rows, axis=0))
+    for b in range(blocks):
+        lanes = slice(b * BLOCK_VOX, (b + 1) * BLOCK_VOX)
+        total = keep_ref[:, lanes] + arrived_ref[:, lanes].astype(F32)
+        out_ref[:, lanes] = total * cols[:, b : b + 1]
 
 
 def shards(
@@ -308,27 +380,29 @@
         other = v + 1 if v % 2 else v - 1
         return (t, other) if 0 <= other < vox_count else None
 
-    payload = jnp.concatenate(
-        [
-            clip_features[rows - 2 * MARGIN :],
-            clip_features[:MARGIN],
-            jnp.pad(bold_target[:MARGIN], ((0, 0), (0, feats - slots))),
+    payload, ends = pl.pallas_call(
+        functools.partial(pack_kernel, blocks),
+        out_shape=(
+            jax.ShapeDtypeStruct((4 * MARGIN, feats), BF16),
+            jax.ShapeDtypeStruct((8, BLOCK_VOX), jnp.int32),
+        ),
+        grid=(1,),
+        in_specs=[
+            SMEM,
+            SMEM,
+            pl.BlockSpec((2 * MARGIN, feats), lambda i: (rows // (2 * MARGIN) - 1, 0)),
+            pl.BlockSpec((MARGIN, feats), lambda i: (0, 0)),
+            pl.BlockSpec((MARGIN, slots), lambda i: (0, 0)),
         ],
-        axis=0,
-    )
+        out_specs=(VMEM, VMEM),
+        cost_estimate=pl.CostEstimate(
+            flops=int(6 * 1.15e9), bytes_accessed=1000000, transcendentals=0
+        ),
+    )(block_subject, block_live, clip_features, clip_features, bold_target)
     far = across(payload, next_tm)
-    own_blocks = jnp.concatenate([block_subject, block_live])
-    mine = across(own_blocks, next_vox)
+    mine = across(ends, next_vox)
     near = swap_tm(payload, 0)
-    twin = swap_tm(mine, 0)
-
-    effective = call(
-        functools.partial(gain_kernel, blocks),
-        jax.ShapeDtypeStruct((feats, slots), BF16),
-        [(SMEM, block_subject), (VMEM, subject_feature_gains), (VMEM, readout_weight)],
-        feats * slots,
-        4 * feats * slots,
-    )
+
     depth_half, core_out = call(
         functools.partial(core_kernel, rows),
         (
@@ -343,12 +417,21 @@
             (VMEM, depth_kernel),
             (VMEM, point_weight),
         ],
-        2 * rows * feats * feats,
-        2 * feats * feats,
+        2.0,
         [
             pltpu.VMEM((rows + 3 * MARGIN, feats), BF16),
             pltpu.VMEM((rows + 2 * MARGIN, feats), BF16),
         ],
+    )
+    core_out, late_gains, mine = lax.optimization_barrier(
+        (core_out, subject_feature_gains, mine)
+    )
+    twin = swap_tm(mine, 0)
+    effective = call(
+        functools.partial(gain_kernel, blocks),
+        jax.ShapeDtypeStruct((feats, slots), BF16),
+        [(SMEM, block_subject), (VMEM, late_gains), (VMEM, readout_weight)],
+        1.5,
     )
     half, send, lost = call(
         functools.partial(voxel_kernel, rows, blocks, orders, width),
@@ -359,9 +442,10 @@
         ),
         [
             (SMEM, session_lengths),
-            (SMEM, own_blocks),
-            (SMEM, mine),
-            (SMEM, twin),
+            (SMEM, block_subject),
+            (SMEM, block_live),
+            (VMEM, mine),
+            (VMEM, twin),
             (VMEM, core_out),
             (VMEM, effective),
             (VMEM, hrf_kernel),
@@ -369,8 +453,7 @@
             (VMEM, near),
             (VMEM, far),
         ],
-        4 * rows * feats * slots,
-        8 * rows * slots,
+        5.0,
         [
             pltpu.VMEM((blocks, rows + 2 * MARGIN, BLOCK_VOX), F32),
             pltpu.VMEM((blocks, rows + MARGIN, BLOCK_VOX), F32),
@@ -388,8 +471,7 @@
             jax.ShapeDtypeStruct((feats // 2, slots), F32),
         ),
         [(VMEM, core_out), (VMEM, effective), (VMEM, half)],
-        4 * rows * feats * slots,
-        8 * feats * slots,
+        1.1,
         [pltpu.VMEM((feats, rows), BF16)],
     )
 
@@ -402,49 +484,95 @@
         pair = arrived[:, :BLOCK_VOX].astype(F32)
         return pair[:8] + pair[8:]
 
-    for stage in range(len(vox_bits)):
-        arrived = across(send, lambda t, v: (t, v ^ (1 << orders[t % 2][stage])))
-        size = keep.shape[0]
-        keep = keep + arrived[:size].astype(F32)
-        lost = lost + loss_of(arrived[size:])
-        if stage + 1 < len(vox_bits):
-            send = jnp.concatenate([keep[size // 2 :].astype(BF16), loss_rows(lost)], axis=0)
-            keep = keep[: size // 2]
-
     col = lax.axis_index("vox") * width
     point_cols = lax.dynamic_slice_in_dim(point_weight, col, width, 1)
-    pre_act = lax.dot_general(
-        point_cols, depth_half, (((0,), (1,)), ((), ())), preferred_element_type=F32
-    )
-    pre_grad = jax.vjp(jax.nn.gelu, pre_act)[1](keep)[0].astype(BF16)
-    gathered = jnp.concatenate([pre_grad, loss_rows(lost)], axis=0)[None]
-    depths = [depth_half]
-    for bit in reversed(tm_bits):
-        depths = depths + [swap_tm(value, bit) for value in depths]
-        gathered = jnp.concatenate([gathered, swap_tm(gathered, bit)], axis=0)
-    loss_sum = jnp.sum(gathered[:, width:, :BLOCK_VOX].astype(F32))
-    loss_total = loss_sum / (subjects * rows * tm_count)
-    grad_point = call(
-        functools.partial(last_kernel, tm_count, width),
-        jax.ShapeDtypeStruct((feats, width), F32),
-        [(VMEM, gathered)] + [(VMEM, value) for value in depths],
-        2 * rows * tm_count * feats * width,
-        2 * rows * tm_count * feats,
-    )
-
-    for bit in tm_bits:
-        arrived = swap_tm(raw_send, bit)
-        raw_keep = raw_keep + arrived.astype(F32)
-        if bit + 1 < len(tm_bits):
-            size = raw_keep.shape[0] // 2
-            raw_send = raw_keep[size:].astype(BF16)
-            raw_keep = raw_keep[:size]
+    slope = call(
+        slope_kernel,
+        jax.ShapeDtypeStruct((width, rows), F32),
+        [(VMEM, point_cols), (VMEM, depth_half)],
+        0.7,
+    )
     own_gains = lax.dynamic_slice_in_dim(
         subject_feature_gains, lax.axis_index("tm") * share, share, 1
     )
-    gain_cols = jnp.transpose(own_gains[block_subject])
-    grad_readout = raw_keep * jnp.repeat(gain_cols, BLOCK_VOX, axis=1)
-    return (loss_total, grad_readout, grad_point)
+    stages = len(vox_bits)
+    paths = [()]
+    for bit in reversed(tm_bits):
+        paths = paths + [path + (bit,) for path in paths]
+    depths = {(): depth_half}
+    first = [(bit,) for bit in reversed(tm_bits)]
+    for path in first:
+        depths[path] = swap_tm(depth_half, path[0])
+    raw_came = swap_tm(raw_send, tm_bits[0])
+    for stage in range(stages):
+        arrived = across(send, lambda t, v: (t, v ^ (1 << orders[t % 2][stage])))
+        if stage == 0:
+            held = lax.optimization_barrier((arrived, *[depths[path] for path in first]))
+            arrived = held[0]
+            depths.update(zip(first, held[1:]))
+        if stage == min(1, stages - 1):
+            for bit in tm_bits[1:]:
+                raw_keep = raw_keep + raw_came.astype(F32)
+                size = raw_keep.shape[0] // 2
+                raw_send, raw_keep = raw_keep[size:].astype(BF16), raw_keep[:size]
+                raw_came = swap_tm(raw_send, bit)
+            arrived, raw_keep, slope, own_gains = lax.optimization_barrier(
+                (arrived, raw_keep, slope, own_gains)
+            )
+        if stage + 1 < stages:
+            size = keep.shape[0] // 2
+            keep = keep + arrived[: 2 * size].astype(F32)
+            lost = lost + loss_of(arrived[2 * size :])
+            send = jnp.concatenate([keep[size:].astype(BF16), loss_rows(lost)], axis=0)
+            keep = keep[:size]
+    arrived, raw_came = lax.optimization_barrier((arrived, raw_came))
+    for path in paths[1:]:
+        if path not in depths:
+            depths[path] = swap_tm(depths[path[:-1]], path[-1])
+    pre_grad = call(
+        grad_kernel,
+        jax.ShapeDtypeStruct((width + 16, rows), BF16),
+        [(VMEM, keep), (VMEM, arrived), (VMEM, lost), (VMEM, slope)],
+        0.3,
+    )
+    grads = {(): pre_grad}
+    for path in paths[1:]:
+        grads[path] = swap_tm(grads[path[:-1]], path[-1])
+    early = [(), (0,)]
+    late = [path for path in paths if path not in early]
+    total = call(
+        functools.partial(early_kernel, len(early), width),
+        jax.ShapeDtypeStruct((width, feats), F32),
+        [(VMEM, grads[path]) for path in early] + [(VMEM, depths[path]) for path in early],
+        0.8,
+    )
+    grad_readout = call(
+        functools.partial(readout_kernel, blocks),
+        jax.ShapeDtypeStruct((share, slots), F32),
+        [(SMEM, block_subject), (VMEM, raw_keep), (VMEM, raw_came), (VMEM, own_gains)],
+        0.8,
+    )
+    grad_point, loss_total = pl.pallas_call(
+        functools.partial(
+            last_kernel, len(early), len(late), width, 1.0 / (subjects * rows * tm_count)
+        ),
+        out_shape=(
+            jax.ShapeDtypeStruct((feats, width), F32),
+            jax.ShapeDtypeStruct((1, 1), F32),
+        ),
+        in_specs=[VMEM] * (1 + len(early) + 2 * len(late)),
+        out_specs=(VMEM, SMEM),
+        compiler_params=pltpu.CompilerParams(vmem_limit_bytes=16 << 20),
+        cost_estimate=pl.CostEstimate(
+            flops=int(1.15e9), bytes_accessed=1000000, transcendentals=0
+        ),
+    )(
+        total,
+        *[grads[path] for path in early],
+        *[grads[path] for path in late],
+        *[depths[path] for path in late],
+    )
+    return (loss_total.reshape(()), grad_readout, grad_point)
 
 
 def solution(mesh):

time: 71 us -> 47.2 us (0.66)
  local copies, waits for them, and re-layouts: 9.45 us -> 0.25 us
  other arithmetic: 6.14 us -> 0.3 us
  waiting for transfers between devices: 19.5 us -> 13.9 us
  Pallas kernels: 12.1 us -> 15 us
  starting transfers between devices: 19 us -> 16.6 us
  between operations: 2.68 us -> 0.99 us
  matrix products: 1.52 us -> 0 us
    ppermute x9 -> x10, waiting for transfers between devices: 11.5 us -> 5.02 us  [swap_tm(): lax.ppermute(value, 'tm', [(i, i ^ 1 << bit) for i in range(tm_count)])]
    unnamed x26 -> x20, local copies, waits for them, and re-layouts: 3.93 us -> 0.05 us
    ppermute x5, starting transfers between devices: 14.4 us -> 11 us  [across(): return lax.ppermute(value, ('tm', 'vox'), pairs)]
    slice x6 -> x5, local copies, waits for them, and re-layouts: 3.12 us -> 0.12 us  [the longest x2 0.08 us: shards(): raw_send, raw_keep = (raw_keep[size:].astype(BF16), raw_keep[:size])]
    pallas_call x0 -> x2, Pallas kernels: none -> 2.94 us  [the longest x1 1.69 us: shards(): pl.pallas_call(functools.partial(pack_kernel, blocks), out_shape=(jax.Sha...]
    concatenate x6 -> x2, other arithmetic: 2.39 us -> 0.02 us  [shards(): send = jnp.concatenate([keep[size:].astype(BF16), loss_rows(lost)], axis=0)]
    mul x1 -> x0, other arithmetic: 2.13 us -> none  [shards(): grad_readout = raw_keep * jnp.repeat(gain_cols, BLOCK_VOX, axis=1)]
    dot_general x1 -> x0, matrix products: 1.52 us -> none  [shards(): lax.dot_general(point_cols, depth_half, (((0,), (1,)), ((), ())), preferr...]
  transfers between devices with their start and end apart: 14 -> 15, of which waited for: 6 -> 6; matrix products, arithmetic and copies ran while one was open for 15% -> 1% of each run, Pallas kernels for 6% -> 26%
where the time goes in v2:
time: 47.2 us; the launch traced here: 47 us
  starting transfers between devices  16.6 us (35%)
  Pallas kernels  15 us (32%)
  waiting for transfers between devices  13.9 us (29%)
  between operations  0.99 us (2%)
    pallas_call x8, Pallas kernels, call(): pl.pallas_call(body, out_shape=outs, in_specs=[spec for spec, _ in ins],...  12 us
    ppermute x5, starting transfers between devices, across(): return lax.ppermute(value, ('tm', 'vox'), pairs)  11 us
    ppermute x5, waiting for transfers between devices, across(): return lax.ppermute(value, ('tm', 'vox'), pairs)  8.9 us
    ppermute x10, starting transfers between devices, swap_tm(): lax.ppermute(value, 'tm', [(i, i ^ 1 << bit) for i in range(tm_count)])  5.63 us
    ppermute x10, waiting for transfers between devices, swap_tm(): lax.ppermute(value, 'tm', [(i, i ^ 1 << bit) for i in range(tm_count)])  5.02 us
    pallas_call x1, Pallas kernels, shards(): pl.pallas_call(functools.partial(pack_kernel, blocks), out_shape=(jax.Sha...  1.69 us
    pallas_call x1, Pallas kernels, shards(): pl.pallas_call(functools.partial(last_kernel, len(early), len(late), widt...  1.26 us
  transfers between devices with their start and end apart: 15, of which 6 were waited for; matrix products, arithmetic and copies ran while one was open for 1% of the time, Pallas kernels for 26%

profile of v2, /device:TPU:0, one launch (start us, length us, event | category | flops | bytes accessed | tf_op | source)
XLA Modules:
  0.0 47.0 jit_solution(277893724831633905)
XLA Ops:
  0.7 1.7 %shard_map.121 = (bf16[64,1024]{1,0:T(8,128)(2,1)}, s32[8,128]{1,0:T(8,128)}) custom-call(s32[5]{0:T(128)} %subject_ref.7, s32[5]{0:T(128)} %live_ref.3, bf16[256,1024]{1,0:T(8,128)(2,1)} %clip_ref.1, bf16[256,1024]{1,0:T(8,128)(2,1)} %clip_ref.1, bf16[256,640]{1,0:T(8,128)(2,1)} %bold_ref.3), custom_call_target="tpu_custom_call" | custom-call | flops 6899999744 | bytes 1000000 | tf_op jit(solution)/shard_map/pallas_call | solution.py:383
  2.4 0.5 collective-permute-start
  2.8 0.7 %collective-permute-start.1 = (bf16[64,1024]{1,0:T(8,128)(2,1)}, bf16[64,1024]{1,0:T(8,128)(2,1)S(1)}, u32[]{:S(2)}, u32[]{:S(2)}) collective-permute-start(bf16[64,1024]{1,0:T(8,128)(2,1)} %get-tuple-element.27), channel_id=1, source_target_pairs={{8,16},{9,17},{10,18},{11,19},{12,20},{13,21},{14,22},{15,23},{16,... | collective-permute-start | bytes 393224 | tf_op jit(solution)/shard_map/ppermute | solution.py:371
  3.5 4.4 %collective-permute-start.2 = (s32[8,128]{1,0:T(8,128)}, s32[8,128]{1,0:T(8,128)S(1)}, u32[]{:S(2)}, u32[]{:S(2)}) collective-permute-start(s32[8,128]{1,0:T(8,128)} %get-tuple-element.29), channel_id=1, source_target_pairs={{0,1},{1,0},{2,3},{3,2},{4,5},{5,4},{6,7},{7,6},{9,10},{10,9},{11,... | collective-permute-start | bytes 12296 | tf_op jit(solution)/shard_map/ppermute | solution.py:371
  7.9 0.1 constant_dynamic-slice_fusion.1.point_ref
  8.0 0.0 copy-start.2
  8.0 0.0 copy-start.9
  8.1 1.8 %shard_map.122 = (bf16[256,1024]{1,0:T(8,128)(2,1)S(1)}, bf16[288,1024]{1,0:T(8,128)(2,1)S(1)}) custom-call(s32[8]{0:T(128)S(1)} %copy-done.7, bf16[256,1024]{1,0:T(8,128)(2,1)S(1)} %copy-done.3, bf16[64,1024]{1,0:T(8,128)(2,1)S(1)} %collective-permute-done.near_ref, bf16[64,1024]{1,0:T(8,128)(2,1)S(1)} %collective-permute-done.1.far_ref, ...), custom_call_target="tpu_custom_call" | custom-call | flops 2300000000 | bytes 2000000 | tf_op jit(solution)/shard_map/pallas_call | solution.py:23
  9.9 3.8 %collective-permute-start.5 = (bf16[256,1024]{1,0:T(8,128)(2,1)S(1)}, bf16[256,1024]{1,0:T(8,128)(2,1)S(1)}, u32[]{:S(2)}, u32[]{:S(2)}) collective-permute-start(bf16[256,1024]{1,0:T(8,128)(2,1)S(1)} %get-tuple-element.36.depth_ref.refs_2_), channel_id=1, source_target_pairs={{0,16},{8,24},{16,0},{24,8},{1,17},{9,25},{17,1},{25,9},{2,18},{10... | collective-permute-start | bytes 1572872 | tf_op jit(solution)/shard_map/ppermute | solution.py:362
  13.7 0.6 %collective-permute-start.3 = (s32[8,128]{1,0:T(8,128)S(1)}, s32[8,128]{1,0:T(8,128)S(1)}, u32[]{:S(2)}, u32[]{:S(2)}) collective-permute-start(s32[8,128]{1,0:T(8,128)S(1)} %collective-permute-done.2.mine_ref), channel_id=1, source_target_pairs={{0,8},{8,0},{16,24},{24,16},{1,9},{9,1},{17,25},{25,17},{2,10},{10... | collective-permute-start | bytes 12296 | tf_op jit(solution)/shard_map/ppermute | solution.py:362
  14.3 1.5 %shard_map.123.effective_ref = bf16[1024,640]{1,0:T(8,128)(2,1)S(1)} custom-call(s32[5]{0:T(128)S(1)} %copy-done.9, f32[16,1024]{1,0:T(8,128)S(1)} %copy-done.1, bf16[1024,640]{1,0:T(8,128)(2,1)S(1)} %copy-done.2), custom_call_target="tpu_custom_call" | custom-call | flops 1724999936 | bytes 1500000 | tf_op jit(solution)/shard_map/pallas_call | solution.py:23
  15.8 5.1 %shard_map.124 = (bf16[256,640]{1,0:T(8,128)(2,1)S(1)}, bf16[528,256]{1,0:T(8,128)(2,1)S(1)}, f32[8,128]{1,0:T(8,128)S(1)}) custom-call(s32[8]{0:T(128)S(1)} %copy-done.7, s32[5]{0:T(128)S(1)} %copy-done.9, s32[5]{0:T(128)S(1)} %copy-done.8, s32[8,128]{1,0:T(8,128)S(1)} %collective-permute-done.2.mine_ref, s32[8,128]{1,0:T(8,128)S(1)} %collective-permute-done.3.twin_ref, ...), custom_call_target="tpu_custom_call" | custom-call | flops 5750000128 | bytes 5000000 | tf_op jit(solution)/shard_map/pallas_call | solution.py:23
  20.9 1.6 %collective-permute-start.4 = (bf16[528,256]{1,0:T(8,128)(2,1)S(1)}, bf16[528,256]{1,0:T(8,128)(2,1)S(1)}, u32[]{:S(2)}, u32[]{:S(2)}) collective-permute-start(bf16[528,256]{1,0:T(8,128)(2,1)S(1)} %get-tuple-element.35), channel_id=1, source_target_pairs={{0,1},{1,0},{2,3},{3,2},{4,5},{5,4},{6,7},{7,6},{8,10},{9,11},{10,... | collective-permute-start | bytes 811016 | tf_op jit(solution)/shard_map/ppermute | solution.py:371
  22.5 0.4 shard_map.126.slope_ref
  22.9 1.1 %shard_map.125 = (f32[512,256]{1,0:T(8,128)S(1)}, bf16[512,640]{1,0:T(8,128)(2,1)S(1)}, f32[512,640]{1,0:T(8,128)S(1)}) custom-call(bf16[288,1024]{1,0:T(8,128)(2,1)S(1)} %get-tuple-element.30.core_ref, bf16[1024,640]{1,0:T(8,128)(2,1)S(1)} %shard_map.123.effective_ref, bf16[256,640]{1,0:T(8,128)(2,1)S(1)} %get-tuple-element.33.half_ref), custom_call_target="tpu_custom_call" | custom-call | flops 1264999936 | bytes 1100000 | tf_op jit(solution)/shard_map/pallas_call | solution.py:23
  24.0 0.1 collective-permute-start.8
  24.1 3.4 %collective-permute-done.4 = bf16[528,256]{1,0:T(8,128)(2,1)S(1)} collective-permute-done((bf16[528,256]{1,0:T(8,128)(2,1)S(1)}, bf16[528,256]{1,0:T(8,128)(2,1)S(1)}, u32[]{:S(2)}, u32[]{:S(2)}) %collective-permute-start.4) | collective-permute-done | bytes 270368 | tf_op jit(solution)/shard_map/ppermute | solution.py:371
  27.5 0.1 convert_add_fusion.1
  27.6 1.6 %collective-permute-start.7 = (bf16[272,256]{1,0:T(8,128)(2,1)S(1)}, bf16[272,256]{1,0:T(8,128)(2,1)S(1)}, u32[]{:S(2)}, u32[]{:S(2)}) collective-permute-start(bf16[272,256]{1,0:T(8,128)(2,1)S(1)} %pad_maximum_fusion), channel_id=1, source_target_pairs={{0,2},{1,3},{2,0},{3,1},{4,6},{5,7},{6,4},{7,5},{8,9},{9,8},{10,11... | collective-permute-start | bytes 417800 | tf_op jit(solution)/shard_map/ppermute | solution.py:371
  29.3 0.2 convert_add_fusion
  29.5 0.4 collective-permute-start.10
  29.9 2.9 %collective-permute-done.7 = bf16[272,256]{1,0:T(8,128)(2,1)S(1)} collective-permute-done((bf16[272,256]{1,0:T(8,128)(2,1)S(1)}, bf16[272,256]{1,0:T(8,128)(2,1)S(1)}, u32[]{:S(2)}, u32[]{:S(2)}) %collective-permute-start.7) | collective-permute-done | bytes 139296 | tf_op jit(solution)/shard_map/ppermute | solution.py:371
  32.8 2.7 %collective-permute-start.9 = (bf16[144,256]{1,0:T(8,128)(2,1)S(1)}, bf16[144,256]{1,0:T(8,128)(2,1)S(1)}, u32[]{:S(2)}, u32[]{:S(2)}) collective-permute-start(bf16[144,256]{1,0:T(8,128)(2,1)S(1)} %pad_maximum_fusion.1), channel_id=1, source_target_pairs={{0,4},{1,5},{2,6},{3,7},{4,0},{5,1},{6,2},{7,3},{8,12},{9,13},{10,... | collective-permute-start | bytes 221192 | tf_op jit(solution)/shard_map/ppermute | solution.py:371
  35.5 2.6 %collective-permute-done.9.arrived_ref = bf16[144,256]{1,0:T(8,128)(2,1)S(1)} collective-permute-done((bf16[144,256]{1,0:T(8,128)(2,1)S(1)}, bf16[144,256]{1,0:T(8,128)(2,1)S(1)}, u32[]{:S(2)}, u32[]{:S(2)}) %collective-permute-start.9) | collective-permute-done | bytes 73760 | tf_op jit(solution)/shard_map/ppermute | solution.py:371
  38.2 1.6 %collective-permute-done.10.arrived_ref = bf16[256,640]{1,0:T(8,128)(2,1)S(1)} collective-permute-done((bf16[256,640]{1,0:T(8,128)(2,1)S(1)}, bf16[256,640]{1,0:T(8,128)(2,1)S(1)}, u32[]{:S(2)}, u32[]{:S(2)}) %collective-permute-start.10) | collective-permute-done | bytes 327712 | tf_op jit(solution)/shard_map/ppermute | solution.py:362
  39.7 0.1 collective-permute-start.11
  39.8 0.4 collective-permute-start.12
  40.2 1.8 %shard_map.130 = f32[256,640]{1,0:T(8,128)} custom-call(s32[5]{0:T(128)S(1)} %copy-done.9, f32[256,640]{1,0:T(8,128)S(1)} %slice.67.keep_ref, bf16[256,640]{1,0:T(8,128)(2,1)S(1)} %collective-permute-done.10.arrived_ref, f32[16,256]{1,0:T(8,128)S(1)} %constant_dynamic-slice_fusion.gains_ref), custom_call_target="tpu_custom_call" | custom-call | flops 920000000 | bytes 800000 | tf_op jit(solution)/shard_map/pallas_call | solution.py:23
  42.0 2.5 %collective-permute-done.12.refs_2_ = bf16[144,256]{1,0:T(8,128)(2,1)S(1)} collective-permute-done((bf16[144,256]{1,0:T(8,128)(2,1)S(1)}, bf16[144,256]{1,0:T(8,128)(2,1)S(1)}, u32[]{:S(2)}, u32[]{:S(2)}) %collective-permute-start.12) | collective-permute-done | bytes 73760 | tf_op jit(solution)/shard_map/ppermute | solution.py:362
  44.5 0.3 shard_map.128.total_ref
  44.9 0.9 %collective-permute-done.13.refs_3_ = bf16[144,256]{1,0:T(8,128)(2,1)S(1)} collective-permute-done((bf16[144,256]{1,0:T(8,128)(2,1)S(1)}, bf16[144,256]{1,0:T(8,128)(2,1)S(1)}, u32[]{:S(2)}, u32[]{:S(2)}) %collective-permute-start.13) | collective-permute-done | bytes 73760 | tf_op jit(solution)/shard_map/ppermute | solution.py:362
  45.8 1.3 %shard_map.129 = (f32[1024,128]{1,0:T(8,128)}, f32[1,1]{1,0:T(1,128)}) custom-call(f32[128,1024]{1,0:T(8,128)S(1)} %shard_map.128.total_ref, bf16[144,256]{1,0:T(8,128)(2,1)S(1)} %shard_map.127.refs_0_, bf16[144,256]{1,0:T(8,128)(2,1)S(1)} %collective-permute-done.11.refs_1_, bf16[144,256]{1,0:T(8,128)(2,1)S(1)} %collective-permute-done.12.refs_2_, ...), custom_call_target="tpu_custom_call" | custom-call | flops 1150000000 | bytes 1000000 | tf_op jit(solution)/shard_map/pallas_call | solution.py:555
  (48 shorter events, 0.3 us)
Async XLA Ops:
  0.6 7.4 %copy-start.3 = (bf16[256,1024]{1,0:T(8,128)(2,1)S(1)}, bf16[256,1024]{1,0:T(8,128)(2,1)}, u32[]{:S(2)}) copy-start(bf16[256,1024]{1,0:T(8,128)(2,1)} %clip_ref.1) | copy-start | bytes 1572868
  0.6 7.3 %copy-start = (bf16[1024,1024]{1,0:T(8,128)(2,1)S(1)}, bf16[1024,1024]{1,0:T(8,128)(2,1)}, u32[]{:S(2)}) copy-start(bf16[1024,1024]{1,0:T(8,128)(2,1)} %point_ref.1) | copy-start | bytes 6291460
  0.7 7.4 %copy-start.6 = (f32[3,1024]{1,0:T(4,128)S(1)}, f32[3,1024]{1,0:T(4,128)}, u32[]{:S(2)}) copy-start(f32[3,1024]{1,0:T(4,128)} %taps_ref.1) | copy-start | bytes 36868
  0.7 7.4 %copy-start.7 = (s32[8]{0:T(128)S(1)}, s32[8]{0:T(128)}, u32[]{:S(2)}) copy-start(s32[8]{0:T(128)} %lengths_ref.3) | copy-start | bytes 100
  2.4 5.7 %collective-permute-start = (bf16[64,1024]{1,0:T(8,128)(2,1)}, bf16[64,1024]{1,0:T(8,128)(2,1)S(1)}, u32[]{:S(2)}, u32[]{:S(2)}) collective-permute-start(bf16[64,1024]{1,0:T(8,128)(2,1)} %get-tuple-element.27), channel_id=1, source_target_pairs={{0,8},{8,0},{16,24},{24,16},{1,9},{9,1},{17,25},{25,17},{2,10},{10... | collective-permute-start | bytes 393224 | tf_op jit(solution)/shard_map/ppermute | solution.py:362
  2.8 5.2 %collective-permute-start.1 = (bf16[64,1024]{1,0:T(8,128)(2,1)}, bf16[64,1024]{1,0:T(8,128)(2,1)S(1)}, u32[]{:S(2)}, u32[]{:S(2)}) collective-permute-start(bf16[64,1024]{1,0:T(8,128)(2,1)} %get-tuple-element.27), channel_id=1, source_target_pairs={{8,16},{9,17},{10,18},{11,19},{12,20},{13,21},{14,22},{15,23},{16,... | collective-permute-start | bytes 393224 | tf_op jit(solution)/shard_map/ppermute | solution.py:371
  3.5 10.2 %collective-permute-start.2 = (s32[8,128]{1,0:T(8,128)}, s32[8,128]{1,0:T(8,128)S(1)}, u32[]{:S(2)}, u32[]{:S(2)}) collective-permute-start(s32[8,128]{1,0:T(8,128)} %get-tuple-element.29), channel_id=1, source_target_pairs={{0,1},{1,0},{2,3},{3,2},{4,5},{5,4},{6,7},{7,6},{9,10},{10,9},{11,... | collective-permute-start | bytes 12296 | tf_op jit(solution)/shard_map/ppermute | solution.py:371
  8.0 6.3 %copy-start.1 = (f32[16,1024]{1,0:T(8,128)S(1)}, f32[16,1024]{1,0:T(8,128)}, u32[]{:S(2)}) copy-start(f32[16,1024]{1,0:T(8,128)} %gains_ref) | copy-start | bytes 196612
  8.0 6.3 %copy-start.2 = (bf16[1024,640]{1,0:T(8,128)(2,1)S(1)}, bf16[1024,640]{1,0:T(8,128)(2,1)}, u32[]{:S(2)}) copy-start(bf16[1024,640]{1,0:T(8,128)(2,1)} %weight_ref.1) | copy-start | bytes 3932164
  8.0 6.3 %copy-start.9 = (s32[5]{0:T(128)S(1)}, s32[5]{0:T(128)}, u32[]{:S(2)}) copy-start(s32[5]{0:T(128)} %subject_ref.7) | copy-start | bytes 64
  9.9 17.5 %collective-permute-start.5 = (bf16[256,1024]{1,0:T(8,128)(2,1)S(1)}, bf16[256,1024]{1,0:T(8,128)(2,1)S(1)}, u32[]{:S(2)}, u32[]{:S(2)}) collective-permute-start(bf16[256,1024]{1,0:T(8,128)(2,1)S(1)} %get-tuple-element.36.depth_ref.refs_2_), channel_id=1, source_target_pairs={{0,16},{8,24},{16,0},{24,8},{1,17},{9,25},{17,1},{25,9},{2,18},{10... | collective-permute-start | bytes 1572872 | tf_op jit(solution)/shard_map/ppermute | solution.py:362
  13.7 13.8 %collective-permute-start.6 = (bf16[256,1024]{1,0:T(8,128)(2,1)S(1)}, bf16[256,1024]{1,0:T(8,128)(2,1)S(1)}, u32[]{:S(2)}, u32[]{:S(2)}) collective-permute-start(bf16[256,1024]{1,0:T(8,128)(2,1)S(1)} %get-tuple-element.36.depth_ref.refs_2_), channel_id=1, source_target_pairs={{0,8},{8,0},{16,24},{24,16},{1,9},{9,1},{17,25},{25,17},{2,10},{10... | collective-permute-start | bytes 1572872 | tf_op jit(solution)/shard_map/ppermute | solution.py:362
  13.7 2.1 %copy-start.4 = (bf16[256,640]{1,0:T(8,128)(2,1)S(1)}, bf16[256,640]{1,0:T(8,128)(2,1)}, u32[]{:S(2)}) copy-start(bf16[256,640]{1,0:T(8,128)(2,1)} %bold_ref.3) | copy-start | bytes 983044
  13.7 2.1 %copy-start.5 = (f32[16,640]{1,0:T(8,128)S(1)}, f32[16,640]{1,0:T(8,128)}, u32[]{:S(2)}) copy-start(f32[16,640]{1,0:T(8,128)} %hrf_ref.1) | copy-start | bytes 122884
  13.7 2.1 %copy-start.8 = (s32[5]{0:T(128)S(1)}, s32[5]{0:T(128)}, u32[]{:S(2)}) copy-start(s32[5]{0:T(128)} %live_ref.3) | copy-start | bytes 64
  13.7 2.1 %collective-permute-start.3 = (s32[8,128]{1,0:T(8,128)S(1)}, s32[8,128]{1,0:T(8,128)S(1)}, u32[]{:S(2)}, u32[]{:S(2)}) collective-permute-start(s32[8,128]{1,0:T(8,128)S(1)} %collective-permute-done.2.mine_ref), channel_id=1, source_target_pairs={{0,8},{8,0},{16,24},{24,16},{1,9},{9,1},{17,25},{25,17},{2,10},{10... | collective-permute-start | bytes 12296 | tf_op jit(solution)/shard_map/ppermute | solution.py:362
  20.9 6.5 %collective-permute-start.4 = (bf16[528,256]{1,0:T(8,128)(2,1)S(1)}, bf16[528,256]{1,0:T(8,128)(2,1)S(1)}, u32[]{:S(2)}, u32[]{:S(2)}) collective-permute-start(bf16[528,256]{1,0:T(8,128)(2,1)S(1)} %get-tuple-element.35), channel_id=1, source_target_pairs={{0,1},{1,0},{2,3},{3,2},{4,5},{5,4},{6,7},{7,6},{8,10},{9,11},{10,... | collective-permute-start | bytes 811016 | tf_op jit(solution)/shard_map/ppermute | solution.py:371
  24.0 5.3 %collective-permute-start.8 = (bf16[512,640]{1,0:T(8,128)(2,1)S(1)}, bf16[512,640]{1,0:T(8,128)(2,1)S(1)}, u32[]{:S(2)}, u32[]{:S(2)}) collective-permute-start(bf16[512,640]{1,0:T(8,128)(2,1)S(1)} %get-tuple-element.40), channel_id=1, source_target_pairs={{0,8},{8,0},{16,24},{24,16},{1,9},{9,1},{17,25},{25,17},{2,10},{10... | collective-permute-start | bytes 1966088 | tf_op jit(solution)/shard_map/ppermute | solution.py:362
  27.6 5.1 %collective-permute-start.7 = (bf16[272,256]{1,0:T(8,128)(2,1)S(1)}, bf16[272,256]{1,0:T(8,128)(2,1)S(1)}, u32[]{:S(2)}, u32[]{:S(2)}) collective-permute-start(bf16[272,256]{1,0:T(8,128)(2,1)S(1)} %pad_maximum_fusion), channel_id=1, source_target_pairs={{0,2},{1,3},{2,0},{3,1},{4,6},{5,7},{6,4},{7,5},{8,9},{9,8},{10,11... | collective-permute-start | bytes 417800 | tf_op jit(solution)/shard_map/ppermute | solution.py:371
  29.3 15.6 %collective-permute-start.14 = (bf16[256,1024]{1,0:T(8,128)(2,1)S(1)}, bf16[256,1024]{1,0:T(8,128)(2,1)S(1)}, u32[]{:S(2)}, u32[]{:S(2)}) collective-permute-start(bf16[256,1024]{1,0:T(8,128)(2,1)S(1)} %collective-permute-done.5.refs_4_), channel_id=1, source_target_pairs={{0,8},{8,0},{16,24},{24,16},{1,9},{9,1},{17,25},{25,17},{2,10},{10... | collective-permute-start | bytes 1572872 | tf_op jit(solution)/shard_map/ppermute | solution.py:362
  29.5 10.2 %collective-permute-start.10 = (bf16[256,640]{1,0:T(8,128)(2,1)S(1)}, bf16[256,640]{1,0:T(8,128)(2,1)S(1)}, u32[]{:S(2)}, u32[]{:S(2)}) collective-permute-start(bf16[256,640]{1,0:T(8,128)(2,1)S(1)} %slice.89), channel_id=1, source_target_pairs={{0,16},{8,24},{16,0},{24,8},{1,17},{9,25},{17,1},{25,9},{2,18},{10... | collective-permute-start | bytes 983048 | tf_op jit(solution)/shard_map/ppermute | solution.py:362
  32.8 5.3 %collective-permute-start.9 = (bf16[144,256]{1,0:T(8,128)(2,1)S(1)}, bf16[144,256]{1,0:T(8,128)(2,1)S(1)}, u32[]{:S(2)}, u32[]{:S(2)}) collective-permute-start(bf16[144,256]{1,0:T(8,128)(2,1)S(1)} %pad_maximum_fusion.1), channel_id=1, source_target_pairs={{0,4},{1,5},{2,6},{3,7},{4,0},{5,1},{6,2},{7,3},{8,12},{9,13},{10,... | collective-permute-start | bytes 221192 | tf_op jit(solution)/shard_map/ppermute | solution.py:371
  39.7 4.8 %collective-permute-start.11 = (bf16[144,256]{1,0:T(8,128)(2,1)S(1)}, bf16[144,256]{1,0:T(8,128)(2,1)S(1)}, u32[]{:S(2)}, u32[]{:S(2)}) collective-permute-start(bf16[144,256]{1,0:T(8,128)(2,1)S(1)} %shard_map.127.refs_0_), channel_id=1, source_target_pairs={{0,8},{8,0},{16,24},{24,16},{1,9},{9,1},{17,25},{25,17},{2,10},{10... | collective-permute-start | bytes 221192 | tf_op jit(solution)/shard_map/ppermute | solution.py:362
  39.8 4.7 %collective-permute-start.12 = (bf16[144,256]{1,0:T(8,128)(2,1)S(1)}, bf16[144,256]{1,0:T(8,128)(2,1)S(1)}, u32[]{:S(2)}, u32[]{:S(2)}) collective-permute-start(bf16[144,256]{1,0:T(8,128)(2,1)S(1)} %shard_map.127.refs_0_), channel_id=1, source_target_pairs={{0,16},{8,24},{16,0},{24,8},{1,17},{9,25},{17,1},{25,9},{2,18},{10... | collective-permute-start | bytes 221192 | tf_op jit(solution)/shard_map/ppermute | solution.py:362
  44.5 1.3 %collective-permute-start.13 = (bf16[144,256]{1,0:T(8,128)(2,1)S(1)}, bf16[144,256]{1,0:T(8,128)(2,1)S(1)}, u32[]{:S(2)}, u32[]{:S(2)}) collective-permute-start(bf16[144,256]{1,0:T(8,128)(2,1)S(1)} %collective-permute-done.12.refs_2_), channel_id=1, source_target_pairs={{0,8},{8,0},{16,24},{24,16},{1,9},{9,1},{17,25},{25,17},{2,10},{10... | collective-permute-start | bytes 221192 | tf_op jit(solution)/shard_map/ppermute | solution.py:362

commit v3 on v2

--- a/solution.py
+++ b/solution.py
@@ -33,54 +33,107 @@
     )(*[value for _, value in ins])
 
 
-def session_starts(lengths_ref, time):
+def session_starts(ends, time):
     start = jnp.zeros_like(time)
-    end = jnp.int32(0)
-    for at in range(lengths_ref.shape[0]):
-        end = end + lengths_ref[at]
+    for end in ends:
         start = jnp.where(time >= end, end, start)
     return start
 
 
-def session_stops(lengths_ref, time):
+def session_stops(ends, time):
     stop = jnp.zeros_like(time)
-    ends = []
-    end = jnp.int32(0)
-    for at in range(lengths_ref.shape[0]):
-        end = end + lengths_ref[at]
-        ends.append(end)
     for end in reversed(ends):
         stop = jnp.where(time < end, end, stop)
     return stop
 
 
-def pack_kernel(blocks, subject_ref, live_ref, tail_ref, head_ref, bold_ref, payload_ref, ends_ref):
+def facts_of(ref, blocks):
+    row = [ref[at : at + 1, :] for at in range(ref.shape[0])]
+    return row[:blocks], row[blocks : 2 * blocks], row[2 * blocks :]
+
+
+def pack_kernel(
+    rows,
+    blocks,
+    subject_hbm,
+    live_hbm,
+    lengths_hbm,
+    clip_ref,
+    bold_ref,
+    payload_ref,
+    ends_ref,
+    facts_ref,
+    subject_ref,
+    live_ref,
+    lengths_ref,
+    sems,
+):
     slots = bold_ref.shape[1]
-    payload_ref[: 2 * MARGIN, :] = tail_ref[...]
-    payload_ref[2 * MARGIN : 3 * MARGIN, :] = head_ref[...]
-    payload_ref[3 * MARGIN :, :slots] = bold_ref[...]
+    tail = 2 * MARGIN
+    moves = [
+        (clip_ref.at[pl.ds(rows - tail, tail), :], payload_ref.at[pl.ds(0, tail), :]),
+        (clip_ref.at[pl.ds(0, MARGIN), :], payload_ref.at[pl.ds(tail, MARGIN), :]),
+        (
+            bold_ref.at[pl.ds(0, MARGIN), :],
+            payload_ref.at[pl.ds(tail + MARGIN, MARGIN), pl.ds(0, slots)],
+        ),
+        (subject_hbm, subject_ref),
+        (live_hbm, live_ref),
+        (lengths_hbm, lengths_ref),
+    ]
+    copies = [pltpu.make_async_copy(*move, sems.at[at]) for at, move in enumerate(moves)]
+    for copy in copies:
+        copy.start()
     payload_ref[3 * MARGIN :, slots:] = jnp.zeros_like(payload_ref[3 * MARGIN :, slots:])
+    for copy in copies[3:]:
+        copy.wait()
     row = lax.broadcasted_iota(jnp.int32, ends_ref.shape, 0)
     last = blocks - 1
     ends = jnp.where(row == 0, subject_ref[0], live_ref[0])
     ends = jnp.where(row == 2, subject_ref[last], ends)
     ends_ref[...] = jnp.where(row == 3, live_ref[last], ends)
-
-
-def gain_kernel(blocks, subject_ref, gains_ref, weight_ref, effective_ref):
-    rows = [gains_ref[pl.ds(subject_ref[b], 1), :] for b in range(blocks)]
-    rows += [rows[-1]] * (-blocks % 8)
-    cols = jnp.transpose(jnp.concatenate(rows, axis=0))
-    for b in range(blocks):
-        lanes = slice(b * BLOCK_VOX, (b + 1) * BLOCK_VOX)
-        effective_ref[:, lanes] = (
-            weight_ref[:, lanes].astype(F32) * cols[:, b : b + 1]
-        ).astype(BF16)
+    values = [subject_ref[b] for b in range(blocks)] + [live_ref[b] for b in range(blocks)]
+    end = jnp.int32(0)
+    for at in range(lengths_ref.shape[0]):
+        end = end + lengths_ref[at]
+        values.append(end)
+    row = lax.broadcasted_iota(jnp.int32, facts_ref.shape, 0)
+    facts = jnp.full(facts_ref.shape, end, jnp.int32)
+    for at, value in enumerate(values):
+        facts = jnp.where(row == at, value, facts)
+    facts_ref[...] = facts
+    for copy in copies[:3]:
+        copy.wait()
+
+
+def gain_kernel(blocks, facts_ref, gains_ref, weight_ref, core_ref, effective_ref, response_ref):
+    slots = blocks * BLOCK_VOX
+    subjects = gains_ref.shape[0]
+    whole = gains_ref[...]
+    high = whole.astype(BF16).astype(F32)
+    middle = (whole - high).astype(BF16).astype(F32)
+    low = whole - high - middle
+    terms = jnp.concatenate([high, middle, low], axis=0).astype(BF16)
+    owner = jnp.concatenate(facts_of(facts_ref, blocks)[0], axis=1)
+    row = lax.broadcasted_iota(jnp.int32, (3 * subjects, slots), 0) % subjects
+    pick = jnp.where(row == owner, 1.0, 0.0).astype(BF16)
+    scale = lax.dot_general(
+        terms, pick, (((0,), (0,)), ((), ())), preferred_element_type=F32
+    )
+    effective_ref[...] = (weight_ref[...].astype(F32) * scale).astype(BF16)
+    for b in range(0, blocks, 2):
+        many = min(2, blocks - b)
+        lanes = slice(b * BLOCK_VOX, (b + many) * BLOCK_VOX)
+        part = jnp.dot(core_ref[...], effective_ref[:, lanes], preferred_element_type=F32)
+        part = part.astype(BF16).astype(F32)
+        for c in range(many):
+            response_ref[b + c] = part[:, c * BLOCK_VOX : (c + 1) * BLOCK_VOX]
 
 
 def core_kernel(
     rows,
-    lengths_ref,
+    blocks,
+    facts_ref,
     clip_ref,
     near_ref,
     far_ref,
@@ -106,10 +159,11 @@
         ext[2 * MARGIN + rows :, :] = far_ref[2 * MARGIN : 3 * MARGIN, :]
 
     first = lax.axis_index("tm") * rows - MARGIN
+    session_ends = facts_of(facts_ref, blocks)[2]
     taps = [taps_ref[k : k + 1, :] for k in range(KERNEL_TAPS)]
     for at in range(0, rows + 2 * MARGIN, 16):
         time = first + at + lax.broadcasted_iota(jnp.int32, (16, 128), 0)
-        since = time - session_starts(lengths_ref, time)
+        since = time - session_starts(session_ends, time)
         values = ext[at : at + 32, :].astype(F32)
         total = taps[0] * values[16:32]
         for k in range(1, KERNEL_TAPS):
@@ -139,108 +193,111 @@
     return lax.axis_index("vox") ^ mask
 
 
-def voxel_kernel(
+def spread_taps(hrf_ref, taps):
+    for k in range(HRF):
+        taps[k] = jnp.broadcast_to(hrf_ref[k : k + 1, :], taps.shape[1:])
+
+
+def filtered(at, blocks, taps, limit, source, base, step):
+    pairs = [(b, h) for b in range(blocks) for h in (0, 8)]
+    depth = {h: limit[at + h : at + h + 8, :] for h in (0, 8)}
+    total = {}
+    for b, h in pairs:
+        lanes = slice(b * BLOCK_VOX, (b + 1) * BLOCK_VOX)
+        row = at + h + base
+        total[b, h] = taps[0, :, lanes] * source[b, row : row + 8, :]
+    for k in range(1, HRF):
+        valid = {h: depth[h] >= k for h in (0, 8)}
+        for b, h in pairs:
+            lanes = slice(b * BLOCK_VOX, (b + 1) * BLOCK_VOX)
+            row = at + h + base + step * k
+            moved = jnp.where(valid[h], source[b, row : row + 8, :], 0.0)
+            total[b, h] = total[b, h] + taps[k, :, lanes] * moved
+    return total
+
+
+def forward_kernel(
+    rows, blocks, facts_ref, response_ref, hrf_ref, bold_ref, near_ref, far_ref, misfit_ref, bold, since, taps
+):
+    lead_rows = rows + MARGIN
+    slots = blocks * BLOCK_VOX
+    odd = lax.axis_index("tm") % 2
+    bold[:rows, :] = bold_ref[...]
+
+    @pl.when(odd == 0)
+    def _():
+        bold[rows:, :] = near_ref[3 * MARGIN :, :slots]
+
+    @pl.when(odd == 1)
+    def _():
+        bold[rows:, :] = far_ref[3 * MARGIN :, :slots]
+
+    first = lax.axis_index("tm") * rows
+    time = first + lax.broadcasted_iota(jnp.int32, (lead_rows, BLOCK_VOX), 0)
+    since[...] = time - session_starts(facts_of(facts_ref, blocks)[2], time)
+    spread_taps(hrf_ref, taps)
+    for at in range(0, lead_rows, 16):
+        total = filtered(at, blocks, taps, since, response_ref, MARGIN, -1)
+        for b in range(blocks):
+            target = bold[at : at + 16, b * BLOCK_VOX : (b + 1) * BLOCK_VOX].astype(F32)
+            for h in (0, 8):
+                misfit_ref[b, at + h : at + h + 8, :] = total[b, h] - target[h : h + 8]
+
+
+def backward_kernel(
     rows,
     blocks,
     orders,
     width,
-    lengths_ref,
-    subject_ref,
-    live_ref,
+    facts_ref,
     mine_ref,
     twin_ref,
-    core_ref,
+    misfit_ref,
     effective_ref,
     hrf_ref,
-    bold_ref,
-    near_ref,
-    far_ref,
     half_ref,
     send_ref,
     loss_ref,
-    response,
     grads,
-    bold,
-    since,
     left,
-    scale,
+    taps,
 ):
-    ext_rows = rows + 2 * MARGIN
     lead_rows = rows + MARGIN
-    slots = blocks * BLOCK_VOX
-    odd = lax.axis_index("tm") % 2
-    bold[:rows, :] = bold_ref[...]
-
-    @pl.when(odd == 0)
-    def _():
-        bold[rows:, :] = near_ref[3 * MARGIN :, :slots]
-
-    @pl.when(odd == 1)
-    def _():
-        bold[rows:, :] = far_ref[3 * MARGIN :, :slots]
-
-    first = lax.axis_index("tm") * rows
-    time = first + lax.broadcasted_iota(jnp.int32, (lead_rows, 128), 0)
-    since[...] = time - session_starts(lengths_ref, time)
-    left[...] = session_stops(lengths_ref, time) - 1 - time
-
-    first_core = odd == 0
+    own_subjects, own_lives, session_ends = facts_of(facts_ref, blocks)
+    first_core = lax.axis_index("tm") % 2 == 0
     low = jnp.where(first_core, mine_ref[...], twin_ref[...])
     high = jnp.where(first_core, twin_ref[...], mine_ref[...])
     even_vox = lax.axis_index("vox") % 2 == 0
     before = jnp.where(even_vox, high, low)
     after = jnp.where(even_vox, low, high)
-    subjects = [before[2:3]] + [subject_ref[b] for b in range(blocks)] + [after[0:1]]
-    lives = [before[3:4]] + [live_ref[b] for b in range(blocks)] + [after[1:2]]
-    lane = lax.broadcasted_iota(jnp.int32, (16, BLOCK_VOX), 1)
+    subjects = [before[2:3]] + own_subjects + [after[0:1]]
+    lives = [before[3:4]] + own_lives + [after[1:2]]
+    lane = lax.broadcasted_iota(jnp.int32, (8, BLOCK_VOX), 1)
+    lost = jnp.zeros((8, BLOCK_VOX), F32)
     for b in range(blocks):
-        count = jnp.full((1, BLOCK_VOX), lives[b + 1], jnp.int32)
+        count = lives[b + 1]
         count = count + jnp.where(subjects[b] == subjects[b + 1], lives[b], 0)
         count = count + jnp.where(subjects[b + 2] == subjects[b + 1], lives[b + 2], 0)
         inverse = 1.0 / jnp.maximum(count, 1).astype(F32)
-        scale[b] = jnp.where(lane < lives[b + 1], inverse, 0.0)
-
-    for b in range(0, blocks, 2):
-        many = min(2, blocks - b)
-        lanes = slice(b * BLOCK_VOX, (b + many) * BLOCK_VOX)
-        part = jnp.dot(core_ref[...], effective_ref[:, lanes], preferred_element_type=F32)
-        part = part.astype(BF16).astype(F32)
-        for c in range(many):
-            response[b + c] = part[:, c * BLOCK_VOX : (c + 1) * BLOCK_VOX]
-
-    def one_block(b, lost):
-        lanes = pl.ds(pl.multiple_of(b * BLOCK_VOX, BLOCK_VOX), BLOCK_VOX)
-        taps = [jnp.broadcast_to(hrf_ref[k : k + 1, lanes], (16, BLOCK_VOX)) for k in range(HRF)]
-        weight = scale[b]
+        weight = jnp.where(lane < lives[b + 1], inverse, 0.0)
         double = 2.0 * weight
-        for at in range(0, lead_rows, 16):
-            depth = since[at : at + 16, :]
-            total = taps[0] * response[b, MARGIN + at : MARGIN + at + 16, :]
-            for k in range(1, HRF):
-                moved = response[b, MARGIN + at - k : MARGIN + at - k + 16, :]
-                total = total + taps[k] * jnp.where(depth >= k, moved, 0.0)
-            misfit = total - bold[at : at + 16, lanes].astype(F32)
-            grads[b, at : at + 16, :] = double * misfit
+        for at in range(0, lead_rows, 8):
+            misfit = misfit_ref[b, at : at + 8, :]
+            grads[b, at : at + 8, :] = double * misfit
             if at < rows:
-                cost = weight * misfit * misfit
-                lost = lost + cost[:8] + cost[8:]
-        for at in range(0, rows, 16):
-            depth = left[at : at + 16, :]
-            total = taps[0] * grads[b, at : at + 16, :]
-            for k in range(1, HRF):
-                moved = grads[b, at + k : at + k + 16, :]
-                total = total + taps[k] * jnp.where(depth >= k, moved, 0.0)
-            half_ref[at : at + 16, lanes] = total.astype(BF16)
-        return lost
-
-    lost = lax.fori_loop(0, blocks, one_block, jnp.zeros((8, BLOCK_VOX), F32))
+                lost = lost + weight * misfit * misfit
     loss_ref[...] = lost
-    high = lost.astype(BF16).astype(F32)
-    pair = jnp.concatenate([high, lost - high], axis=0)
-    pad = jnp.zeros((16, rows - BLOCK_VOX), F32)
-    pieces = 1 << len(orders[0])
-    halves = pieces // 2
-    send_ref[halves * width :, :] = jnp.concatenate([pair, pad], axis=1).astype(BF16)
+    time = lax.axis_index("tm") * rows + lax.broadcasted_iota(jnp.int32, (rows, BLOCK_VOX), 0)
+    left[...] = session_stops(session_ends, time) - 1 - time
+    spread_taps(hrf_ref, taps)
+    for at in range(0, rows, 16):
+        total = filtered(at, blocks, taps, left, grads, 0, 1)
+        for b in range(blocks):
+            half_ref[at : at + 16, b * BLOCK_VOX : (b + 1) * BLOCK_VOX] = jnp.concatenate(
+                [total[b, 0], total[b, 8]], axis=0
+            ).astype(BF16)
+    halves = 1 << (len(orders[0]) - 1)
+    send_ref[halves * width :, :] = loss_pair(lost, rows)
     for p in range(halves):
         at = pl.multiple_of(picked(halves + p, orders) * width, width)
         send_ref[p * width : (p + 1) * width, :] = lax.dot_general(
@@ -380,37 +437,44 @@
         other = v + 1 if v % 2 else v - 1
         return (t, other) if 0 <= other < vox_count else None
 
-    payload, ends = pl.pallas_call(
-        functools.partial(pack_kernel, blocks),
+    fact_rows = 2 * blocks + session_lengths.shape[0]
+    fact_rows += -fact_rows % 8
+    payload, ends, facts = pl.pallas_call(
+        functools.partial(pack_kernel, rows, blocks),
         out_shape=(
-            jax.ShapeDtypeStruct((4 * MARGIN, feats), BF16),
-            jax.ShapeDtypeStruct((8, BLOCK_VOX), jnp.int32),
-        ),
-        grid=(1,),
-        in_specs=[
-            SMEM,
-            SMEM,
-            pl.BlockSpec((2 * MARGIN, feats), lambda i: (rows // (2 * MARGIN) - 1, 0)),
-            pl.BlockSpec((MARGIN, feats), lambda i: (0, 0)),
-            pl.BlockSpec((MARGIN, slots), lambda i: (0, 0)),
+            pltpu.VMEM((4 * MARGIN, feats), BF16),
+            pltpu.VMEM((8, BLOCK_VOX), jnp.int32),
+            pltpu.VMEM((fact_rows, BLOCK_VOX), jnp.int32),
+        ),
+        in_specs=[HBM] * 5,
+        out_specs=(VMEM, VMEM, VMEM),
+        scratch_shapes=[
+            pltpu.SMEM((blocks,), jnp.int32),
+            pltpu.SMEM((blocks,), jnp.int32),
+            pltpu.SMEM(session_lengths.shape, jnp.int32),
+            pltpu.SemaphoreType.DMA((6,)),
         ],
-        out_specs=(VMEM, VMEM),
         cost_estimate=pl.CostEstimate(
             flops=int(6 * 1.15e9), bytes_accessed=1000000, transcendentals=0
         ),
-    )(block_subject, block_live, clip_features, clip_features, bold_target)
+    )(
+        *[
+            pltpu.with_memory_space_constraint(value, pltpu.HBM)
+            for value in (block_subject, block_live, session_lengths, clip_features, bold_target)
+        ]
+    )
     far = across(payload, next_tm)
     mine = across(ends, next_vox)
     near = swap_tm(payload, 0)
 
     depth_half, core_out = call(
-        functools.partial(core_kernel, rows),
+        functools.partial(core_kernel, rows, blocks),
         (
             jax.ShapeDtypeStruct((rows, feats), BF16),
             jax.ShapeDtypeStruct((rows + 2 * MARGIN, feats), BF16),
         ),
         [
-            (SMEM, session_lengths),
+            (VMEM, facts),
             (VMEM, clip_features),
             (VMEM, near),
             (VMEM, far),
@@ -423,44 +487,56 @@
             pltpu.VMEM((rows + 2 * MARGIN, feats), BF16),
         ],
     )
-    core_out, late_gains, mine = lax.optimization_barrier(
-        (core_out, subject_feature_gains, mine)
-    )
+    core_out, late_gains = lax.optimization_barrier((core_out, subject_feature_gains))
+    effective, response = call(
+        functools.partial(gain_kernel, blocks),
+        (
+            jax.ShapeDtypeStruct((feats, slots), BF16),
+            jax.ShapeDtypeStruct((blocks, rows + 2 * MARGIN, BLOCK_VOX), F32),
+        ),
+        [(VMEM, facts), (VMEM, late_gains), (VMEM, readout_weight), (VMEM, core_out)],
+        1.5,
+    )
+    response, mine = lax.optimization_barrier((response, mine))
     twin = swap_tm(mine, 0)
-    effective = call(
-        functools.partial(gain_kernel, blocks),
-        jax.ShapeDtypeStruct((feats, slots), BF16),
-        [(SMEM, block_subject), (VMEM, late_gains), (VMEM, readout_weight)],
-        1.5,
-    )
-    half, send, lost = call(
-        functools.partial(voxel_kernel, rows, blocks, orders, width),
-        (
-            jax.ShapeDtypeStruct((rows, slots), BF16),
-            jax.ShapeDtypeStruct((feats // 2 + 16, rows), BF16),
-            jax.ShapeDtypeStruct((8, BLOCK_VOX), F32),
-        ),
+    misfit = call(
+        functools.partial(forward_kernel, rows, blocks),
+        jax.ShapeDtypeStruct((blocks, rows + MARGIN, BLOCK_VOX), F32),
         [
-            (SMEM, session_lengths),
-            (SMEM, block_subject),
-            (SMEM, block_live),
-            (VMEM, mine),
-            (VMEM, twin),
-            (VMEM, core_out),
-            (VMEM, effective),
+            (VMEM, facts),
+            (VMEM, response),
             (VMEM, hrf_kernel),
             (VMEM, bold_target),
             (VMEM, near),
             (VMEM, far),
         ],
-        5.0,
+        1.5,
         [
-            pltpu.VMEM((blocks, rows + 2 * MARGIN, BLOCK_VOX), F32),
-            pltpu.VMEM((blocks, rows + MARGIN, BLOCK_VOX), F32),
             pltpu.VMEM((rows + MARGIN, slots), BF16),
             pltpu.VMEM((rows + MARGIN, BLOCK_VOX), jnp.int32),
-            pltpu.VMEM((rows + MARGIN, BLOCK_VOX), jnp.int32),
-            pltpu.VMEM((blocks, 16, BLOCK_VOX), F32),
+            pltpu.VMEM((HRF, 8, slots), F32),
+        ],
+    )
+    half, send, lost = call(
+        functools.partial(backward_kernel, rows, blocks, orders, width),
+        (
+            jax.ShapeDtypeStruct((rows, slots), BF16),
+            jax.ShapeDtypeStruct((feats // 2 + 16, rows), BF16),
+            jax.ShapeDtypeStruct((8, BLOCK_VOX), F32),
+        ),
+        [
+            (VMEM, facts),
+            (VMEM, mine),
+            (VMEM, twin),
+            (VMEM, misfit),
+            (VMEM, effective),
+            (VMEM, hrf_kernel),
+        ],
+        2.5,
+        [
+            pltpu.VMEM((blocks, rows + MARGIN, BLOCK_VOX), F32),
+            pltpu.VMEM((rows, BLOCK_VOX), jnp.int32),
+            pltpu.VMEM((HRF, 8, slots), F32),
         ],
     )
     keep, raw_send, raw_keep = call(

time: 47.2 us -> 45 us (0.953)
  Pallas kernels: 15 us -> 11.9 us
  starting transfers between devices: 16.6 us -> 17.7 us
    pallas_call x8 -> x9, Pallas kernels: 12 us -> 9.63 us  [call(): pl.pallas_call(body, out_shape=outs, in_specs=[spec for spec, _ in ins],...]
    ppermute x5, starting transfers between devices: 11 us -> 12 us  [across(): return lax.ppermute(value, ('tm', 'vox'), pairs)]
    pallas_call x1, Pallas kernels: 1.69 us -> 1.05 us  [shards(): pl.pallas_call(functools.partial(pack_kernel, rows, blocks), out_shape=(p...]
  transfers between devices with their start and end apart: 15 -> 15, of which waited for: 6 -> 7; matrix products, arithmetic and copies ran while one was open for 1% -> 1% of each run, Pallas kernels for 26% -> 21%
where the time goes in v3:
time: 45 us; the launch traced here: 44.8 us
  starting transfers between devices  17.7 us (39%)
  waiting for transfers between devices  13.7 us (30%)
  Pallas kernels  11.9 us (26%)
  between operations  0.96 us (2%)
    ppermute x5, starting transfers between devices, across(): return lax.ppermute(value, ('tm', 'vox'), pairs)  12 us
    pallas_call x9, Pallas kernels, call(): pl.pallas_call(body, out_shape=outs, in_specs=[spec for spec, _ in ins],...  9.63 us
    ppermute x5, waiting for transfers between devices, across(): return lax.ppermute(value, ('tm', 'vox'), pairs)  8.43 us
    ppermute x10, starting transfers between devices, swap_tm(): lax.ppermute(value, 'tm', [(i, i ^ 1 << bit) for i in range(tm_count)])  5.7 us
    ppermute x10, waiting for transfers between devices, swap_tm(): lax.ppermute(value, 'tm', [(i, i ^ 1 << bit) for i in range(tm_count)])  5.24 us
    pallas_call x1, Pallas kernels, shards(): pl.pallas_call(functools.partial(last_kernel, len(early), len(late), widt...  1.26 us
    pallas_call x1, Pallas kernels, shards(): pl.pallas_call(functools.partial(pack_kernel, rows, blocks), out_shape=(p...  1.05 us
  transfers between devices with their start and end apart: 15, of which 7 were waited for; matrix products, arithmetic and copies ran while one was open for 1% of the time, Pallas kernels for 21%

profile of v3, /device:TPU:0, one launch (start us, length us, event | category | flops | bytes accessed | tf_op | source)
XLA Modules:
  0.0 44.8 jit_solution(13986858134907095811)
XLA Ops:
  0.7 1.0 %shard_map.121 = (bf16[64,1024]{1,0:T(8,128)(2,1)S(1)}, s32[8,128]{1,0:T(8,128)S(1)}, s32[24,128]{1,0:T(8,128)S(1)}) custom-call(s32[5]{0:T(128)} %subject_ref.1, s32[5]{0:T(128)} %live_hbm.1, s32[8]{0:T(128)} %lengths_hbm.1, bf16[256,1024]{1,0:T(8,128)(2,1)} %clip_ref.3, bf16[256,640]{1,0:T(8,128)(2,1)} %bold_ref.3), custom_call_target="tpu_custom_call" | custom-call | flops 6899999744 | bytes 1000000 | tf_op jit(solution)/shard_map/pallas_call | solution.py:442
  1.7 0.5 %collective-permute-start = (bf16[64,1024]{1,0:T(8,128)(2,1)S(1)}, bf16[64,1024]{1,0:T(8,128)(2,1)S(1)}, u32[]{:S(2)}, u32[]{:S(2)}) collective-permute-start(bf16[64,1024]{1,0:T(8,128)(2,1)S(1)} %get-tuple-element.32), channel_id=1, source_target_pairs={{0,8},{8,0},{16,24},{24,16},{1,9},{9,1},{17,25},{25,17},{2,10},{10... | collective-permute-start | bytes 393224 | tf_op jit(solution)/shard_map/ppermute | solution.py:419
  2.2 0.7 %collective-permute-start.1 = (bf16[64,1024]{1,0:T(8,128)(2,1)S(1)}, bf16[64,1024]{1,0:T(8,128)(2,1)S(1)}, u32[]{:S(2)}, u32[]{:S(2)}) collective-permute-start(bf16[64,1024]{1,0:T(8,128)(2,1)S(1)} %get-tuple-element.32), channel_id=1, source_target_pairs={{8,16},{9,17},{10,18},{11,19},{12,20},{13,21},{14,22},{15,23},{16,... | collective-permute-start | bytes 393224 | tf_op jit(solution)/shard_map/ppermute | solution.py:428
  2.9 4.4 %collective-permute-start.2 = (s32[8,128]{1,0:T(8,128)S(1)}, s32[8,128]{1,0:T(8,128)S(1)}, u32[]{:S(2)}, u32[]{:S(2)}) collective-permute-start(s32[8,128]{1,0:T(8,128)S(1)} %get-tuple-element.38), channel_id=1, source_target_pairs={{0,1},{1,0},{2,3},{3,2},{4,5},{5,4},{6,7},{7,6},{9,10},{10,9},{11,... | collective-permute-start | bytes 12296 | tf_op jit(solution)/shard_map/ppermute | solution.py:428
  7.4 0.1 constant_dynamic-slice_fusion.1.point_ref
  7.5 1.4 %shard_map.122 = (bf16[256,1024]{1,0:T(8,128)(2,1)S(1)}, bf16[288,1024]{1,0:T(8,128)(2,1)S(1)}) custom-call(s32[24,128]{1,0:T(8,128)S(1)} %get-tuple-element.31.facts_ref, bf16[256,1024]{1,0:T(8,128)(2,1)S(1)} %copy-done.3, bf16[64,1024]{1,0:T(8,128)(2,1)S(1)} %collective-permute-done.near_ref, bf16[64,1024]{1,0:T(8,128)(2,1)S(1)} %collective-permute-done.1.far_ref, ...), custom_call_target="tpu_custom_call" | custom-call | flops 2300000000 | bytes 2000000 | tf_op jit(solution)/shard_map/pallas_call | solution.py:23
  8.9 3.6 %collective-permute-start.5 = (bf16[256,1024]{1,0:T(8,128)(2,1)S(1)}, bf16[256,1024]{1,0:T(8,128)(2,1)S(1)}, u32[]{:S(2)}, u32[]{:S(2)}) collective-permute-start(bf16[256,1024]{1,0:T(8,128)(2,1)S(1)} %get-tuple-element.44.depth_ref.refs_2_), channel_id=1, source_target_pairs={{0,16},{8,24},{16,0},{24,8},{1,17},{9,25},{17,1},{25,9},{2,18},{10... | collective-permute-start | bytes 1572872 | tf_op jit(solution)/shard_map/ppermute | solution.py:419
  12.5 1.0 %shard_map.123 = (bf16[1024,640]{1,0:T(8,128)(2,1)S(1)}, f32[5,288,128]{2,1,0:T(8,128)S(1)}) custom-call(s32[24,128]{1,0:T(8,128)S(1)} %get-tuple-element.31.facts_ref, f32[16,1024]{1,0:T(8,128)S(1)} %copy-done.1, bf16[1024,640]{1,0:T(8,128)(2,1)S(1)} %copy-done.2, bf16[288,1024]{1,0:T(8,128)(2,1)S(1)} %get-tuple-element.34.core_ref), custom_call_target="tpu_custom_call" | custom-call | flops 1724999936 | bytes 1500000 | tf_op jit(solution)/shard_map/pallas_call | solution.py:23
  13.6 0.6 %collective-permute-start.3 = (s32[8,128]{1,0:T(8,128)S(1)}, s32[8,128]{1,0:T(8,128)S(1)}, u32[]{:S(2)}, u32[]{:S(2)}) collective-permute-start(s32[8,128]{1,0:T(8,128)S(1)} %collective-permute-done.2.mine_ref), channel_id=1, source_target_pairs={{0,8},{8,0},{16,24},{24,16},{1,9},{9,1},{17,25},{25,17},{2,10},{10... | collective-permute-start | bytes 12296 | tf_op jit(solution)/shard_map/ppermute | solution.py:419
  14.1 1.6 %shard_map.124.misfit_ref = f32[5,272,128]{2,1,0:T(8,128)S(1)} custom-call(s32[24,128]{1,0:T(8,128)S(1)} %get-tuple-element.31.facts_ref, f32[5,288,128]{2,1,0:T(8,128)S(1)} %get-tuple-element.40.response_ref, f32[16,640]{1,0:T(8,128)S(1)} %copy-done.5, bf16[256,640]{1,0:T(8,128)(2,1)S(1)} %copy-done.4, bf16[64,1024]{1,0:T(8,128)(2,1)S(1)} %collective-permute-done.near_ref, ...), custom_call_target="tpu_custom_call" | custom-call | flops 1724999936 | bytes 1500000 | tf_op jit(solution)/shard_map/pallas_call | solution.py:23
  15.8 2.0 %shard_map.125 = (bf16[256,640]{1,0:T(8,128)(2,1)S(1)}, bf16[528,256]{1,0:T(8,128)(2,1)S(1)}, f32[8,128]{1,0:T(8,128)S(1)}) custom-call(s32[24,128]{1,0:T(8,128)S(1)} %get-tuple-element.31.facts_ref, s32[8,128]{1,0:T(8,128)S(1)} %collective-permute-done.2.mine_ref, s32[8,128]{1,0:T(8,128)S(1)} %collective-permute-done.3.twin_ref, ...), custom_call_target="tpu_custom_call" | custom-call | flops 2875000064 | bytes 2500000 | tf_op jit(solution)/shard_map/pallas_call | solution.py:23
  17.8 1.6 %collective-permute-start.4 = (bf16[528,256]{1,0:T(8,128)(2,1)S(1)}, bf16[528,256]{1,0:T(8,128)(2,1)S(1)}, u32[]{:S(2)}, u32[]{:S(2)}) collective-permute-start(bf16[528,256]{1,0:T(8,128)(2,1)S(1)} %get-tuple-element.43), channel_id=1, source_target_pairs={{0,1},{1,0},{2,3},{3,2},{4,5},{5,4},{6,7},{7,6},{8,10},{9,11},{10,... | collective-permute-start | bytes 811016 | tf_op jit(solution)/shard_map/ppermute | solution.py:428
  19.4 0.4 shard_map.127.slope_ref
  19.7 1.1 %shard_map.126 = (f32[512,256]{1,0:T(8,128)S(1)}, bf16[512,640]{1,0:T(8,128)(2,1)S(1)}, f32[512,640]{1,0:T(8,128)S(1)}) custom-call(bf16[288,1024]{1,0:T(8,128)(2,1)S(1)} %get-tuple-element.34.core_ref, bf16[1024,640]{1,0:T(8,128)(2,1)S(1)} %get-tuple-element.36.effective_ref, bf16[256,640]{1,0:T(8,128)(2,1)S(1)} %get-tuple-element.41.half_ref), custom_call_target="tpu_custom_call" | custom-call | flops 1264999936 | bytes 1100000 | tf_op jit(solution)/shard_map/pallas_call | solution.py:23
  20.8 0.1 collective-permute-start.8
  20.9 3.4 %collective-permute-done.4 = bf16[528,256]{1,0:T(8,128)(2,1)S(1)} collective-permute-done((bf16[528,256]{1,0:T(8,128)(2,1)S(1)}, bf16[528,256]{1,0:T(8,128)(2,1)S(1)}, u32[]{:S(2)}, u32[]{:S(2)}) %collective-permute-start.4) | collective-permute-done | bytes 270368 | tf_op jit(solution)/shard_map/ppermute | solution.py:428
  24.3 0.4 collective-permute-done.5.refs_4_
  24.7 0.1 convert_add_fusion.1
  24.8 2.2 %collective-permute-start.7 = (bf16[272,256]{1,0:T(8,128)(2,1)S(1)}, bf16[272,256]{1,0:T(8,128)(2,1)S(1)}, u32[]{:S(2)}, u32[]{:S(2)}) collective-permute-start(bf16[272,256]{1,0:T(8,128)(2,1)S(1)} %pad_maximum_fusion), channel_id=1, source_target_pairs={{0,2},{1,3},{2,0},{3,1},{4,6},{5,7},{6,4},{7,5},{8,9},{9,8},{10,11... | collective-permute-start | bytes 417800 | tf_op jit(solution)/shard_map/ppermute | solution.py:428
  27.0 0.2 convert_add_fusion
  27.3 0.4 collective-permute-start.10
  27.7 2.3 %collective-permute-done.7 = bf16[272,256]{1,0:T(8,128)(2,1)S(1)} collective-permute-done((bf16[272,256]{1,0:T(8,128)(2,1)S(1)}, bf16[272,256]{1,0:T(8,128)(2,1)S(1)}, u32[]{:S(2)}, u32[]{:S(2)}) %collective-permute-start.7) | collective-permute-done | bytes 139296 | tf_op jit(solution)/shard_map/ppermute | solution.py:428
  30.1 3.1 %collective-permute-start.9 = (bf16[144,256]{1,0:T(8,128)(2,1)S(1)}, bf16[144,256]{1,0:T(8,128)(2,1)S(1)}, u32[]{:S(2)}, u32[]{:S(2)}) collective-permute-start(bf16[144,256]{1,0:T(8,128)(2,1)S(1)} %pad_maximum_fusion.1), channel_id=1, source_target_pairs={{0,4},{1,5},{2,6},{3,7},{4,0},{5,1},{6,2},{7,3},{8,12},{9,13},{10,... | collective-permute-start | bytes 221192 | tf_op jit(solution)/shard_map/ppermute | solution.py:428
  33.3 2.7 %collective-permute-done.9.arrived_ref = bf16[144,256]{1,0:T(8,128)(2,1)S(1)} collective-permute-done((bf16[144,256]{1,0:T(8,128)(2,1)S(1)}, bf16[144,256]{1,0:T(8,128)(2,1)S(1)}, u32[]{:S(2)}, u32[]{:S(2)}) %collective-permute-start.9) | collective-permute-done | bytes 73760 | tf_op jit(solution)/shard_map/ppermute | solution.py:428
  36.0 1.5 %collective-permute-done.10.arrived_ref = bf16[256,640]{1,0:T(8,128)(2,1)S(1)} collective-permute-done((bf16[256,640]{1,0:T(8,128)(2,1)S(1)}, bf16[256,640]{1,0:T(8,128)(2,1)S(1)}, u32[]{:S(2)}, u32[]{:S(2)}) %collective-permute-start.10) | collective-permute-done | bytes 327712 | tf_op jit(solution)/shard_map/ppermute | solution.py:419
  37.5 0.1 collective-permute-start.11
  37.6 0.4 collective-permute-start.12
  38.0 1.8 %shard_map.131 = f32[256,640]{1,0:T(8,128)} custom-call(s32[5]{0:T(128)S(1)} %copy-done.7, f32[256,640]{1,0:T(8,128)S(1)} %slice.67.keep_ref, bf16[256,640]{1,0:T(8,128)(2,1)S(1)} %collective-permute-done.10.arrived_ref, f32[16,256]{1,0:T(8,128)S(1)} %constant_dynamic-slice_fusion.gains_ref), custom_call_target="tpu_custom_call" | custom-call | flops 920000000 | bytes 800000 | tf_op jit(solution)/shard_map/pallas_call | solution.py:23
  39.8 2.4 %collective-permute-done.12.refs_2_ = bf16[144,256]{1,0:T(8,128)(2,1)S(1)} collective-permute-done((bf16[144,256]{1,0:T(8,128)(2,1)S(1)}, bf16[144,256]{1,0:T(8,128)(2,1)S(1)}, u32[]{:S(2)}, u32[]{:S(2)}) %collective-permute-start.12) | collective-permute-done | bytes 73760 | tf_op jit(solution)/shard_map/ppermute | solution.py:419
  42.3 0.3 shard_map.129.total_ref
  42.6 0.9 %collective-permute-done.13.refs_3_ = bf16[144,256]{1,0:T(8,128)(2,1)S(1)} collective-permute-done((bf16[144,256]{1,0:T(8,128)(2,1)S(1)}, bf16[144,256]{1,0:T(8,128)(2,1)S(1)}, u32[]{:S(2)}, u32[]{:S(2)}) %collective-permute-start.13) | collective-permute-done | bytes 73760 | tf_op jit(solution)/shard_map/ppermute | solution.py:419
  43.5 1.3 %shard_map.130 = (f32[1024,128]{1,0:T(8,128)}, f32[1,1]{1,0:T(1,128)}) custom-call(f32[128,1024]{1,0:T(8,128)S(1)} %shard_map.129.total_ref, bf16[144,256]{1,0:T(8,128)(2,1)S(1)} %shard_map.128.refs_0_, bf16[144,256]{1,0:T(8,128)(2,1)S(1)} %collective-permute-done.11.refs_1_, bf16[144,256]{1,0:T(8,128)(2,1)S(1)} %collective-permute-done.12.refs_2_, ...), custom_call_target="tpu_custom_call" | custom-call | flops 1150000000 | bytes 1000000 | tf_op jit(solution)/shard_map/pallas_call | solution.py:631
  (45 shorter events, 0.3 us)
Async XLA Ops:
  0.6 6.8 %copy-start.3 = (bf16[256,1024]{1,0:T(8,128)(2,1)S(1)}, bf16[256,1024]{1,0:T(8,128)(2,1)}, u32[]{:S(2)}) copy-start(bf16[256,1024]{1,0:T(8,128)(2,1)} %clip_ref.3) | copy-start | bytes 1572868
  0.6 6.7 %copy-start = (bf16[1024,1024]{1,0:T(8,128)(2,1)S(1)}, bf16[1024,1024]{1,0:T(8,128)(2,1)}, u32[]{:S(2)}) copy-start(bf16[1024,1024]{1,0:T(8,128)(2,1)} %point_ref.1) | copy-start | bytes 6291460
  0.7 6.8 %copy-start.6 = (f32[3,1024]{1,0:T(4,128)S(1)}, f32[3,1024]{1,0:T(4,128)}, u32[]{:S(2)}) copy-start(f32[3,1024]{1,0:T(4,128)} %taps_ref.1) | copy-start | bytes 36868
  1.7 5.7 %collective-permute-start = (bf16[64,1024]{1,0:T(8,128)(2,1)S(1)}, bf16[64,1024]{1,0:T(8,128)(2,1)S(1)}, u32[]{:S(2)}, u32[]{:S(2)}) collective-permute-start(bf16[64,1024]{1,0:T(8,128)(2,1)S(1)} %get-tuple-element.32), channel_id=1, source_target_pairs={{0,8},{8,0},{16,24},{24,16},{1,9},{9,1},{17,25},{25,17},{2,10},{10... | collective-permute-start | bytes 393224 | tf_op jit(solution)/shard_map/ppermute | solution.py:419
  2.2 5.2 %collective-permute-start.1 = (bf16[64,1024]{1,0:T(8,128)(2,1)S(1)}, bf16[64,1024]{1,0:T(8,128)(2,1)S(1)}, u32[]{:S(2)}, u32[]{:S(2)}) collective-permute-start(bf16[64,1024]{1,0:T(8,128)(2,1)S(1)} %get-tuple-element.32), channel_id=1, source_target_pairs={{8,16},{9,17},{10,18},{11,19},{12,20},{13,21},{14,22},{15,23},{16,... | collective-permute-start | bytes 393224 | tf_op jit(solution)/shard_map/ppermute | solution.py:428
  2.9 10.7 %collective-permute-start.2 = (s32[8,128]{1,0:T(8,128)S(1)}, s32[8,128]{1,0:T(8,128)S(1)}, u32[]{:S(2)}, u32[]{:S(2)}) collective-permute-start(s32[8,128]{1,0:T(8,128)S(1)} %get-tuple-element.38), channel_id=1, source_target_pairs={{0,1},{1,0},{2,3},{3,2},{4,5},{5,4},{6,7},{7,6},{9,10},{10,9},{11,... | collective-permute-start | bytes 12296 | tf_op jit(solution)/shard_map/ppermute | solution.py:428
  7.5 5.0 %copy-start.1 = (f32[16,1024]{1,0:T(8,128)S(1)}, f32[16,1024]{1,0:T(8,128)}, u32[]{:S(2)}) copy-start(f32[16,1024]{1,0:T(8,128)} %gains_ref) | copy-start | bytes 196612
  7.5 5.0 %copy-start.2 = (bf16[1024,640]{1,0:T(8,128)(2,1)S(1)}, bf16[1024,640]{1,0:T(8,128)(2,1)}, u32[]{:S(2)}) copy-start(bf16[1024,640]{1,0:T(8,128)(2,1)} %weight_ref.1) | copy-start | bytes 3932164
  8.9 15.8 %collective-permute-start.5 = (bf16[256,1024]{1,0:T(8,128)(2,1)S(1)}, bf16[256,1024]{1,0:T(8,128)(2,1)S(1)}, u32[]{:S(2)}, u32[]{:S(2)}) collective-permute-start(bf16[256,1024]{1,0:T(8,128)(2,1)S(1)} %get-tuple-element.44.depth_ref.refs_2_), channel_id=1, source_target_pairs={{0,16},{8,24},{16,0},{24,8},{1,17},{9,25},{17,1},{25,9},{2,18},{10... | collective-permute-start | bytes 1572872 | tf_op jit(solution)/shard_map/ppermute | solution.py:419
  12.5 12.2 %collective-permute-start.6 = (bf16[256,1024]{1,0:T(8,128)(2,1)S(1)}, bf16[256,1024]{1,0:T(8,128)(2,1)S(1)}, u32[]{:S(2)}, u32[]{:S(2)}) collective-permute-start(bf16[256,1024]{1,0:T(8,128)(2,1)S(1)} %get-tuple-element.44.depth_ref.refs_2_), channel_id=1, source_target_pairs={{0,8},{8,0},{16,24},{24,16},{1,9},{9,1},{17,25},{25,17},{2,10},{10... | collective-permute-start | bytes 1572872 | tf_op jit(solution)/shard_map/ppermute | solution.py:419
  12.5 1.7 %copy-start.4 = (bf16[256,640]{1,0:T(8,128)(2,1)S(1)}, bf16[256,640]{1,0:T(8,128)(2,1)}, u32[]{:S(2)}) copy-start(bf16[256,640]{1,0:T(8,128)(2,1)} %bold_ref.3) | copy-start | bytes 983044
  12.5 1.6 %copy-start.5 = (f32[16,640]{1,0:T(8,128)S(1)}, f32[16,640]{1,0:T(8,128)}, u32[]{:S(2)}) copy-start(f32[16,640]{1,0:T(8,128)} %hrf_ref.3) | copy-start | bytes 122884
  13.6 2.2 %collective-permute-start.3 = (s32[8,128]{1,0:T(8,128)S(1)}, s32[8,128]{1,0:T(8,128)S(1)}, u32[]{:S(2)}, u32[]{:S(2)}) collective-permute-start(s32[8,128]{1,0:T(8,128)S(1)} %collective-permute-done.2.mine_ref), channel_id=1, source_target_pairs={{0,8},{8,0},{16,24},{24,16},{1,9},{9,1},{17,25},{25,17},{2,10},{10... | collective-permute-start | bytes 12296 | tf_op jit(solution)/shard_map/ppermute | solution.py:419
  17.8 6.5 %collective-permute-start.4 = (bf16[528,256]{1,0:T(8,128)(2,1)S(1)}, bf16[528,256]{1,0:T(8,128)(2,1)S(1)}, u32[]{:S(2)}, u32[]{:S(2)}) collective-permute-start(bf16[528,256]{1,0:T(8,128)(2,1)S(1)} %get-tuple-element.43), channel_id=1, source_target_pairs={{0,1},{1,0},{2,3},{3,2},{4,5},{5,4},{6,7},{7,6},{8,10},{9,11},{10,... | collective-permute-start | bytes 811016 | tf_op jit(solution)/shard_map/ppermute | solution.py:428
  20.8 6.2 %collective-permute-start.8 = (bf16[512,640]{1,0:T(8,128)(2,1)S(1)}, bf16[512,640]{1,0:T(8,128)(2,1)S(1)}, u32[]{:S(2)}, u32[]{:S(2)}) collective-permute-start(bf16[512,640]{1,0:T(8,128)(2,1)S(1)} %get-tuple-element.48), channel_id=1, source_target_pairs={{0,8},{8,0},{16,24},{24,16},{1,9},{9,1},{17,25},{25,17},{2,10},{10... | collective-permute-start | bytes 1966088 | tf_op jit(solution)/shard_map/ppermute | solution.py:419
  24.8 5.2 %collective-permute-start.7 = (bf16[272,256]{1,0:T(8,128)(2,1)S(1)}, bf16[272,256]{1,0:T(8,128)(2,1)S(1)}, u32[]{:S(2)}, u32[]{:S(2)}) collective-permute-start(bf16[272,256]{1,0:T(8,128)(2,1)S(1)} %pad_maximum_fusion), channel_id=1, source_target_pairs={{0,2},{1,3},{2,0},{3,1},{4,6},{5,7},{6,4},{7,5},{8,9},{9,8},{10,11... | collective-permute-start | bytes 417800 | tf_op jit(solution)/shard_map/ppermute | solution.py:428
  27.0 15.6 %collective-permute-start.14 = (bf16[256,1024]{1,0:T(8,128)(2,1)S(1)}, bf16[256,1024]{1,0:T(8,128)(2,1)S(1)}, u32[]{:S(2)}, u32[]{:S(2)}) collective-permute-start(bf16[256,1024]{1,0:T(8,128)(2,1)S(1)} %collective-permute-done.5.refs_4_), channel_id=1, source_target_pairs={{0,8},{8,0},{16,24},{24,16},{1,9},{9,1},{17,25},{25,17},{2,10},{10... | collective-permute-start | bytes 1572872 | tf_op jit(solution)/shard_map/ppermute | solution.py:419
  27.3 10.8 %copy-start.7 = (s32[5]{0:T(128)S(1)}, s32[5]{0:T(128)}, u32[]{:S(2)}) copy-start(s32[5]{0:T(128)} %subject_ref.1) | copy-start | bytes 64
  27.3 10.2 %collective-permute-start.10 = (bf16[256,640]{1,0:T(8,128)(2,1)S(1)}, bf16[256,640]{1,0:T(8,128)(2,1)S(1)}, u32[]{:S(2)}, u32[]{:S(2)}) collective-permute-start(bf16[256,640]{1,0:T(8,128)(2,1)S(1)} %slice.89), channel_id=1, source_target_pairs={{0,16},{8,24},{16,0},{24,8},{1,17},{9,25},{17,1},{25,9},{2,18},{10... | collective-permute-start | bytes 983048 | tf_op jit(solution)/shard_map/ppermute | solution.py:419
  30.1 5.9 %collective-permute-start.9 = (bf16[144,256]{1,0:T(8,128)(2,1)S(1)}, bf16[144,256]{1,0:T(8,128)(2,1)S(1)}, u32[]{:S(2)}, u32[]{:S(2)}) collective-permute-start(bf16[144,256]{1,0:T(8,128)(2,1)S(1)} %pad_maximum_fusion.1), channel_id=1, source_target_pairs={{0,4},{1,5},{2,6},{3,7},{4,0},{5,1},{6,2},{7,3},{8,12},{9,13},{10,... | collective-permute-start | bytes 221192 | tf_op jit(solution)/shard_map/ppermute | solution.py:428
  37.5 4.8 %collective-permute-start.11 = (bf16[144,256]{1,0:T(8,128)(2,1)S(1)}, bf16[144,256]{1,0:T(8,128)(2,1)S(1)}, u32[]{:S(2)}, u32[]{:S(2)}) collective-permute-start(bf16[144,256]{1,0:T(8,128)(2,1)S(1)} %shard_map.128.refs_0_), channel_id=1, source_target_pairs={{0,8},{8,0},{16,24},{24,16},{1,9},{9,1},{17,25},{25,17},{2,10},{10... | collective-permute-start | bytes 221192 | tf_op jit(solution)/shard_map/ppermute | solution.py:419
  37.6 4.7 %collective-permute-start.12 = (bf16[144,256]{1,0:T(8,128)(2,1)S(1)}, bf16[144,256]{1,0:T(8,128)(2,1)S(1)}, u32[]{:S(2)}, u32[]{:S(2)}) collective-permute-start(bf16[144,256]{1,0:T(8,128)(2,1)S(1)} %shard_map.128.refs_0_), channel_id=1, source_target_pairs={{0,16},{8,24},{16,0},{24,8},{1,17},{9,25},{17,1},{25,9},{2,18},{10... | collective-permute-start | bytes 221192 | tf_op jit(solution)/shard_map/ppermute | solution.py:419
  42.3 1.3 %collective-permute-start.13 = (bf16[144,256]{1,0:T(8,128)(2,1)S(1)}, bf16[144,256]{1,0:T(8,128)(2,1)S(1)}, u32[]{:S(2)}, u32[]{:S(2)}) collective-permute-start(bf16[144,256]{1,0:T(8,128)(2,1)S(1)} %collective-permute-done.12.refs_2_), channel_id=1, source_target_pairs={{0,8},{8,0},{16,24},{24,16},{1,9},{9,1},{17,25},{25,17},{2,10},{10... | collective-permute-start | bytes 221192 | tf_op jit(solution)/shard_map/ppermute | solution.py:419

commit v4 on v3

--- a/solution.py
+++ b/solution.py
@@ -130,19 +130,8 @@
             response_ref[b + c] = part[:, c * BLOCK_VOX : (c + 1) * BLOCK_VOX]
 
 
-def core_kernel(
-    rows,
-    blocks,
-    facts_ref,
-    clip_ref,
-    near_ref,
-    far_ref,
-    taps_ref,
-    point_ref,
-    depth_ref,
-    core_ref,
-    ext,
-    deep,
+def conv_kernel(
+    rows, blocks, facts_ref, clip_ref, near_ref, far_ref, taps_ref, depth_ref, deep_ref, ext
 ):
     feats = clip_ref.shape[1]
     odd = lax.axis_index("tm") % 2
@@ -171,14 +160,29 @@
             shift = MARGIN - k * TAP_SPACING
             moved = values[shift : shift + 16] * jnp.tile(valid, (1, feats // 128))
             total = total + taps[k] * moved
-        deep[at : at + 16, :] = total.astype(BF16)
-    depth_ref[...] = deep[MARGIN : MARGIN + rows, :]
+        deep_ref[at : at + 16, :] = total.astype(BF16)
+    depth_ref[...] = deep_ref[MARGIN : MARGIN + rows, :]
+
+
+def core_kernel(rows, clip_ref, near_ref, far_ref, deep_ref, point_ref, core_ref, ext):
+    feats = clip_ref.shape[1]
+    odd = lax.axis_index("tm") % 2
+    ext[MARGIN : MARGIN + rows, :] = clip_ref[...]
+
+    @pl.when(odd == 0)
+    def _():
+        ext[:MARGIN, :] = far_ref[MARGIN : 2 * MARGIN, :]
+        ext[MARGIN + rows :, :] = near_ref[2 * MARGIN : 3 * MARGIN, :]
+
+    @pl.when(odd == 1)
+    def _():
+        ext[:MARGIN, :] = near_ref[MARGIN : 2 * MARGIN, :]
+        ext[MARGIN + rows :, :] = far_ref[2 * MARGIN : 3 * MARGIN, :]
+
     for col in range(0, feats, 256):
         lanes = slice(col, col + 256)
-        act = jnp.dot(deep[...], point_ref[:, lanes], preferred_element_type=F32)
-        core_ref[:, lanes] = (
-            ext[MARGIN : MARGIN + rows + 2 * MARGIN, lanes].astype(F32) + jax.nn.gelu(act)
-        ).astype(BF16)
+        act = jnp.dot(deep_ref[...], point_ref[:, lanes], preferred_element_type=F32)
+        core_ref[:, lanes] = (ext[:, lanes].astype(F32) + jax.nn.gelu(act)).astype(BF16)
 
 
 def block_at(position, bits):
@@ -361,11 +365,28 @@
         total_ref[:, lanes] = total
 
 
-def last_kernel(early, late, width, scale, total_ref, *refs):
-    first_refs = refs[:early]
-    grad_refs = refs[early : early + late]
-    depth_refs = refs[early + late : early + 2 * late]
-    point_ref, loss_ref = refs[early + 2 * late :]
+def later_kernel(parts, width, before_ref, *refs):
+    grad_refs, depth_refs, (total_ref,) = refs[:parts], refs[parts : 2 * parts], refs[2 * parts :]
+    for col in range(0, total_ref.shape[1], 256):
+        lanes = slice(col, col + 256)
+        total = before_ref[:, lanes]
+        for grad_ref, depth_ref in zip(grad_refs, depth_refs):
+            total = total + jnp.dot(
+                grad_ref[:width, :], depth_ref[:, lanes], preferred_element_type=F32
+            )
+        total_ref[:, lanes] = total
+
+
+def last_kernel(others, parts, width, scale, total_ref, *refs):
+    other_refs = refs[:others]
+    grad_refs = refs[others : others + parts]
+    depth_refs = refs[others + parts : others + 2 * parts]
+    point_ref, loss_ref = refs[others + 2 * parts :]
+    lost = None
+    for ref in other_refs + grad_refs:
+        part = ref[width:, :BLOCK_VOX].astype(F32)
+        lost = part if lost is None else lost + part
+    loss_ref[0, 0] = jnp.sum(lost) * scale
     for col in range(0, total_ref.shape[1], 256):
         lanes = slice(col, col + 256)
         total = total_ref[:, lanes]
@@ -374,11 +395,6 @@
                 grad_ref[:width, :], depth_ref[:, lanes], preferred_element_type=F32
             )
         point_ref[lanes, :] = jnp.transpose(total)
-    lost = None
-    for ref in first_refs + grad_refs:
-        part = ref[width:, :BLOCK_VOX].astype(F32)
-        lost = part if lost is None else lost + part
-    loss_ref[0, 0] = jnp.sum(lost) * scale
 
 
 def readout_kernel(blocks, subject_ref, keep_ref, arrived_ref, gains_ref, out_ref):
@@ -467,25 +483,23 @@
     mine = across(ends, next_vox)
     near = swap_tm(payload, 0)
 
-    depth_half, core_out = call(
-        functools.partial(core_kernel, rows, blocks),
+    halos = [(VMEM, clip_features), (VMEM, near), (VMEM, far)]
+    depth_half, deep = call(
+        functools.partial(conv_kernel, rows, blocks),
         (
             jax.ShapeDtypeStruct((rows, feats), BF16),
             jax.ShapeDtypeStruct((rows + 2 * MARGIN, feats), BF16),
         ),
-        [
-            (VMEM, facts),
-            (VMEM, clip_features),
-            (VMEM, near),
-            (VMEM, far),
-            (VMEM, depth_kernel),
-            (VMEM, point_weight),
-        ],
-        2.0,
-        [
-            pltpu.VMEM((rows + 3 * MARGIN, feats), BF16),
-            pltpu.VMEM((rows + 2 * MARGIN, feats), BF16),
-        ],
+        [(VMEM, facts)] + halos + [(VMEM, depth_kernel)],
+        0.6,
+        [pltpu.VMEM((rows + 3 * MARGIN, feats), BF16)],
+    )
+    core_out = call(
+        functools.partial(core_kernel, rows),
+        jax.ShapeDtypeStruct((rows + 2 * MARGIN, feats), BF16),
+        halos + [(VMEM, deep), (VMEM, point_weight)],
+        1.0,
+        [pltpu.VMEM((rows + 2 * MARGIN, feats), BF16)],
     )
     core_out, late_gains = lax.optimization_barrier((core_out, subject_feature_gains))
     effective, response = call(
@@ -611,43 +625,54 @@
         [(VMEM, keep), (VMEM, arrived), (VMEM, lost), (VMEM, slope)],
         0.3,
     )
+    groups = [[(), (0,)], [path for path in paths[1:] if path[-1] != 0]]
+    groups.append([path for path in paths if path not in groups[0] + groups[1]])
+
+    def operands(group):
+        return [(VMEM, grads[path]) for path in group] + [(VMEM, depths[path]) for path in group]
+
     grads = {(): pre_grad}
-    for path in paths[1:]:
+    for path in groups[0][1:] + groups[1]:
         grads[path] = swap_tm(grads[path[:-1]], path[-1])
-    early = [(), (0,)]
-    late = [path for path in paths if path not in early]
+    total_shape = jax.ShapeDtypeStruct((width, feats), F32)
     total = call(
-        functools.partial(early_kernel, len(early), width),
-        jax.ShapeDtypeStruct((width, feats), F32),
-        [(VMEM, grads[path]) for path in early] + [(VMEM, depths[path]) for path in early],
-        0.8,
-    )
+        functools.partial(early_kernel, len(groups[0]), width), total_shape, operands(groups[0]), 0.3
+    )
+    top = groups[1][-1]
     grad_readout = call(
         functools.partial(readout_kernel, blocks),
         jax.ShapeDtypeStruct((share, slots), F32),
         [(SMEM, block_subject), (VMEM, raw_keep), (VMEM, raw_came), (VMEM, own_gains)],
         0.8,
     )
+    grads[top], total, grad_readout = lax.optimization_barrier(
+        (grads[top], total, grad_readout)
+    )
+    for path in groups[2]:
+        grads[path] = swap_tm(grads[path[:-1]], path[-1])
+    total = call(
+        functools.partial(later_kernel, len(groups[1]), width),
+        total_shape,
+        [(VMEM, total)] + operands(groups[1]),
+        0.3,
+    )
+    others = groups[0] + groups[1]
+    ins = [(VMEM, total)] + [(VMEM, grads[path]) for path in others] + operands(groups[2])
     grad_point, loss_total = pl.pallas_call(
         functools.partial(
-            last_kernel, len(early), len(late), width, 1.0 / (subjects * rows * tm_count)
+            last_kernel, len(others), len(groups[2]), width, 1.0 / (subjects * rows * tm_count)
         ),
         out_shape=(
             jax.ShapeDtypeStruct((feats, width), F32),
             jax.ShapeDtypeStruct((1, 1), F32),
         ),
-        in_specs=[VMEM] * (1 + len(early) + 2 * len(late)),
+        in_specs=[spec for spec, _ in ins],
         out_specs=(VMEM, SMEM),
         compiler_params=pltpu.CompilerParams(vmem_limit_bytes=16 << 20),
         cost_estimate=pl.CostEstimate(
             flops=int(1.15e9), bytes_accessed=1000000, transcendentals=0
         ),
-    )(
-        total,
-        *[grads[path] for path in early],
-        *[grads[path] for path in late],
-        *[depths[path] for path in late],
-    )
+    )(*[value for _, value in ins])
     return (loss_total.reshape(()), grad_readout, grad_point)
 
 

time: 45 us -> 44.5 us (0.989)
  starting transfers between devices: 17.7 us -> 16.5 us
  Pallas kernels: 11.9 us -> 12.4 us
    ppermute x5, starting transfers between devices: 12 us -> 11 us  [across(): return lax.ppermute(value, ('tm', 'vox'), pairs)]
    pallas_call x9 -> x11, Pallas kernels: 9.63 us -> 10.2 us  [call(): pl.pallas_call(body, out_shape=outs, in_specs=[spec for spec, _ in ins],...]
    ppermute x5, waiting for transfers between devices: 8.43 us -> 8.89 us  [across(): return lax.ppermute(value, ('tm', 'vox'), pairs)]
  transfers between devices with their start and end apart: 15 -> 15, of which waited for: 7 -> 6; matrix products, arithmetic and copies ran while one was open for 1% -> 1% of each run, Pallas kernels for 21% -> 23%
where the time goes in v4:
time: 44.5 us; the launch traced here: 44.3 us
  starting transfers between devices  16.5 us (37%)
  waiting for transfers between devices  13.7 us (31%)
  Pallas kernels  12.4 us (28%)
  between operations  0.96 us (2%)
    ppermute x5, starting transfers between devices, across(): return lax.ppermute(value, ('tm', 'vox'), pairs)  11 us
    pallas_call x11, Pallas kernels, call(): pl.pallas_call(body, out_shape=outs, in_specs=[spec for spec, _ in ins],...  10.2 us
    ppermute x5, waiting for transfers between devices, across(): return lax.ppermute(value, ('tm', 'vox'), pairs)  8.89 us
    ppermute x10, starting transfers between devices, swap_tm(): lax.ppermute(value, 'tm', [(i, i ^ 1 << bit) for i in range(tm_count)])  5.52 us
    ppermute x10, waiting for transfers between devices, swap_tm(): lax.ppermute(value, 'tm', [(i, i ^ 1 << bit) for i in range(tm_count)])  4.8 us
    pallas_call x1, Pallas kernels, shards(): pl.pallas_call(functools.partial(last_kernel, len(others), len(groups[2])...  1.17 us
    pallas_call x1, Pallas kernels, shards(): pl.pallas_call(functools.partial(pack_kernel, rows, blocks), out_shape=(p...  1.05 us
  transfers between devices with their start and end apart: 15, of which 6 were waited for; matrix products, arithmetic and copies ran while one was open for 1% of the time, Pallas kernels for 23%

profile of v4, /device:TPU:0, one launch (start us, length us, event | category | flops | bytes accessed | tf_op | source)
XLA Modules:
  0.0 44.3 jit_solution(18367751736269256017)
XLA Ops:
  0.7 1.0 %shard_map.121 = (bf16[64,1024]{1,0:T(8,128)(2,1)S(1)}, s32[8,128]{1,0:T(8,128)S(1)}, s32[24,128]{1,0:T(8,128)S(1)}) custom-call(s32[5]{0:T(128)} %subject_ref.1, s32[5]{0:T(128)} %live_hbm.1, s32[8]{0:T(128)} %lengths_hbm.1, bf16[256,1024]{1,0:T(8,128)(2,1)} %clip_ref.5, bf16[256,640]{1,0:T(8,128)(2,1)} %bold_ref.3), custom_call_target="tpu_custom_call" | custom-call | flops 6899999744 | bytes 1000000 | tf_op jit(solution)/shard_map/pallas_call | solution.py:458
  1.7 0.5 %collective-permute-start = (bf16[64,1024]{1,0:T(8,128)(2,1)S(1)}, bf16[64,1024]{1,0:T(8,128)(2,1)S(1)}, u32[]{:S(2)}, u32[]{:S(2)}) collective-permute-start(bf16[64,1024]{1,0:T(8,128)(2,1)S(1)} %get-tuple-element.34), channel_id=1, source_target_pairs={{0,8},{8,0},{16,24},{24,16},{1,9},{9,1},{17,25},{25,17},{2,10},{10... | collective-permute-start | bytes 393224 | tf_op jit(solution)/shard_map/ppermute | solution.py:435
  2.2 0.7 %collective-permute-start.1 = (bf16[64,1024]{1,0:T(8,128)(2,1)S(1)}, bf16[64,1024]{1,0:T(8,128)(2,1)S(1)}, u32[]{:S(2)}, u32[]{:S(2)}) collective-permute-start(bf16[64,1024]{1,0:T(8,128)(2,1)S(1)} %get-tuple-element.34), channel_id=1, source_target_pairs={{8,16},{9,17},{10,18},{11,19},{12,20},{13,21},{14,22},{15,23},{16,... | collective-permute-start | bytes 393224 | tf_op jit(solution)/shard_map/ppermute | solution.py:444
  2.9 4.4 %collective-permute-start.2 = (s32[8,128]{1,0:T(8,128)S(1)}, s32[8,128]{1,0:T(8,128)S(1)}, u32[]{:S(2)}, u32[]{:S(2)}) collective-permute-start(s32[8,128]{1,0:T(8,128)S(1)} %get-tuple-element.41), channel_id=1, source_target_pairs={{0,1},{1,0},{2,3},{3,2},{4,5},{5,4},{6,7},{7,6},{9,10},{10,9},{11,... | collective-permute-start | bytes 12296 | tf_op jit(solution)/shard_map/ppermute | solution.py:444
  7.4 0.1 constant_dynamic-slice_fusion.1.point_ref
  7.5 0.6 %shard_map.122 = (bf16[256,1024]{1,0:T(8,128)(2,1)S(1)}, bf16[288,1024]{1,0:T(8,128)(2,1)S(1)}) custom-call(s32[24,128]{1,0:T(8,128)S(1)} %get-tuple-element.35.facts_ref, bf16[256,1024]{1,0:T(8,128)(2,1)S(1)} %copy-done.3, bf16[64,1024]{1,0:T(8,128)(2,1)S(1)} %collective-permute-done.near_ref, bf16[64,1024]{1,0:T(8,128)(2,1)S(1)} %collective-permute-done.1.far_ref, ...), custom_call_target="tpu_custom_call" | custom-call | flops 690000000 | bytes 600000 | tf_op jit(solution)/shard_map/pallas_call | solution.py:23
  8.1 3.6 %collective-permute-start.5 = (bf16[256,1024]{1,0:T(8,128)(2,1)S(1)}, bf16[256,1024]{1,0:T(8,128)(2,1)S(1)}, u32[]{:S(2)}, u32[]{:S(2)}) collective-permute-start(bf16[256,1024]{1,0:T(8,128)(2,1)S(1)} %get-tuple-element.47.depth_ref.refs_2_), channel_id=1, source_target_pairs={{0,16},{8,24},{16,0},{24,8},{1,17},{9,25},{17,1},{25,9},{2,18},{10... | collective-permute-start | bytes 1572872 | tf_op jit(solution)/shard_map/ppermute | solution.py:435
  11.7 1.1 %shard_map.123.core_ref = bf16[288,1024]{1,0:T(8,128)(2,1)S(1)} custom-call(bf16[256,1024]{1,0:T(8,128)(2,1)S(1)} %copy-done.3, bf16[64,1024]{1,0:T(8,128)(2,1)S(1)} %collective-permute-done.near_ref, bf16[64,1024]{1,0:T(8,128)(2,1)S(1)} %collective-permute-done.1.far_ref, bf16[288,1024]{1,0:T(8,128)(2,1)S(1)} %get-tuple-element.36.deep_ref, ...), custom_call_target="tpu_custom_call" | custom-call | flops 1150000000 | bytes 1000000 | tf_op jit(solution)/shard_map/pallas_call | solution.py:23
  12.8 0.2 copy-done.2
  13.0 1.0 %shard_map.124 = (bf16[1024,640]{1,0:T(8,128)(2,1)S(1)}, f32[5,288,128]{2,1,0:T(8,128)S(1)}) custom-call(s32[24,128]{1,0:T(8,128)S(1)} %get-tuple-element.35.facts_ref, f32[16,1024]{1,0:T(8,128)S(1)} %copy-done.1, bf16[1024,640]{1,0:T(8,128)(2,1)S(1)} %copy-done.2, bf16[288,1024]{1,0:T(8,128)(2,1)S(1)} %shard_map.123.core_ref), custom_call_target="tpu_custom_call" | custom-call | flops 1724999936 | bytes 1500000 | tf_op jit(solution)/shard_map/pallas_call | solution.py:23
  14.1 0.6 %collective-permute-start.3 = (s32[8,128]{1,0:T(8,128)S(1)}, s32[8,128]{1,0:T(8,128)S(1)}, u32[]{:S(2)}, u32[]{:S(2)}) collective-permute-start(s32[8,128]{1,0:T(8,128)S(1)} %collective-permute-done.2.mine_ref), channel_id=1, source_target_pairs={{0,8},{8,0},{16,24},{24,16},{1,9},{9,1},{17,25},{25,17},{2,10},{10... | collective-permute-start | bytes 12296 | tf_op jit(solution)/shard_map/ppermute | solution.py:435
  14.7 1.6 %shard_map.125.misfit_ref = f32[5,272,128]{2,1,0:T(8,128)S(1)} custom-call(s32[24,128]{1,0:T(8,128)S(1)} %get-tuple-element.35.facts_ref, f32[5,288,128]{2,1,0:T(8,128)S(1)} %get-tuple-element.43.response_ref, f32[16,640]{1,0:T(8,128)S(1)} %copy-done.5, bf16[256,640]{1,0:T(8,128)(2,1)S(1)} %copy-done.4, bf16[64,1024]{1,0:T(8,128)(2,1)S(1)} %collective-permute-done.near_ref, ...), custom_call_target="tpu_custom_call" | custom-call | flops 1724999936 | bytes 1500000 | tf_op jit(solution)/shard_map/pallas_call | solution.py:23
  16.3 1.9 %shard_map.126 = (bf16[256,640]{1,0:T(8,128)(2,1)S(1)}, bf16[528,256]{1,0:T(8,128)(2,1)S(1)}, f32[8,128]{1,0:T(8,128)S(1)}) custom-call(s32[24,128]{1,0:T(8,128)S(1)} %get-tuple-element.35.facts_ref, s32[8,128]{1,0:T(8,128)S(1)} %collective-permute-done.2.mine_ref, s32[8,128]{1,0:T(8,128)S(1)} %collective-permute-done.3.twin_ref, ...), custom_call_target="tpu_custom_call" | custom-call | flops 2875000064 | bytes 2500000 | tf_op jit(solution)/shard_map/pallas_call | solution.py:23
  18.3 1.6 %collective-permute-start.4 = (bf16[528,256]{1,0:T(8,128)(2,1)S(1)}, bf16[528,256]{1,0:T(8,128)(2,1)S(1)}, u32[]{:S(2)}, u32[]{:S(2)}) collective-permute-start(bf16[528,256]{1,0:T(8,128)(2,1)S(1)} %get-tuple-element.46), channel_id=1, source_target_pairs={{0,1},{1,0},{2,3},{3,2},{4,5},{5,4},{6,7},{7,6},{8,10},{9,11},{10,... | collective-permute-start | bytes 811016 | tf_op jit(solution)/shard_map/ppermute | solution.py:444
  19.8 0.4 shard_map.128.slope_ref
  20.2 1.1 %shard_map.127 = (f32[512,256]{1,0:T(8,128)S(1)}, bf16[512,640]{1,0:T(8,128)(2,1)S(1)}, f32[512,640]{1,0:T(8,128)S(1)}) custom-call(bf16[288,1024]{1,0:T(8,128)(2,1)S(1)} %shard_map.123.core_ref, bf16[1024,640]{1,0:T(8,128)(2,1)S(1)} %get-tuple-element.39.effective_ref, bf16[256,640]{1,0:T(8,128)(2,1)S(1)} %get-tuple-element.44.half_ref), custom_call_target="tpu_custom_call" | custom-call | flops 1264999936 | bytes 1100000 | tf_op jit(solution)/shard_map/pallas_call | solution.py:23
  21.3 0.1 collective-permute-start.8
  21.4 3.4 %collective-permute-done.4 = bf16[528,256]{1,0:T(8,128)(2,1)S(1)} collective-permute-done((bf16[528,256]{1,0:T(8,128)(2,1)S(1)}, bf16[528,256]{1,0:T(8,128)(2,1)S(1)}, u32[]{:S(2)}, u32[]{:S(2)}) %collective-permute-start.4) | collective-permute-done | bytes 270368 | tf_op jit(solution)/shard_map/ppermute | solution.py:444
  24.9 1.6 %collective-permute-start.7 = (bf16[272,256]{1,0:T(8,128)(2,1)S(1)}, bf16[272,256]{1,0:T(8,128)(2,1)S(1)}, u32[]{:S(2)}, u32[]{:S(2)}) collective-permute-start(bf16[272,256]{1,0:T(8,128)(2,1)S(1)} %pad_maximum_fusion), channel_id=1, source_target_pairs={{0,2},{1,3},{2,0},{3,1},{4,6},{5,7},{6,4},{7,5},{8,9},{9,8},{10,11... | collective-permute-start | bytes 417800 | tf_op jit(solution)/shard_map/ppermute | solution.py:444
  26.6 0.2 convert_add_fusion
  26.9 0.3 collective-permute-start.10
  27.2 2.9 %collective-permute-done.7 = bf16[272,256]{1,0:T(8,128)(2,1)S(1)} collective-permute-done((bf16[272,256]{1,0:T(8,128)(2,1)S(1)}, bf16[272,256]{1,0:T(8,128)(2,1)S(1)}, u32[]{:S(2)}, u32[]{:S(2)}) %collective-permute-start.7) | collective-permute-done | bytes 139296 | tf_op jit(solution)/shard_map/ppermute | solution.py:444
  30.2 2.7 %collective-permute-start.9 = (bf16[144,256]{1,0:T(8,128)(2,1)S(1)}, bf16[144,256]{1,0:T(8,128)(2,1)S(1)}, u32[]{:S(2)}, u32[]{:S(2)}) collective-permute-start(bf16[144,256]{1,0:T(8,128)(2,1)S(1)} %pad_maximum_fusion.1), channel_id=1, source_target_pairs={{0,4},{1,5},{2,6},{3,7},{4,0},{5,1},{6,2},{7,3},{8,12},{9,13},{10,... | collective-permute-start | bytes 221192 | tf_op jit(solution)/shard_map/ppermute | solution.py:444
  32.8 2.6 %collective-permute-done.9.arrived_ref = bf16[144,256]{1,0:T(8,128)(2,1)S(1)} collective-permute-done((bf16[144,256]{1,0:T(8,128)(2,1)S(1)}, bf16[144,256]{1,0:T(8,128)(2,1)S(1)}, u32[]{:S(2)}, u32[]{:S(2)}) %collective-permute-start.9) | collective-permute-done | bytes 73760 | tf_op jit(solution)/shard_map/ppermute | solution.py:444
  35.5 1.6 %collective-permute-done.10.arrived_ref = bf16[256,640]{1,0:T(8,128)(2,1)S(1)} collective-permute-done((bf16[256,640]{1,0:T(8,128)(2,1)S(1)}, bf16[256,640]{1,0:T(8,128)(2,1)S(1)}, u32[]{:S(2)}, u32[]{:S(2)}) %collective-permute-start.10) | collective-permute-done | bytes 327712 | tf_op jit(solution)/shard_map/ppermute | solution.py:435
  37.2 0.4 collective-permute-start.11
  37.5 1.8 %shard_map.131 = f32[256,640]{1,0:T(8,128)} custom-call(s32[5]{0:T(128)S(1)} %copy-done.7, f32[256,640]{1,0:T(8,128)S(1)} %slice.67.keep_ref, bf16[256,640]{1,0:T(8,128)(2,1)S(1)} %collective-permute-done.10.arrived_ref, f32[16,256]{1,0:T(8,128)S(1)} %constant_dynamic-slice_fusion.gains_ref), custom_call_target="tpu_custom_call" | custom-call | flops 920000000 | bytes 800000 | tf_op jit(solution)/shard_map/pallas_call | solution.py:23
  39.3 0.3 shard_map.130.before_ref
  39.6 2.2 %collective-permute-done.11.refs_0_.refs_2_ = bf16[144,256]{1,0:T(8,128)(2,1)S(1)} collective-permute-done((bf16[144,256]{1,0:T(8,128)(2,1)S(1)}, bf16[144,256]{1,0:T(8,128)(2,1)S(1)}, u32[]{:S(2)}, u32[]{:S(2)}) %collective-permute-start.11) | collective-permute-done | bytes 73760 | tf_op jit(solution)/shard_map/ppermute | solution.py:435
  41.8 0.2 shard_map.132.total_ref
  42.1 1.0 %collective-permute-done.13.refs_3_ = bf16[144,256]{1,0:T(8,128)(2,1)S(1)} collective-permute-done((bf16[144,256]{1,0:T(8,128)(2,1)S(1)}, bf16[144,256]{1,0:T(8,128)(2,1)S(1)}, u32[]{:S(2)}, u32[]{:S(2)}) %collective-permute-start.13) | collective-permute-done | bytes 73760 | tf_op jit(solution)/shard_map/ppermute | solution.py:435
  43.1 1.2 %shard_map.133 = (f32[1024,128]{1,0:T(8,128)}, f32[1,1]{1,0:T(1,128)}) custom-call(f32[128,1024]{1,0:T(8,128)S(1)} %shard_map.132.total_ref, bf16[144,256]{1,0:T(8,128)(2,1)S(1)} %shard_map.129.refs_0_, bf16[144,256]{1,0:T(8,128)(2,1)S(1)} %collective-permute-done.12.refs_1_, bf16[144,256]{1,0:T(8,128)(2,1)S(1)} %collective-permute-done.11.refs_0_.refs_2_, ...), custom_call_target="tpu_custom_call" | custom-call | flops 1150000000 | bytes 1000000 | tf_op jit(solution)/shard_map/pallas_call | solution.py:661
  (47 shorter events, 0.4 us)
Async XLA Ops:
  0.6 6.8 %copy-start.3 = (bf16[256,1024]{1,0:T(8,128)(2,1)S(1)}, bf16[256,1024]{1,0:T(8,128)(2,1)}, u32[]{:S(2)}) copy-start(bf16[256,1024]{1,0:T(8,128)(2,1)} %clip_ref.5) | copy-start | bytes 1572868
  0.6 6.7 %copy-start = (bf16[1024,1024]{1,0:T(8,128)(2,1)S(1)}, bf16[1024,1024]{1,0:T(8,128)(2,1)}, u32[]{:S(2)}) copy-start(bf16[1024,1024]{1,0:T(8,128)(2,1)} %point_ref.1) | copy-start | bytes 6291460
  0.7 6.8 %copy-start.6 = (f32[3,1024]{1,0:T(4,128)S(1)}, f32[3,1024]{1,0:T(4,128)}, u32[]{:S(2)}) copy-start(f32[3,1024]{1,0:T(4,128)} %taps_ref.1) | copy-start | bytes 36868
  1.7 5.7 %collective-permute-start = (bf16[64,1024]{1,0:T(8,128)(2,1)S(1)}, bf16[64,1024]{1,0:T(8,128)(2,1)S(1)}, u32[]{:S(2)}, u32[]{:S(2)}) collective-permute-start(bf16[64,1024]{1,0:T(8,128)(2,1)S(1)} %get-tuple-element.34), channel_id=1, source_target_pairs={{0,8},{8,0},{16,24},{24,16},{1,9},{9,1},{17,25},{25,17},{2,10},{10... | collective-permute-start | bytes 393224 | tf_op jit(solution)/shard_map/ppermute | solution.py:435
  2.2 5.2 %collective-permute-start.1 = (bf16[64,1024]{1,0:T(8,128)(2,1)S(1)}, bf16[64,1024]{1,0:T(8,128)(2,1)S(1)}, u32[]{:S(2)}, u32[]{:S(2)}) collective-permute-start(bf16[64,1024]{1,0:T(8,128)(2,1)S(1)} %get-tuple-element.34), channel_id=1, source_target_pairs={{8,16},{9,17},{10,18},{11,19},{12,20},{13,21},{14,22},{15,23},{16,... | collective-permute-start | bytes 393224 | tf_op jit(solution)/shard_map/ppermute | solution.py:444
  2.9 11.2 %collective-permute-start.2 = (s32[8,128]{1,0:T(8,128)S(1)}, s32[8,128]{1,0:T(8,128)S(1)}, u32[]{:S(2)}, u32[]{:S(2)}) collective-permute-start(s32[8,128]{1,0:T(8,128)S(1)} %get-tuple-element.41), channel_id=1, source_target_pairs={{0,1},{1,0},{2,3},{3,2},{4,5},{5,4},{6,7},{7,6},{9,10},{10,9},{11,... | collective-permute-start | bytes 12296 | tf_op jit(solution)/shard_map/ppermute | solution.py:444
  8.1 16.7 %collective-permute-start.5 = (bf16[256,1024]{1,0:T(8,128)(2,1)S(1)}, bf16[256,1024]{1,0:T(8,128)(2,1)S(1)}, u32[]{:S(2)}, u32[]{:S(2)}) collective-permute-start(bf16[256,1024]{1,0:T(8,128)(2,1)S(1)} %get-tuple-element.47.depth_ref.refs_2_), channel_id=1, source_target_pairs={{0,16},{8,24},{16,0},{24,8},{1,17},{9,25},{17,1},{25,9},{2,18},{10... | collective-permute-start | bytes 1572872 | tf_op jit(solution)/shard_map/ppermute | solution.py:435
  11.7 13.1 %collective-permute-start.6 = (bf16[256,1024]{1,0:T(8,128)(2,1)S(1)}, bf16[256,1024]{1,0:T(8,128)(2,1)S(1)}, u32[]{:S(2)}, u32[]{:S(2)}) collective-permute-start(bf16[256,1024]{1,0:T(8,128)(2,1)S(1)} %get-tuple-element.47.depth_ref.refs_2_), channel_id=1, source_target_pairs={{0,8},{8,0},{16,24},{24,16},{1,9},{9,1},{17,25},{25,17},{2,10},{10... | collective-permute-start | bytes 1572872 | tf_op jit(solution)/shard_map/ppermute | solution.py:435
  11.7 1.2 %copy-start.1 = (f32[16,1024]{1,0:T(8,128)S(1)}, f32[16,1024]{1,0:T(8,128)}, u32[]{:S(2)}) copy-start(f32[16,1024]{1,0:T(8,128)} %gains_ref) | copy-start | bytes 196612
  11.7 1.4 %copy-start.2 = (bf16[1024,640]{1,0:T(8,128)(2,1)S(1)}, bf16[1024,640]{1,0:T(8,128)(2,1)}, u32[]{:S(2)}) copy-start(bf16[1024,640]{1,0:T(8,128)(2,1)} %weight_ref.1) | copy-start | bytes 3932164
  13.0 1.6 %copy-start.4 = (bf16[256,640]{1,0:T(8,128)(2,1)S(1)}, bf16[256,640]{1,0:T(8,128)(2,1)}, u32[]{:S(2)}) copy-start(bf16[256,640]{1,0:T(8,128)(2,1)} %bold_ref.3) | copy-start | bytes 983044
  13.0 1.6 %copy-start.5 = (f32[16,640]{1,0:T(8,128)S(1)}, f32[16,640]{1,0:T(8,128)}, u32[]{:S(2)}) copy-start(f32[16,640]{1,0:T(8,128)} %hrf_ref.3) | copy-start | bytes 122884
  14.1 2.2 %collective-permute-start.3 = (s32[8,128]{1,0:T(8,128)S(1)}, s32[8,128]{1,0:T(8,128)S(1)}, u32[]{:S(2)}, u32[]{:S(2)}) collective-permute-start(s32[8,128]{1,0:T(8,128)S(1)} %collective-permute-done.2.mine_ref), channel_id=1, source_target_pairs={{0,8},{8,0},{16,24},{24,16},{1,9},{9,1},{17,25},{25,17},{2,10},{10... | collective-permute-start | bytes 12296 | tf_op jit(solution)/shard_map/ppermute | solution.py:435
  18.3 6.5 %collective-permute-start.4 = (bf16[528,256]{1,0:T(8,128)(2,1)S(1)}, bf16[528,256]{1,0:T(8,128)(2,1)S(1)}, u32[]{:S(2)}, u32[]{:S(2)}) collective-permute-start(bf16[528,256]{1,0:T(8,128)(2,1)S(1)} %get-tuple-element.46), channel_id=1, source_target_pairs={{0,1},{1,0},{2,3},{3,2},{4,5},{5,4},{6,7},{7,6},{8,10},{9,11},{10,... | collective-permute-start | bytes 811016 | tf_op jit(solution)/shard_map/ppermute | solution.py:444
  21.3 5.3 %collective-permute-start.8 = (bf16[512,640]{1,0:T(8,128)(2,1)S(1)}, bf16[512,640]{1,0:T(8,128)(2,1)S(1)}, u32[]{:S(2)}, u32[]{:S(2)}) collective-permute-start(bf16[512,640]{1,0:T(8,128)(2,1)S(1)} %get-tuple-element.51), channel_id=1, source_target_pairs={{0,8},{8,0},{16,24},{24,16},{1,9},{9,1},{17,25},{25,17},{2,10},{10... | collective-permute-start | bytes 1966088 | tf_op jit(solution)/shard_map/ppermute | solution.py:435
  24.9 5.1 %collective-permute-start.7 = (bf16[272,256]{1,0:T(8,128)(2,1)S(1)}, bf16[272,256]{1,0:T(8,128)(2,1)S(1)}, u32[]{:S(2)}, u32[]{:S(2)}) collective-permute-start(bf16[272,256]{1,0:T(8,128)(2,1)S(1)} %pad_maximum_fusion), channel_id=1, source_target_pairs={{0,2},{1,3},{2,0},{3,1},{4,6},{5,7},{6,4},{7,5},{8,9},{9,8},{10,11... | collective-permute-start | bytes 417800 | tf_op jit(solution)/shard_map/ppermute | solution.py:444
  26.6 15.5 %collective-permute-start.14 = (bf16[256,1024]{1,0:T(8,128)(2,1)S(1)}, bf16[256,1024]{1,0:T(8,128)(2,1)S(1)}, u32[]{:S(2)}, u32[]{:S(2)}) collective-permute-start(bf16[256,1024]{1,0:T(8,128)(2,1)S(1)} %collective-permute-done.5.refs_1_), channel_id=1, source_target_pairs={{0,8},{8,0},{16,24},{24,16},{1,9},{9,1},{17,25},{25,17},{2,10},{10... | collective-permute-start | bytes 1572872 | tf_op jit(solution)/shard_map/ppermute | solution.py:435
  26.8 10.7 %copy-start.7 = (s32[5]{0:T(128)S(1)}, s32[5]{0:T(128)}, u32[]{:S(2)}) copy-start(s32[5]{0:T(128)} %subject_ref.1) | copy-start | bytes 64
  26.9 10.2 %collective-permute-start.10 = (bf16[256,640]{1,0:T(8,128)(2,1)S(1)}, bf16[256,640]{1,0:T(8,128)(2,1)S(1)}, u32[]{:S(2)}, u32[]{:S(2)}) collective-permute-start(bf16[256,640]{1,0:T(8,128)(2,1)S(1)} %slice.89), channel_id=1, source_target_pairs={{0,16},{8,24},{16,0},{24,8},{1,17},{9,25},{17,1},{25,9},{2,18},{10... | collective-permute-start | bytes 983048 | tf_op jit(solution)/shard_map/ppermute | solution.py:435
  30.2 5.3 %collective-permute-start.9 = (bf16[144,256]{1,0:T(8,128)(2,1)S(1)}, bf16[144,256]{1,0:T(8,128)(2,1)S(1)}, u32[]{:S(2)}, u32[]{:S(2)}) collective-permute-start(bf16[144,256]{1,0:T(8,128)(2,1)S(1)} %pad_maximum_fusion.1), channel_id=1, source_target_pairs={{0,4},{1,5},{2,6},{3,7},{4,0},{5,1},{6,2},{7,3},{8,12},{9,13},{10,... | collective-permute-start | bytes 221192 | tf_op jit(solution)/shard_map/ppermute | solution.py:444
  37.1 2.2 %collective-permute-start.12 = (bf16[144,256]{1,0:T(8,128)(2,1)S(1)}, bf16[144,256]{1,0:T(8,128)(2,1)S(1)}, u32[]{:S(2)}, u32[]{:S(2)}) collective-permute-start(bf16[144,256]{1,0:T(8,128)(2,1)S(1)} %shard_map.129.refs_0_), channel_id=1, source_target_pairs={{0,8},{8,0},{16,24},{24,16},{1,9},{9,1},{17,25},{25,17},{2,10},{10... | collective-permute-start | bytes 221192 | tf_op jit(solution)/shard_map/ppermute | solution.py:435
  37.2 4.7 %collective-permute-start.11 = (bf16[144,256]{1,0:T(8,128)(2,1)S(1)}, bf16[144,256]{1,0:T(8,128)(2,1)S(1)}, u32[]{:S(2)}, u32[]{:S(2)}) collective-permute-start(bf16[144,256]{1,0:T(8,128)(2,1)S(1)} %shard_map.129.refs_0_), channel_id=1, source_target_pairs={{0,16},{8,24},{16,0},{24,8},{1,17},{9,25},{17,1},{25,9},{2,18},{10... | collective-permute-start | bytes 221192 | tf_op jit(solution)/shard_map/ppermute | solution.py:435
  41.8 1.3 %collective-permute-start.13 = (bf16[144,256]{1,0:T(8,128)(2,1)S(1)}, bf16[144,256]{1,0:T(8,128)(2,1)S(1)}, u32[]{:S(2)}, u32[]{:S(2)}) collective-permute-start(bf16[144,256]{1,0:T(8,128)(2,1)S(1)} %collective-permute-done.11.refs_0_.refs_2_), channel_id=1, source_target_pairs={{0,8},{8,0},{16,24},{24,16},{1,9},{9,1},{17,25},{25,17},{2,10},{10... | collective-permute-start | bytes 221192 | tf_op jit(solution)/shard_map/ppermute | solution.py:435

commit v5 on v4

--- a/solution.py
+++ b/solution.py
@@ -106,30 +106,6 @@
         copy.wait()
 
 
-def gain_kernel(blocks, facts_ref, gains_ref, weight_ref, core_ref, effective_ref, response_ref):
-    slots = blocks * BLOCK_VOX
-    subjects = gains_ref.shape[0]
-    whole = gains_ref[...]
-    high = whole.astype(BF16).astype(F32)
-    middle = (whole - high).astype(BF16).astype(F32)
-    low = whole - high - middle
-    terms = jnp.concatenate([high, middle, low], axis=0).astype(BF16)
-    owner = jnp.concatenate(facts_of(facts_ref, blocks)[0], axis=1)
-    row = lax.broadcasted_iota(jnp.int32, (3 * subjects, slots), 0) % subjects
-    pick = jnp.where(row == owner, 1.0, 0.0).astype(BF16)
-    scale = lax.dot_general(
-        terms, pick, (((0,), (0,)), ((), ())), preferred_element_type=F32
-    )
-    effective_ref[...] = (weight_ref[...].astype(F32) * scale).astype(BF16)
-    for b in range(0, blocks, 2):
-        many = min(2, blocks - b)
-        lanes = slice(b * BLOCK_VOX, (b + many) * BLOCK_VOX)
-        part = jnp.dot(core_ref[...], effective_ref[:, lanes], preferred_element_type=F32)
-        part = part.astype(BF16).astype(F32)
-        for c in range(many):
-            response_ref[b + c] = part[:, c * BLOCK_VOX : (c + 1) * BLOCK_VOX]
-
-
 def conv_kernel(
     rows, blocks, facts_ref, clip_ref, near_ref, far_ref, taps_ref, depth_ref, deep_ref, ext
 ):
@@ -164,7 +140,22 @@
     depth_ref[...] = deep_ref[MARGIN : MARGIN + rows, :]
 
 
-def core_kernel(rows, clip_ref, near_ref, far_ref, deep_ref, point_ref, core_ref, ext):
+def core_kernel(
+    rows,
+    blocks,
+    clip_ref,
+    near_ref,
+    far_ref,
+    deep_ref,
+    point_ref,
+    facts_ref,
+    gains_ref,
+    weight_ref,
+    core_ref,
+    effective_ref,
+    response_ref,
+    ext,
+):
     feats = clip_ref.shape[1]
     odd = lax.axis_index("tm") % 2
     ext[MARGIN : MARGIN + rows, :] = clip_ref[...]
@@ -179,10 +170,31 @@
         ext[:MARGIN, :] = near_ref[MARGIN : 2 * MARGIN, :]
         ext[MARGIN + rows :, :] = far_ref[2 * MARGIN : 3 * MARGIN, :]
 
+    slots = blocks * BLOCK_VOX
+    subjects = gains_ref.shape[0]
+    whole = gains_ref[...]
+    high = whole.astype(BF16).astype(F32)
+    middle = (whole - high).astype(BF16).astype(F32)
+    low = whole - high - middle
+    terms = jnp.concatenate([high, middle, low], axis=0).astype(BF16)
+    owner = jnp.concatenate(facts_of(facts_ref, blocks)[0], axis=1)
+    row = lax.broadcasted_iota(jnp.int32, (3 * subjects, slots), 0) % subjects
+    pick = jnp.where(row == owner, 1.0, 0.0).astype(BF16)
+    scale = lax.dot_general(
+        terms, pick, (((0,), (0,)), ((), ())), preferred_element_type=F32
+    )
+    effective_ref[...] = (weight_ref[...].astype(F32) * scale).astype(BF16)
     for col in range(0, feats, 256):
         lanes = slice(col, col + 256)
         act = jnp.dot(deep_ref[...], point_ref[:, lanes], preferred_element_type=F32)
         core_ref[:, lanes] = (ext[:, lanes].astype(F32) + jax.nn.gelu(act)).astype(BF16)
+    for b in range(0, blocks, 2):
+        many = min(2, blocks - b)
+        lanes = slice(b * BLOCK_VOX, (b + many) * BLOCK_VOX)
+        part = jnp.dot(core_ref[...], effective_ref[:, lanes], preferred_element_type=F32)
+        part = part.astype(BF16).astype(F32)
+        for c in range(many):
+            response_ref[b + c] = part[:, c * BLOCK_VOX : (c + 1) * BLOCK_VOX]
 
 
 def block_at(position, bits):
@@ -491,25 +503,21 @@
             jax.ShapeDtypeStruct((rows + 2 * MARGIN, feats), BF16),
         ),
         [(VMEM, facts)] + halos + [(VMEM, depth_kernel)],
-        0.6,
+        0.1,
         [pltpu.VMEM((rows + 3 * MARGIN, feats), BF16)],
     )
-    core_out = call(
-        functools.partial(core_kernel, rows),
-        jax.ShapeDtypeStruct((rows + 2 * MARGIN, feats), BF16),
-        halos + [(VMEM, deep), (VMEM, point_weight)],
+    core_out, effective, response = call(
+        functools.partial(core_kernel, rows, blocks),
+        (
+            jax.ShapeDtypeStruct((rows + 2 * MARGIN, feats), BF16),
+            jax.ShapeDtypeStruct((feats, slots), BF16),
+            jax.ShapeDtypeStruct((blocks, rows + 2 * MARGIN, BLOCK_VOX), F32),
+        ),
+        halos
+        + [(VMEM, deep), (VMEM, point_weight), (VMEM, facts)]
+        + [(VMEM, subject_feature_gains), (VMEM, readout_weight)],
         1.0,
         [pltpu.VMEM((rows + 2 * MARGIN, feats), BF16)],
-    )
-    core_out, late_gains = lax.optimization_barrier((core_out, subject_feature_gains))
-    effective, response = call(
-        functools.partial(gain_kernel, blocks),
-        (
-            jax.ShapeDtypeStruct((feats, slots), BF16),
-            jax.ShapeDtypeStruct((blocks, rows + 2 * MARGIN, BLOCK_VOX), F32),
-        ),
-        [(VMEM, facts), (VMEM, late_gains), (VMEM, readout_weight), (VMEM, core_out)],
-        1.5,
     )
     response, mine = lax.optimization_barrier((response, mine))
     twin = swap_tm(mine, 0)

time: 44.5 us -> 44.1 us (level)
    pallas_call x11 -> x10, Pallas kernels: 10.2 us -> 10.1 us  [call(): pl.pallas_call(body, out_shape=outs, in_specs=[spec for spec, _ in ins],...]
where the time goes in v5:
time: 44.1 us; the launch traced here: 43.9 us
  starting transfers between devices  16.5 us (37%)
  waiting for transfers between devices  13.6 us (31%)
  Pallas kernels  12.3 us (28%)
  between operations  0.99 us (2%)
    ppermute x5, starting transfers between devices, across(): return lax.ppermute(value, ('tm', 'vox'), pairs)  11 us
    pallas_call x10, Pallas kernels, call(): pl.pallas_call(body, out_shape=outs, in_specs=[spec for spec, _ in ins],...  10.1 us
    ppermute x5, waiting for transfers between devices, across(): return lax.ppermute(value, ('tm', 'vox'), pairs)  8.98 us
    ppermute x10, starting transfers between devices, swap_tm(): lax.ppermute(value, 'tm', [(i, i ^ 1 << bit) for i in range(tm_count)])  5.55 us
    ppermute x10, waiting for transfers between devices, swap_tm(): lax.ppermute(value, 'tm', [(i, i ^ 1 << bit) for i in range(tm_count)])  4.65 us
    pallas_call x1, Pallas kernels, shards(): pl.pallas_call(functools.partial(last_kernel, len(others), len(groups[2])...  1.17 us
    pallas_call x1, Pallas kernels, shards(): pl.pallas_call(functools.partial(pack_kernel, rows, blocks), out_shape=(p...  1.05 us
  transfers between devices with their start and end apart: 15, of which 6 were waited for; matrix products, arithmetic and copies ran while one was open for 1% of the time, Pallas kernels for 23%

profile of v5, /device:TPU:0, one launch (start us, length us, event | category | flops | bytes accessed | tf_op | source)
XLA Modules:
  0.0 43.9 jit_solution(17897018958913320498)
XLA Ops:
  0.7 1.0 %shard_map.121 = (bf16[64,1024]{1,0:T(8,128)(2,1)S(1)}, s32[8,128]{1,0:T(8,128)S(1)}, s32[24,128]{1,0:T(8,128)S(1)}) custom-call(s32[5]{0:T(128)} %subject_ref.1, s32[5]{0:T(128)} %live_hbm.1, s32[8]{0:T(128)} %lengths_hbm.1, bf16[256,1024]{1,0:T(8,128)(2,1)} %clip_ref.5, bf16[256,640]{1,0:T(8,128)(2,1)} %bold_ref.3), custom_call_target="tpu_custom_call" | custom-call | flops 6899999744 | bytes 1000000 | tf_op jit(solution)/shard_map/pallas_call | solution.py:470
  1.7 0.5 %collective-permute-start = (bf16[64,1024]{1,0:T(8,128)(2,1)S(1)}, bf16[64,1024]{1,0:T(8,128)(2,1)S(1)}, u32[]{:S(2)}, u32[]{:S(2)}) collective-permute-start(bf16[64,1024]{1,0:T(8,128)(2,1)S(1)} %get-tuple-element.33), channel_id=1, source_target_pairs={{0,8},{8,0},{16,24},{24,16},{1,9},{9,1},{17,25},{25,17},{2,10},{10... | collective-permute-start | bytes 393224 | tf_op jit(solution)/shard_map/ppermute | solution.py:447
  2.2 0.7 %collective-permute-start.1 = (bf16[64,1024]{1,0:T(8,128)(2,1)S(1)}, bf16[64,1024]{1,0:T(8,128)(2,1)S(1)}, u32[]{:S(2)}, u32[]{:S(2)}) collective-permute-start(bf16[64,1024]{1,0:T(8,128)(2,1)S(1)} %get-tuple-element.33), channel_id=1, source_target_pairs={{8,16},{9,17},{10,18},{11,19},{12,20},{13,21},{14,22},{15,23},{16,... | collective-permute-start | bytes 393224 | tf_op jit(solution)/shard_map/ppermute | solution.py:456
  2.9 4.4 %collective-permute-start.2 = (s32[8,128]{1,0:T(8,128)S(1)}, s32[8,128]{1,0:T(8,128)S(1)}, u32[]{:S(2)}, u32[]{:S(2)}) collective-permute-start(s32[8,128]{1,0:T(8,128)S(1)} %get-tuple-element.39), channel_id=1, source_target_pairs={{0,1},{1,0},{2,3},{3,2},{4,5},{5,4},{6,7},{7,6},{9,10},{10,9},{11,... | collective-permute-start | bytes 12296 | tf_op jit(solution)/shard_map/ppermute | solution.py:456
  7.4 0.1 constant_dynamic-slice_fusion.1.point_ref
  7.5 0.6 %shard_map.122 = (bf16[256,1024]{1,0:T(8,128)(2,1)S(1)}, bf16[288,1024]{1,0:T(8,128)(2,1)S(1)}) custom-call(s32[24,128]{1,0:T(8,128)S(1)} %get-tuple-element.34.facts_ref, bf16[256,1024]{1,0:T(8,128)(2,1)S(1)} %copy-done.1, bf16[64,1024]{1,0:T(8,128)(2,1)S(1)} %collective-permute-done.near_ref, bf16[64,1024]{1,0:T(8,128)(2,1)S(1)} %collective-permute-done.1.far_ref, ...), custom_call_target="tpu_custom_call" | custom-call | flops 115000000 | bytes 100000 | tf_op jit(solution)/shard_map/pallas_call | solution.py:23
  8.1 3.6 %collective-permute-start.5 = (bf16[256,1024]{1,0:T(8,128)(2,1)S(1)}, bf16[256,1024]{1,0:T(8,128)(2,1)S(1)}, u32[]{:S(2)}, u32[]{:S(2)}) collective-permute-start(bf16[256,1024]{1,0:T(8,128)(2,1)S(1)} %get-tuple-element.45.depth_ref.refs_2_), channel_id=1, source_target_pairs={{0,16},{8,24},{16,0},{24,8},{1,17},{9,25},{17,1},{25,9},{2,18},{10... | collective-permute-start | bytes 1572872 | tf_op jit(solution)/shard_map/ppermute | solution.py:447
  11.7 2.1 %shard_map.123 = (bf16[288,1024]{1,0:T(8,128)(2,1)S(1)}, bf16[1024,640]{1,0:T(8,128)(2,1)S(1)}, f32[5,288,128]{2,1,0:T(8,128)S(1)}) custom-call(bf16[256,1024]{1,0:T(8,128)(2,1)S(1)} %copy-done.1, bf16[64,1024]{1,0:T(8,128)(2,1)S(1)} %collective-permute-done.near_ref, bf16[64,1024]{1,0:T(8,128)(2,1)S(1)} %collective-permute-done.1.far_ref, ...), custom_call_target="tpu_custom_call" | custom-call | flops 1150000000 | bytes 1000000 | tf_op jit(solution)/shard_map/pallas_call | solution.py:23
  13.8 0.6 %collective-permute-start.3 = (s32[8,128]{1,0:T(8,128)S(1)}, s32[8,128]{1,0:T(8,128)S(1)}, u32[]{:S(2)}, u32[]{:S(2)}) collective-permute-start(s32[8,128]{1,0:T(8,128)S(1)} %collective-permute-done.2.mine_ref), channel_id=1, source_target_pairs={{0,8},{8,0},{16,24},{24,16},{1,9},{9,1},{17,25},{25,17},{2,10},{10... | collective-permute-start | bytes 12296 | tf_op jit(solution)/shard_map/ppermute | solution.py:447
  14.3 1.6 %shard_map.124.misfit_ref = f32[5,272,128]{2,1,0:T(8,128)S(1)} custom-call(s32[24,128]{1,0:T(8,128)S(1)} %get-tuple-element.34.facts_ref, f32[5,288,128]{2,1,0:T(8,128)S(1)} %get-tuple-element.41.response_ref, f32[16,640]{1,0:T(8,128)S(1)} %copy-done.6, bf16[256,640]{1,0:T(8,128)(2,1)S(1)} %copy-done.5, bf16[64,1024]{1,0:T(8,128)(2,1)S(1)} %collective-permute-done.near_ref, ...), custom_call_target="tpu_custom_call" | custom-call | flops 1724999936 | bytes 1500000 | tf_op jit(solution)/shard_map/pallas_call | solution.py:23
  16.0 2.0 %shard_map.125 = (bf16[256,640]{1,0:T(8,128)(2,1)S(1)}, bf16[528,256]{1,0:T(8,128)(2,1)S(1)}, f32[8,128]{1,0:T(8,128)S(1)}) custom-call(s32[24,128]{1,0:T(8,128)S(1)} %get-tuple-element.34.facts_ref, s32[8,128]{1,0:T(8,128)S(1)} %collective-permute-done.2.mine_ref, s32[8,128]{1,0:T(8,128)S(1)} %collective-permute-done.3.twin_ref, ...), custom_call_target="tpu_custom_call" | custom-call | flops 2875000064 | bytes 2500000 | tf_op jit(solution)/shard_map/pallas_call | solution.py:23
  17.9 1.6 %collective-permute-start.4 = (bf16[528,256]{1,0:T(8,128)(2,1)S(1)}, bf16[528,256]{1,0:T(8,128)(2,1)S(1)}, u32[]{:S(2)}, u32[]{:S(2)}) collective-permute-start(bf16[528,256]{1,0:T(8,128)(2,1)S(1)} %get-tuple-element.44), channel_id=1, source_target_pairs={{0,1},{1,0},{2,3},{3,2},{4,5},{5,4},{6,7},{7,6},{8,10},{9,11},{10,... | collective-permute-start | bytes 811016 | tf_op jit(solution)/shard_map/ppermute | solution.py:456
  19.5 0.4 shard_map.127.slope_ref
  19.9 1.1 %shard_map.126 = (f32[512,256]{1,0:T(8,128)S(1)}, bf16[512,640]{1,0:T(8,128)(2,1)S(1)}, f32[512,640]{1,0:T(8,128)S(1)}) custom-call(bf16[288,1024]{1,0:T(8,128)(2,1)S(1)} %get-tuple-element.36.core_ref, bf16[1024,640]{1,0:T(8,128)(2,1)S(1)} %get-tuple-element.37.effective_ref, bf16[256,640]{1,0:T(8,128)(2,1)S(1)} %get-tuple-element.42.half_ref), custom_call_target="tpu_custom_call" | custom-call | flops 1264999936 | bytes 1100000 | tf_op jit(solution)/shard_map/pallas_call | solution.py:23
  21.0 0.1 collective-permute-start.8
  21.1 3.4 %collective-permute-done.4 = bf16[528,256]{1,0:T(8,128)(2,1)S(1)} collective-permute-done((bf16[528,256]{1,0:T(8,128)(2,1)S(1)}, bf16[528,256]{1,0:T(8,128)(2,1)S(1)}, u32[]{:S(2)}, u32[]{:S(2)}) %collective-permute-start.4) | collective-permute-done | bytes 270368 | tf_op jit(solution)/shard_map/ppermute | solution.py:456
  24.5 0.1 convert_add_fusion.1
  24.6 1.6 %collective-permute-start.7 = (bf16[272,256]{1,0:T(8,128)(2,1)S(1)}, bf16[272,256]{1,0:T(8,128)(2,1)S(1)}, u32[]{:S(2)}, u32[]{:S(2)}) collective-permute-start(bf16[272,256]{1,0:T(8,128)(2,1)S(1)} %pad_maximum_fusion), channel_id=1, source_target_pairs={{0,2},{1,3},{2,0},{3,1},{4,6},{5,7},{6,4},{7,5},{8,9},{9,8},{10,11... | collective-permute-start | bytes 417800 | tf_op jit(solution)/shard_map/ppermute | solution.py:456
  26.3 0.1 convert_add_fusion
  26.5 0.4 collective-permute-start.10
  26.9 2.9 %collective-permute-done.7 = bf16[272,256]{1,0:T(8,128)(2,1)S(1)} collective-permute-done((bf16[272,256]{1,0:T(8,128)(2,1)S(1)}, bf16[272,256]{1,0:T(8,128)(2,1)S(1)}, u32[]{:S(2)}, u32[]{:S(2)}) %collective-permute-start.7) | collective-permute-done | bytes 139296 | tf_op jit(solution)/shard_map/ppermute | solution.py:456
  29.9 2.6 %collective-permute-start.9 = (bf16[144,256]{1,0:T(8,128)(2,1)S(1)}, bf16[144,256]{1,0:T(8,128)(2,1)S(1)}, u32[]{:S(2)}, u32[]{:S(2)}) collective-permute-start(bf16[144,256]{1,0:T(8,128)(2,1)S(1)} %pad_maximum_fusion.1), channel_id=1, source_target_pairs={{0,4},{1,5},{2,6},{3,7},{4,0},{5,1},{6,2},{7,3},{8,12},{9,13},{10,... | collective-permute-start | bytes 221192 | tf_op jit(solution)/shard_map/ppermute | solution.py:456
  32.5 2.7 %collective-permute-done.9.arrived_ref = bf16[144,256]{1,0:T(8,128)(2,1)S(1)} collective-permute-done((bf16[144,256]{1,0:T(8,128)(2,1)S(1)}, bf16[144,256]{1,0:T(8,128)(2,1)S(1)}, u32[]{:S(2)}, u32[]{:S(2)}) %collective-permute-start.9) | collective-permute-done | bytes 73760 | tf_op jit(solution)/shard_map/ppermute | solution.py:456
  35.2 1.4 %collective-permute-done.10.arrived_ref = bf16[256,640]{1,0:T(8,128)(2,1)S(1)} collective-permute-done((bf16[256,640]{1,0:T(8,128)(2,1)S(1)}, bf16[256,640]{1,0:T(8,128)(2,1)S(1)}, u32[]{:S(2)}, u32[]{:S(2)}) %collective-permute-start.10) | collective-permute-done | bytes 327712 | tf_op jit(solution)/shard_map/ppermute | solution.py:447
  36.7 0.1 collective-permute-start.12
  36.8 0.4 collective-permute-start.11
  37.2 1.8 %shard_map.130 = f32[256,640]{1,0:T(8,128)} custom-call(s32[5]{0:T(128)S(1)} %copy-done.7, f32[256,640]{1,0:T(8,128)S(1)} %slice.67.keep_ref, bf16[256,640]{1,0:T(8,128)(2,1)S(1)} %collective-permute-done.10.arrived_ref, f32[16,256]{1,0:T(8,128)S(1)} %constant_dynamic-slice_fusion.gains_ref), custom_call_target="tpu_custom_call" | custom-call | flops 920000000 | bytes 800000 | tf_op jit(solution)/shard_map/pallas_call | solution.py:23
  39.0 0.3 shard_map.129.before_ref
  39.3 2.2 %collective-permute-done.11.refs_0_.refs_2_ = bf16[144,256]{1,0:T(8,128)(2,1)S(1)} collective-permute-done((bf16[144,256]{1,0:T(8,128)(2,1)S(1)}, bf16[144,256]{1,0:T(8,128)(2,1)S(1)}, u32[]{:S(2)}, u32[]{:S(2)}) %collective-permute-start.11) | collective-permute-done | bytes 73760 | tf_op jit(solution)/shard_map/ppermute | solution.py:447
  41.5 0.2 shard_map.131.total_ref
  41.7 1.0 %collective-permute-done.13.refs_3_ = bf16[144,256]{1,0:T(8,128)(2,1)S(1)} collective-permute-done((bf16[144,256]{1,0:T(8,128)(2,1)S(1)}, bf16[144,256]{1,0:T(8,128)(2,1)S(1)}, u32[]{:S(2)}, u32[]{:S(2)}) %collective-permute-start.13) | collective-permute-done | bytes 73760 | tf_op jit(solution)/shard_map/ppermute | solution.py:447
  42.7 1.2 %shard_map.132 = (f32[1024,128]{1,0:T(8,128)}, f32[1,1]{1,0:T(1,128)}) custom-call(f32[128,1024]{1,0:T(8,128)S(1)} %shard_map.131.total_ref, bf16[144,256]{1,0:T(8,128)(2,1)S(1)} %shard_map.128.refs_0_, bf16[144,256]{1,0:T(8,128)(2,1)S(1)} %collective-permute-done.12.refs_1_, bf16[144,256]{1,0:T(8,128)(2,1)S(1)} %collective-permute-done.11.refs_0_.refs_2_, ...), custom_call_target="tpu_custom_call" | custom-call | flops 1150000000 | bytes 1000000 | tf_op jit(solution)/shard_map/pallas_call | solution.py:669
  (46 shorter events, 0.3 us)
Async XLA Ops:
  0.6 6.9 %copy-start.1 = (bf16[256,1024]{1,0:T(8,128)(2,1)S(1)}, bf16[256,1024]{1,0:T(8,128)(2,1)}, u32[]{:S(2)}) copy-start(bf16[256,1024]{1,0:T(8,128)(2,1)} %clip_ref.5) | copy-start | bytes 1572868
  0.6 6.7 %copy-start = (bf16[1024,1024]{1,0:T(8,128)(2,1)S(1)}, bf16[1024,1024]{1,0:T(8,128)(2,1)}, u32[]{:S(2)}) copy-start(bf16[1024,1024]{1,0:T(8,128)(2,1)} %point_ref.1) | copy-start | bytes 6291460
  0.7 6.9 %copy-start.4 = (f32[3,1024]{1,0:T(4,128)S(1)}, f32[3,1024]{1,0:T(4,128)}, u32[]{:S(2)}) copy-start(f32[3,1024]{1,0:T(4,128)} %taps_ref.1) | copy-start | bytes 36868
  1.7 10.0 %copy-start.3 = (f32[16,1024]{1,0:T(8,128)S(1)}, f32[16,1024]{1,0:T(8,128)}, u32[]{:S(2)}) copy-start(f32[16,1024]{1,0:T(8,128)} %gains_ref.1) | copy-start | bytes 196612
  1.7 5.8 %collective-permute-start = (bf16[64,1024]{1,0:T(8,128)(2,1)S(1)}, bf16[64,1024]{1,0:T(8,128)(2,1)S(1)}, u32[]{:S(2)}, u32[]{:S(2)}) collective-permute-start(bf16[64,1024]{1,0:T(8,128)(2,1)S(1)} %get-tuple-element.33), channel_id=1, source_target_pairs={{0,8},{8,0},{16,24},{24,16},{1,9},{9,1},{17,25},{25,17},{2,10},{10... | collective-permute-start | bytes 393224 | tf_op jit(solution)/shard_map/ppermute | solution.py:447
  2.2 5.2 %collective-permute-start.1 = (bf16[64,1024]{1,0:T(8,128)(2,1)S(1)}, bf16[64,1024]{1,0:T(8,128)(2,1)S(1)}, u32[]{:S(2)}, u32[]{:S(2)}) collective-permute-start(bf16[64,1024]{1,0:T(8,128)(2,1)S(1)} %get-tuple-element.33), channel_id=1, source_target_pairs={{8,16},{9,17},{10,18},{11,19},{12,20},{13,21},{14,22},{15,23},{16,... | collective-permute-start | bytes 393224 | tf_op jit(solution)/shard_map/ppermute | solution.py:456
  2.9 10.9 %collective-permute-start.2 = (s32[8,128]{1,0:T(8,128)S(1)}, s32[8,128]{1,0:T(8,128)S(1)}, u32[]{:S(2)}, u32[]{:S(2)}) collective-permute-start(s32[8,128]{1,0:T(8,128)S(1)} %get-tuple-element.39), channel_id=1, source_target_pairs={{0,1},{1,0},{2,3},{3,2},{4,5},{5,4},{6,7},{7,6},{9,10},{10,9},{11,... | collective-permute-start | bytes 12296 | tf_op jit(solution)/shard_map/ppermute | solution.py:456
  7.4 4.3 %copy-start.2 = (bf16[1024,640]{1,0:T(8,128)(2,1)S(1)}, bf16[1024,640]{1,0:T(8,128)(2,1)}, u32[]{:S(2)}) copy-start(bf16[1024,640]{1,0:T(8,128)(2,1)} %weight_ref.1) | copy-start | bytes 3932164
  8.1 16.4 %collective-permute-start.5 = (bf16[256,1024]{1,0:T(8,128)(2,1)S(1)}, bf16[256,1024]{1,0:T(8,128)(2,1)S(1)}, u32[]{:S(2)}, u32[]{:S(2)}) collective-permute-start(bf16[256,1024]{1,0:T(8,128)(2,1)S(1)} %get-tuple-element.45.depth_ref.refs_2_), channel_id=1, source_target_pairs={{0,16},{8,24},{16,0},{24,8},{1,17},{9,25},{17,1},{25,9},{2,18},{10... | collective-permute-start | bytes 1572872 | tf_op jit(solution)/shard_map/ppermute | solution.py:447
  11.7 12.8 %collective-permute-start.6 = (bf16[256,1024]{1,0:T(8,128)(2,1)S(1)}, bf16[256,1024]{1,0:T(8,128)(2,1)S(1)}, u32[]{:S(2)}, u32[]{:S(2)}) collective-permute-start(bf16[256,1024]{1,0:T(8,128)(2,1)S(1)} %get-tuple-element.45.depth_ref.refs_2_), channel_id=1, source_target_pairs={{0,8},{8,0},{16,24},{24,16},{1,9},{9,1},{17,25},{25,17},{2,10},{10... | collective-permute-start | bytes 1572872 | tf_op jit(solution)/shard_map/ppermute | solution.py:447
  11.7 2.7 %copy-start.5 = (bf16[256,640]{1,0:T(8,128)(2,1)S(1)}, bf16[256,640]{1,0:T(8,128)(2,1)}, u32[]{:S(2)}) copy-start(bf16[256,640]{1,0:T(8,128)(2,1)} %bold_ref.3) | copy-start | bytes 983044
  11.7 2.6 %copy-start.6 = (f32[16,640]{1,0:T(8,128)S(1)}, f32[16,640]{1,0:T(8,128)}, u32[]{:S(2)}) copy-start(f32[16,640]{1,0:T(8,128)} %hrf_ref.3) | copy-start | bytes 122884
  13.8 2.2 %collective-permute-start.3 = (s32[8,128]{1,0:T(8,128)S(1)}, s32[8,128]{1,0:T(8,128)S(1)}, u32[]{:S(2)}, u32[]{:S(2)}) collective-permute-start(s32[8,128]{1,0:T(8,128)S(1)} %collective-permute-done.2.mine_ref), channel_id=1, source_target_pairs={{0,8},{8,0},{16,24},{24,16},{1,9},{9,1},{17,25},{25,17},{2,10},{10... | collective-permute-start | bytes 12296 | tf_op jit(solution)/shard_map/ppermute | solution.py:447
  17.9 6.5 %collective-permute-start.4 = (bf16[528,256]{1,0:T(8,128)(2,1)S(1)}, bf16[528,256]{1,0:T(8,128)(2,1)S(1)}, u32[]{:S(2)}, u32[]{:S(2)}) collective-permute-start(bf16[528,256]{1,0:T(8,128)(2,1)S(1)} %get-tuple-element.44), channel_id=1, source_target_pairs={{0,1},{1,0},{2,3},{3,2},{4,5},{5,4},{6,7},{7,6},{8,10},{9,11},{10,... | collective-permute-start | bytes 811016 | tf_op jit(solution)/shard_map/ppermute | solution.py:456
  21.0 5.2 %collective-permute-start.8 = (bf16[512,640]{1,0:T(8,128)(2,1)S(1)}, bf16[512,640]{1,0:T(8,128)(2,1)S(1)}, u32[]{:S(2)}, u32[]{:S(2)}) collective-permute-start(bf16[512,640]{1,0:T(8,128)(2,1)S(1)} %get-tuple-element.49), channel_id=1, source_target_pairs={{0,8},{8,0},{16,24},{24,16},{1,9},{9,1},{17,25},{25,17},{2,10},{10... | collective-permute-start | bytes 1966088 | tf_op jit(solution)/shard_map/ppermute | solution.py:447
  24.6 5.1 %collective-permute-start.7 = (bf16[272,256]{1,0:T(8,128)(2,1)S(1)}, bf16[272,256]{1,0:T(8,128)(2,1)S(1)}, u32[]{:S(2)}, u32[]{:S(2)}) collective-permute-start(bf16[272,256]{1,0:T(8,128)(2,1)S(1)} %pad_maximum_fusion), channel_id=1, source_target_pairs={{0,2},{1,3},{2,0},{3,1},{4,6},{5,7},{6,4},{7,5},{8,9},{9,8},{10,11... | collective-permute-start | bytes 417800 | tf_op jit(solution)/shard_map/ppermute | solution.py:456
  26.3 15.5 %collective-permute-start.14 = (bf16[256,1024]{1,0:T(8,128)(2,1)S(1)}, bf16[256,1024]{1,0:T(8,128)(2,1)S(1)}, u32[]{:S(2)}, u32[]{:S(2)}) collective-permute-start(bf16[256,1024]{1,0:T(8,128)(2,1)S(1)} %collective-permute-done.5.refs_1_), channel_id=1, source_target_pairs={{0,8},{8,0},{16,24},{24,16},{1,9},{9,1},{17,25},{25,17},{2,10},{10... | collective-permute-start | bytes 1572872 | tf_op jit(solution)/shard_map/ppermute | solution.py:447
  26.5 10.7 %copy-start.7 = (s32[5]{0:T(128)S(1)}, s32[5]{0:T(128)}, u32[]{:S(2)}) copy-start(s32[5]{0:T(128)} %subject_ref.1) | copy-start | bytes 64
  26.5 10.2 %collective-permute-start.10 = (bf16[256,640]{1,0:T(8,128)(2,1)S(1)}, bf16[256,640]{1,0:T(8,128)(2,1)S(1)}, u32[]{:S(2)}, u32[]{:S(2)}) collective-permute-start(bf16[256,640]{1,0:T(8,128)(2,1)S(1)} %slice.89), channel_id=1, source_target_pairs={{0,16},{8,24},{16,0},{24,8},{1,17},{9,25},{17,1},{25,9},{2,18},{10... | collective-permute-start | bytes 983048 | tf_op jit(solution)/shard_map/ppermute | solution.py:447
  29.9 5.4 %collective-permute-start.9 = (bf16[144,256]{1,0:T(8,128)(2,1)S(1)}, bf16[144,256]{1,0:T(8,128)(2,1)S(1)}, u32[]{:S(2)}, u32[]{:S(2)}) collective-permute-start(bf16[144,256]{1,0:T(8,128)(2,1)S(1)} %pad_maximum_fusion.1), channel_id=1, source_target_pairs={{0,4},{1,5},{2,6},{3,7},{4,0},{5,1},{6,2},{7,3},{8,12},{9,13},{10,... | collective-permute-start | bytes 221192 | tf_op jit(solution)/shard_map/ppermute | solution.py:456
  36.7 2.3 %collective-permute-start.12 = (bf16[144,256]{1,0:T(8,128)(2,1)S(1)}, bf16[144,256]{1,0:T(8,128)(2,1)S(1)}, u32[]{:S(2)}, u32[]{:S(2)}) collective-permute-start(bf16[144,256]{1,0:T(8,128)(2,1)S(1)} %shard_map.128.refs_0_), channel_id=1, source_target_pairs={{0,8},{8,0},{16,24},{24,16},{1,9},{9,1},{17,25},{25,17},{2,10},{10... | collective-permute-start | bytes 221192 | tf_op jit(solution)/shard_map/ppermute | solution.py:447
  36.8 4.7 %collective-permute-start.11 = (bf16[144,256]{1,0:T(8,128)(2,1)S(1)}, bf16[144,256]{1,0:T(8,128)(2,1)S(1)}, u32[]{:S(2)}, u32[]{:S(2)}) collective-permute-start(bf16[144,256]{1,0:T(8,128)(2,1)S(1)} %shard_map.128.refs_0_), channel_id=1, source_target_pairs={{0,16},{8,24},{16,0},{24,8},{1,17},{9,25},{17,1},{25,9},{2,18},{10... | collective-permute-start | bytes 221192 | tf_op jit(solution)/shard_map/ppermute | solution.py:447
  41.5 1.3 %collective-permute-start.13 = (bf16[144,256]{1,0:T(8,128)(2,1)S(1)}, bf16[144,256]{1,0:T(8,128)(2,1)S(1)}, u32[]{:S(2)}, u32[]{:S(2)}) collective-permute-start(bf16[144,256]{1,0:T(8,128)(2,1)S(1)} %collective-permute-done.11.refs_0_.refs_2_), channel_id=1, source_target_pairs={{0,8},{8,0},{16,24},{24,16},{1,9},{9,1},{17,25},{25,17},{2,10},{10... | collective-permute-start | bytes 221192 | tf_op jit(solution)/shard_map/ppermute | solution.py:447

commit v6 on v5

--- a/solution.py
+++ b/solution.py
@@ -623,7 +623,6 @@
             lost = lost + loss_of(arrived[2 * size :])
             send = jnp.concatenate([keep[size:].astype(BF16), loss_rows(lost)], axis=0)
             keep = keep[:size]
-    arrived, raw_came = lax.optimization_barrier((arrived, raw_came))
     for path in paths[1:]:
         if path not in depths:
             depths[path] = swap_tm(depths[path[:-1]], path[-1])
@@ -651,7 +650,7 @@
         functools.partial(readout_kernel, blocks),
         jax.ShapeDtypeStruct((share, slots), F32),
         [(SMEM, block_subject), (VMEM, raw_keep), (VMEM, raw_came), (VMEM, own_gains)],
-        0.8,
+        4.0,
     )
     grads[top], total, grad_readout = lax.optimization_barrier(
         (grads[top], total, grad_readout)

time: 44.1 us -> 42.8 us (0.971)
  waiting for transfers between devices: 13.6 us -> 12.2 us
    ppermute x10, waiting for transfers between devices: 4.65 us -> 3.24 us  [swap_tm(): lax.ppermute(value, 'tm', [(i, i ^ 1 << bit) for i in range(tm_count)])]
  transfers between devices with their start and end apart: 15 -> 15, of which waited for: 6 -> 6; matrix products, arithmetic and copies ran while one was open for 1% -> 1% of each run, Pallas kernels for 23% -> 24%
where the time goes in v6:
time: 42.8 us; the launch traced here: 42.6 us
  starting transfers between devices  16.6 us (39%)
  Pallas kernels  12.3 us (29%)
  waiting for transfers between devices  12.2 us (29%)
  between operations  1 us (2%)
    ppermute x5, starting transfers between devices, across(): return lax.ppermute(value, ('tm', 'vox'), pairs)  11 us
    pallas_call x10, Pallas kernels, call(): pl.pallas_call(body, out_shape=outs, in_specs=[spec for spec, _ in ins],...  10.1 us
    ppermute x5, waiting for transfers between devices, across(): return lax.ppermute(value, ('tm', 'vox'), pairs)  8.99 us
    ppermute x10, starting transfers between devices, swap_tm(): lax.ppermute(value, 'tm', [(i, i ^ 1 << bit) for i in range(tm_count)])  5.68 us
    ppermute x10, waiting for transfers between devices, swap_tm(): lax.ppermute(value, 'tm', [(i, i ^ 1 << bit) for i in range(tm_count)])  3.24 us
    pallas_call x1, Pallas kernels, shards(): pl.pallas_call(functools.partial(last_kernel, len(others), len(groups[2])...  1.17 us
    pallas_call x1, Pallas kernels, shards(): pl.pallas_call(functools.partial(pack_kernel, rows, blocks), out_shape=(p...  1.05 us
  transfers between devices with their start and end apart: 15, of which 6 were waited for; matrix products, arithmetic and copies ran while one was open for 1% of the time, Pallas kernels for 24%

profile of v6, /device:TPU:0, one launch (start us, length us, event | category | flops | bytes accessed | tf_op | source)
XLA Modules:
  0.0 42.6 jit_solution(13481417726116280135)
XLA Ops:
  0.7 1.0 %shard_map.121 = (bf16[64,1024]{1,0:T(8,128)(2,1)S(1)}, s32[8,128]{1,0:T(8,128)S(1)}, s32[24,128]{1,0:T(8,128)S(1)}) custom-call(s32[5]{0:T(128)} %subject_ref.1, s32[5]{0:T(128)} %live_hbm.1, s32[8]{0:T(128)} %lengths_hbm.1, bf16[256,1024]{1,0:T(8,128)(2,1)} %clip_ref.5, bf16[256,640]{1,0:T(8,128)(2,1)} %bold_ref.3), custom_call_target="tpu_custom_call" | custom-call | flops 6899999744 | bytes 1000000 | tf_op jit(solution)/shard_map/pallas_call | solution.py:470
  1.7 0.5 %collective-permute-start = (bf16[64,1024]{1,0:T(8,128)(2,1)S(1)}, bf16[64,1024]{1,0:T(8,128)(2,1)S(1)}, u32[]{:S(2)}, u32[]{:S(2)}) collective-permute-start(bf16[64,1024]{1,0:T(8,128)(2,1)S(1)} %get-tuple-element.31), channel_id=1, source_target_pairs={{0,8},{8,0},{16,24},{24,16},{1,9},{9,1},{17,25},{25,17},{2,10},{10... | collective-permute-start | bytes 393224 | tf_op jit(solution)/shard_map/ppermute | solution.py:447
  2.2 0.7 %collective-permute-start.1 = (bf16[64,1024]{1,0:T(8,128)(2,1)S(1)}, bf16[64,1024]{1,0:T(8,128)(2,1)S(1)}, u32[]{:S(2)}, u32[]{:S(2)}) collective-permute-start(bf16[64,1024]{1,0:T(8,128)(2,1)S(1)} %get-tuple-element.31), channel_id=1, source_target_pairs={{8,16},{9,17},{10,18},{11,19},{12,20},{13,21},{14,22},{15,23},{16,... | collective-permute-start | bytes 393224 | tf_op jit(solution)/shard_map/ppermute | solution.py:456
  2.9 4.4 %collective-permute-start.2 = (s32[8,128]{1,0:T(8,128)S(1)}, s32[8,128]{1,0:T(8,128)S(1)}, u32[]{:S(2)}, u32[]{:S(2)}) collective-permute-start(s32[8,128]{1,0:T(8,128)S(1)} %get-tuple-element.37), channel_id=1, source_target_pairs={{0,1},{1,0},{2,3},{3,2},{4,5},{5,4},{6,7},{7,6},{9,10},{10,9},{11,... | collective-permute-start | bytes 12296 | tf_op jit(solution)/shard_map/ppermute | solution.py:456
  7.4 0.1 constant_dynamic-slice_fusion.1.point_ref
  7.5 0.6 %shard_map.122 = (bf16[256,1024]{1,0:T(8,128)(2,1)S(1)}, bf16[288,1024]{1,0:T(8,128)(2,1)S(1)}) custom-call(s32[24,128]{1,0:T(8,128)S(1)} %get-tuple-element.32.facts_ref, bf16[256,1024]{1,0:T(8,128)(2,1)S(1)} %copy-done.1, bf16[64,1024]{1,0:T(8,128)(2,1)S(1)} %collective-permute-done.near_ref, bf16[64,1024]{1,0:T(8,128)(2,1)S(1)} %collective-permute-done.1.far_ref, ...), custom_call_target="tpu_custom_call" | custom-call | flops 115000000 | bytes 100000 | tf_op jit(solution)/shard_map/pallas_call | solution.py:23
  8.1 3.6 %collective-permute-start.5 = (bf16[256,1024]{1,0:T(8,128)(2,1)S(1)}, bf16[256,1024]{1,0:T(8,128)(2,1)S(1)}, u32[]{:S(2)}, u32[]{:S(2)}) collective-permute-start(bf16[256,1024]{1,0:T(8,128)(2,1)S(1)} %get-tuple-element.43.depth_ref.refs_2_), channel_id=1, source_target_pairs={{0,16},{8,24},{16,0},{24,8},{1,17},{9,25},{17,1},{25,9},{2,18},{10... | collective-permute-start | bytes 1572872 | tf_op jit(solution)/shard_map/ppermute | solution.py:447
  11.7 2.1 %shard_map.123 = (bf16[288,1024]{1,0:T(8,128)(2,1)S(1)}, bf16[1024,640]{1,0:T(8,128)(2,1)S(1)}, f32[5,288,128]{2,1,0:T(8,128)S(1)}) custom-call(bf16[256,1024]{1,0:T(8,128)(2,1)S(1)} %copy-done.1, bf16[64,1024]{1,0:T(8,128)(2,1)S(1)} %collective-permute-done.near_ref, bf16[64,1024]{1,0:T(8,128)(2,1)S(1)} %collective-permute-done.1.far_ref, ...), custom_call_target="tpu_custom_call" | custom-call | flops 1150000000 | bytes 1000000 | tf_op jit(solution)/shard_map/pallas_call | solution.py:23
  13.8 0.6 %collective-permute-start.3 = (s32[8,128]{1,0:T(8,128)S(1)}, s32[8,128]{1,0:T(8,128)S(1)}, u32[]{:S(2)}, u32[]{:S(2)}) collective-permute-start(s32[8,128]{1,0:T(8,128)S(1)} %collective-permute-done.2.mine_ref), channel_id=1, source_target_pairs={{0,8},{8,0},{16,24},{24,16},{1,9},{9,1},{17,25},{25,17},{2,10},{10... | collective-permute-start | bytes 12296 | tf_op jit(solution)/shard_map/ppermute | solution.py:447
  14.3 1.6 %shard_map.124.misfit_ref = f32[5,272,128]{2,1,0:T(8,128)S(1)} custom-call(s32[24,128]{1,0:T(8,128)S(1)} %get-tuple-element.32.facts_ref, f32[5,288,128]{2,1,0:T(8,128)S(1)} %get-tuple-element.39.response_ref, f32[16,640]{1,0:T(8,128)S(1)} %copy-done.6, bf16[256,640]{1,0:T(8,128)(2,1)S(1)} %copy-done.5, bf16[64,1024]{1,0:T(8,128)(2,1)S(1)} %collective-permute-done.near_ref, ...), custom_call_target="tpu_custom_call" | custom-call | flops 1724999936 | bytes 1500000 | tf_op jit(solution)/shard_map/pallas_call | solution.py:23
  16.0 2.0 %shard_map.125 = (bf16[256,640]{1,0:T(8,128)(2,1)S(1)}, bf16[528,256]{1,0:T(8,128)(2,1)S(1)}, f32[8,128]{1,0:T(8,128)S(1)}) custom-call(s32[24,128]{1,0:T(8,128)S(1)} %get-tuple-element.32.facts_ref, s32[8,128]{1,0:T(8,128)S(1)} %collective-permute-done.2.mine_ref, s32[8,128]{1,0:T(8,128)S(1)} %collective-permute-done.3.twin_ref, ...), custom_call_target="tpu_custom_call" | custom-call | flops 2875000064 | bytes 2500000 | tf_op jit(solution)/shard_map/pallas_call | solution.py:23
  17.9 1.6 %collective-permute-start.4 = (bf16[528,256]{1,0:T(8,128)(2,1)S(1)}, bf16[528,256]{1,0:T(8,128)(2,1)S(1)}, u32[]{:S(2)}, u32[]{:S(2)}) collective-permute-start(bf16[528,256]{1,0:T(8,128)(2,1)S(1)} %get-tuple-element.42), channel_id=1, source_target_pairs={{0,1},{1,0},{2,3},{3,2},{4,5},{5,4},{6,7},{7,6},{8,10},{9,11},{10,... | collective-permute-start | bytes 811016 | tf_op jit(solution)/shard_map/ppermute | solution.py:456
  19.5 0.4 shard_map.127.slope_ref
  19.9 1.1 %shard_map.126 = (f32[512,256]{1,0:T(8,128)S(1)}, bf16[512,640]{1,0:T(8,128)(2,1)S(1)}, f32[512,640]{1,0:T(8,128)S(1)}) custom-call(bf16[288,1024]{1,0:T(8,128)(2,1)S(1)} %get-tuple-element.34.core_ref, bf16[1024,640]{1,0:T(8,128)(2,1)S(1)} %get-tuple-element.35.effective_ref, bf16[256,640]{1,0:T(8,128)(2,1)S(1)} %get-tuple-element.40.half_ref), custom_call_target="tpu_custom_call" | custom-call | flops 1264999936 | bytes 1100000 | tf_op jit(solution)/shard_map/pallas_call | solution.py:23
  21.0 0.1 collective-permute-start.8
  21.1 3.4 %collective-permute-done.4 = bf16[528,256]{1,0:T(8,128)(2,1)S(1)} collective-permute-done((bf16[528,256]{1,0:T(8,128)(2,1)S(1)}, bf16[528,256]{1,0:T(8,128)(2,1)S(1)}, u32[]{:S(2)}, u32[]{:S(2)}) %collective-permute-start.4) | collective-permute-done | bytes 270368 | tf_op jit(solution)/shard_map/ppermute | solution.py:456
  24.5 0.1 convert_add_fusion.1
  24.6 1.6 %collective-permute-start.7 = (bf16[272,256]{1,0:T(8,128)(2,1)S(1)}, bf16[272,256]{1,0:T(8,128)(2,1)S(1)}, u32[]{:S(2)}, u32[]{:S(2)}) collective-permute-start(bf16[272,256]{1,0:T(8,128)(2,1)S(1)} %pad_maximum_fusion), channel_id=1, source_target_pairs={{0,2},{1,3},{2,0},{3,1},{4,6},{5,7},{6,4},{7,5},{8,9},{9,8},{10,11... | collective-permute-start | bytes 417800 | tf_op jit(solution)/shard_map/ppermute | solution.py:456
  26.3 0.1 convert_add_fusion
  26.5 0.4 collective-permute-start.12
  26.9 2.9 %collective-permute-done.7 = bf16[272,256]{1,0:T(8,128)(2,1)S(1)} collective-permute-done((bf16[272,256]{1,0:T(8,128)(2,1)S(1)}, bf16[272,256]{1,0:T(8,128)(2,1)S(1)}, u32[]{:S(2)}, u32[]{:S(2)}) %collective-permute-start.7) | collective-permute-done | bytes 139296 | tf_op jit(solution)/shard_map/ppermute | solution.py:456
  29.9 2.6 %collective-permute-start.9 = (bf16[144,256]{1,0:T(8,128)(2,1)S(1)}, bf16[144,256]{1,0:T(8,128)(2,1)S(1)}, u32[]{:S(2)}, u32[]{:S(2)}) collective-permute-start(bf16[144,256]{1,0:T(8,128)(2,1)S(1)} %pad_maximum_fusion.1), channel_id=1, source_target_pairs={{0,4},{1,5},{2,6},{3,7},{4,0},{5,1},{6,2},{7,3},{8,12},{9,13},{10,... | collective-permute-start | bytes 221192 | tf_op jit(solution)/shard_map/ppermute | solution.py:456
  32.5 2.7 %collective-permute-done.9.arrived_ref = bf16[144,256]{1,0:T(8,128)(2,1)S(1)} collective-permute-done((bf16[144,256]{1,0:T(8,128)(2,1)S(1)}, bf16[144,256]{1,0:T(8,128)(2,1)S(1)}, u32[]{:S(2)}, u32[]{:S(2)}) %collective-permute-start.9) | collective-permute-done | bytes 73760 | tf_op jit(solution)/shard_map/ppermute | solution.py:456
  35.3 0.1 collective-permute-start.11
  35.3 0.5 %collective-permute-start.14 = (bf16[256,1024]{1,0:T(8,128)(2,1)S(1)}, bf16[256,1024]{1,0:T(8,128)(2,1)S(1)}, u32[]{:S(2)}, u32[]{:S(2)}) collective-permute-start(bf16[256,1024]{1,0:T(8,128)(2,1)S(1)} %collective-permute-done.5.refs_1_), channel_id=1, source_target_pairs={{0,8},{8,0},{16,24},{24,16},{1,9},{9,1},{17,25},{25,17},{2,10},{10... | collective-permute-start | bytes 1572872 | tf_op jit(solution)/shard_map/ppermute | solution.py:447
  35.8 0.8 %collective-permute-done.11.refs_1_ = bf16[144,256]{1,0:T(8,128)(2,1)S(1)} collective-permute-done((bf16[144,256]{1,0:T(8,128)(2,1)S(1)}, bf16[144,256]{1,0:T(8,128)(2,1)S(1)}, u32[]{:S(2)}, u32[]{:S(2)}) %collective-permute-start.11) | collective-permute-done | bytes 73760 | tf_op jit(solution)/shard_map/ppermute | solution.py:447
  36.6 0.3 shard_map.129.before_ref
  36.9 1.8 %shard_map.130 = f32[256,640]{1,0:T(8,128)} custom-call(s32[5]{0:T(128)S(1)} %copy-done.7, f32[256,640]{1,0:T(8,128)S(1)} %slice.67.keep_ref, bf16[256,640]{1,0:T(8,128)(2,1)S(1)} %collective-permute-done.12.arrived_ref, f32[16,256]{1,0:T(8,128)S(1)} %constant_dynamic-slice_fusion.gains_ref), custom_call_target="tpu_custom_call" | custom-call | flops 4600000000 | bytes 4000000 | tf_op jit(solution)/shard_map/pallas_call | solution.py:23
  38.7 1.5 %collective-permute-done.10.refs_0_.refs_2_ = bf16[144,256]{1,0:T(8,128)(2,1)S(1)} collective-permute-done((bf16[144,256]{1,0:T(8,128)(2,1)S(1)}, bf16[144,256]{1,0:T(8,128)(2,1)S(1)}, u32[]{:S(2)}, u32[]{:S(2)}) %collective-permute-start.10) | collective-permute-done | bytes 73760 | tf_op jit(solution)/shard_map/ppermute | solution.py:447
  40.2 0.2 shard_map.131.total_ref
  40.5 1.0 %collective-permute-done.13.refs_3_ = bf16[144,256]{1,0:T(8,128)(2,1)S(1)} collective-permute-done((bf16[144,256]{1,0:T(8,128)(2,1)S(1)}, bf16[144,256]{1,0:T(8,128)(2,1)S(1)}, u32[]{:S(2)}, u32[]{:S(2)}) %collective-permute-start.13) | collective-permute-done | bytes 73760 | tf_op jit(solution)/shard_map/ppermute | solution.py:447
  41.5 1.2 %shard_map.132 = (f32[1024,128]{1,0:T(8,128)}, f32[1,1]{1,0:T(1,128)}) custom-call(f32[128,1024]{1,0:T(8,128)S(1)} %shard_map.131.total_ref, bf16[144,256]{1,0:T(8,128)(2,1)S(1)} %shard_map.128.refs_0_, bf16[144,256]{1,0:T(8,128)(2,1)S(1)} %collective-permute-done.11.refs_1_, bf16[144,256]{1,0:T(8,128)(2,1)S(1)} %collective-permute-done.10.refs_0_.refs_2_, ...), custom_call_target="tpu_custom_call" | custom-call | flops 1150000000 | bytes 1000000 | tf_op jit(solution)/shard_map/pallas_call | solution.py:668
  (46 shorter events, 0.3 us)
Async XLA Ops:
  0.6 6.9 %copy-start.1 = (bf16[256,1024]{1,0:T(8,128)(2,1)S(1)}, bf16[256,1024]{1,0:T(8,128)(2,1)}, u32[]{:S(2)}) copy-start(bf16[256,1024]{1,0:T(8,128)(2,1)} %clip_ref.5) | copy-start | bytes 1572868
  0.6 6.7 %copy-start = (bf16[1024,1024]{1,0:T(8,128)(2,1)S(1)}, bf16[1024,1024]{1,0:T(8,128)(2,1)}, u32[]{:S(2)}) copy-start(bf16[1024,1024]{1,0:T(8,128)(2,1)} %point_ref.1) | copy-start | bytes 6291460
  0.7 6.9 %copy-start.4 = (f32[3,1024]{1,0:T(4,128)S(1)}, f32[3,1024]{1,0:T(4,128)}, u32[]{:S(2)}) copy-start(f32[3,1024]{1,0:T(4,128)} %taps_ref.1) | copy-start | bytes 36868
  1.7 10.0 %copy-start.3 = (f32[16,1024]{1,0:T(8,128)S(1)}, f32[16,1024]{1,0:T(8,128)}, u32[]{:S(2)}) copy-start(f32[16,1024]{1,0:T(8,128)} %gains_ref.1) | copy-start | bytes 196612
  1.7 5.8 %collective-permute-start = (bf16[64,1024]{1,0:T(8,128)(2,1)S(1)}, bf16[64,1024]{1,0:T(8,128)(2,1)S(1)}, u32[]{:S(2)}, u32[]{:S(2)}) collective-permute-start(bf16[64,1024]{1,0:T(8,128)(2,1)S(1)} %get-tuple-element.31), channel_id=1, source_target_pairs={{0,8},{8,0},{16,24},{24,16},{1,9},{9,1},{17,25},{25,17},{2,10},{10... | collective-permute-start | bytes 393224 | tf_op jit(solution)/shard_map/ppermute | solution.py:447
  2.2 5.2 %collective-permute-start.1 = (bf16[64,1024]{1,0:T(8,128)(2,1)S(1)}, bf16[64,1024]{1,0:T(8,128)(2,1)S(1)}, u32[]{:S(2)}, u32[]{:S(2)}) collective-permute-start(bf16[64,1024]{1,0:T(8,128)(2,1)S(1)} %get-tuple-element.31), channel_id=1, source_target_pairs={{8,16},{9,17},{10,18},{11,19},{12,20},{13,21},{14,22},{15,23},{16,... | collective-permute-start | bytes 393224 | tf_op jit(solution)/shard_map/ppermute | solution.py:456
  2.9 10.9 %collective-permute-start.2 = (s32[8,128]{1,0:T(8,128)S(1)}, s32[8,128]{1,0:T(8,128)S(1)}, u32[]{:S(2)}, u32[]{:S(2)}) collective-permute-start(s32[8,128]{1,0:T(8,128)S(1)} %get-tuple-element.37), channel_id=1, source_target_pairs={{0,1},{1,0},{2,3},{3,2},{4,5},{5,4},{6,7},{7,6},{9,10},{10,9},{11,... | collective-permute-start | bytes 12296 | tf_op jit(solution)/shard_map/ppermute | solution.py:456
  7.4 4.3 %copy-start.2 = (bf16[1024,640]{1,0:T(8,128)(2,1)S(1)}, bf16[1024,640]{1,0:T(8,128)(2,1)}, u32[]{:S(2)}) copy-start(bf16[1024,640]{1,0:T(8,128)(2,1)} %weight_ref.1) | copy-start | bytes 3932164
  8.1 16.4 %collective-permute-start.5 = (bf16[256,1024]{1,0:T(8,128)(2,1)S(1)}, bf16[256,1024]{1,0:T(8,128)(2,1)S(1)}, u32[]{:S(2)}, u32[]{:S(2)}) collective-permute-start(bf16[256,1024]{1,0:T(8,128)(2,1)S(1)} %get-tuple-element.43.depth_ref.refs_2_), channel_id=1, source_target_pairs={{0,16},{8,24},{16,0},{24,8},{1,17},{9,25},{17,1},{25,9},{2,18},{10... | collective-permute-start | bytes 1572872 | tf_op jit(solution)/shard_map/ppermute | solution.py:447
  11.7 12.8 %collective-permute-start.6 = (bf16[256,1024]{1,0:T(8,128)(2,1)S(1)}, bf16[256,1024]{1,0:T(8,128)(2,1)S(1)}, u32[]{:S(2)}, u32[]{:S(2)}) collective-permute-start(bf16[256,1024]{1,0:T(8,128)(2,1)S(1)} %get-tuple-element.43.depth_ref.refs_2_), channel_id=1, source_target_pairs={{0,8},{8,0},{16,24},{24,16},{1,9},{9,1},{17,25},{25,17},{2,10},{10... | collective-permute-start | bytes 1572872 | tf_op jit(solution)/shard_map/ppermute | solution.py:447
  11.7 2.7 %copy-start.5 = (bf16[256,640]{1,0:T(8,128)(2,1)S(1)}, bf16[256,640]{1,0:T(8,128)(2,1)}, u32[]{:S(2)}) copy-start(bf16[256,640]{1,0:T(8,128)(2,1)} %bold_ref.3) | copy-start | bytes 983044
  11.7 2.6 %copy-start.6 = (f32[16,640]{1,0:T(8,128)S(1)}, f32[16,640]{1,0:T(8,128)}, u32[]{:S(2)}) copy-start(f32[16,640]{1,0:T(8,128)} %hrf_ref.3) | copy-start | bytes 122884
  13.8 2.2 %collective-permute-start.3 = (s32[8,128]{1,0:T(8,128)S(1)}, s32[8,128]{1,0:T(8,128)S(1)}, u32[]{:S(2)}, u32[]{:S(2)}) collective-permute-start(s32[8,128]{1,0:T(8,128)S(1)} %collective-permute-done.2.mine_ref), channel_id=1, source_target_pairs={{0,8},{8,0},{16,24},{24,16},{1,9},{9,1},{17,25},{25,17},{2,10},{10... | collective-permute-start | bytes 12296 | tf_op jit(solution)/shard_map/ppermute | solution.py:447
  17.9 6.5 %collective-permute-start.4 = (bf16[528,256]{1,0:T(8,128)(2,1)S(1)}, bf16[528,256]{1,0:T(8,128)(2,1)S(1)}, u32[]{:S(2)}, u32[]{:S(2)}) collective-permute-start(bf16[528,256]{1,0:T(8,128)(2,1)S(1)} %get-tuple-element.42), channel_id=1, source_target_pairs={{0,1},{1,0},{2,3},{3,2},{4,5},{5,4},{6,7},{7,6},{8,10},{9,11},{10,... | collective-permute-start | bytes 811016 | tf_op jit(solution)/shard_map/ppermute | solution.py:456
  21.0 5.2 %collective-permute-start.8 = (bf16[512,640]{1,0:T(8,128)(2,1)S(1)}, bf16[512,640]{1,0:T(8,128)(2,1)S(1)}, u32[]{:S(2)}, u32[]{:S(2)}) collective-permute-start(bf16[512,640]{1,0:T(8,128)(2,1)S(1)} %get-tuple-element.47), channel_id=1, source_target_pairs={{0,8},{8,0},{16,24},{24,16},{1,9},{9,1},{17,25},{25,17},{2,10},{10... | collective-permute-start | bytes 1966088 | tf_op jit(solution)/shard_map/ppermute | solution.py:447
  24.6 5.1 %collective-permute-start.7 = (bf16[272,256]{1,0:T(8,128)(2,1)S(1)}, bf16[272,256]{1,0:T(8,128)(2,1)S(1)}, u32[]{:S(2)}, u32[]{:S(2)}) collective-permute-start(bf16[272,256]{1,0:T(8,128)(2,1)S(1)} %pad_maximum_fusion), channel_id=1, source_target_pairs={{0,2},{1,3},{2,0},{3,1},{4,6},{5,7},{6,4},{7,5},{8,9},{9,8},{10,11... | collective-permute-start | bytes 417800 | tf_op jit(solution)/shard_map/ppermute | solution.py:456
  26.5 10.4 %collective-permute-start.12 = (bf16[256,640]{1,0:T(8,128)(2,1)S(1)}, bf16[256,640]{1,0:T(8,128)(2,1)S(1)}, u32[]{:S(2)}, u32[]{:S(2)}) collective-permute-start(bf16[256,640]{1,0:T(8,128)(2,1)S(1)} %slice.89), channel_id=1, source_target_pairs={{0,16},{8,24},{16,0},{24,8},{1,17},{9,25},{17,1},{25,9},{2,18},{10... | collective-permute-start | bytes 983048 | tf_op jit(solution)/shard_map/ppermute | solution.py:447
  29.9 5.4 %collective-permute-start.9 = (bf16[144,256]{1,0:T(8,128)(2,1)S(1)}, bf16[144,256]{1,0:T(8,128)(2,1)S(1)}, u32[]{:S(2)}, u32[]{:S(2)}) collective-permute-start(bf16[144,256]{1,0:T(8,128)(2,1)S(1)} %pad_maximum_fusion.1), channel_id=1, source_target_pairs={{0,4},{1,5},{2,6},{3,7},{4,0},{5,1},{6,2},{7,3},{8,12},{9,13},{10,... | collective-permute-start | bytes 221192 | tf_op jit(solution)/shard_map/ppermute | solution.py:456
  32.5 4.4 %copy-start.7 = (s32[5]{0:T(128)S(1)}, s32[5]{0:T(128)}, u32[]{:S(2)}) copy-start(s32[5]{0:T(128)} %subject_ref.1) | copy-start | bytes 64
  35.3 1.3 %collective-permute-start.11 = (bf16[144,256]{1,0:T(8,128)(2,1)S(1)}, bf16[144,256]{1,0:T(8,128)(2,1)S(1)}, u32[]{:S(2)}, u32[]{:S(2)}) collective-permute-start(bf16[144,256]{1,0:T(8,128)(2,1)S(1)} %shard_map.128.refs_0_), channel_id=1, source_target_pairs={{0,8},{8,0},{16,24},{24,16},{1,9},{9,1},{17,25},{25,17},{2,10},{10... | collective-permute-start | bytes 221192 | tf_op jit(solution)/shard_map/ppermute | solution.py:447
  35.3 5.1 %collective-permute-start.14 = (bf16[256,1024]{1,0:T(8,128)(2,1)S(1)}, bf16[256,1024]{1,0:T(8,128)(2,1)S(1)}, u32[]{:S(2)}, u32[]{:S(2)}) collective-permute-start(bf16[256,1024]{1,0:T(8,128)(2,1)S(1)} %collective-permute-done.5.refs_1_), channel_id=1, source_target_pairs={{0,8},{8,0},{16,24},{24,16},{1,9},{9,1},{17,25},{25,17},{2,10},{10... | collective-permute-start | bytes 1572872 | tf_op jit(solution)/shard_map/ppermute | solution.py:447
  35.8 4.4 %collective-permute-start.10 = (bf16[144,256]{1,0:T(8,128)(2,1)S(1)}, bf16[144,256]{1,0:T(8,128)(2,1)S(1)}, u32[]{:S(2)}, u32[]{:S(2)}) collective-permute-start(bf16[144,256]{1,0:T(8,128)(2,1)S(1)} %shard_map.128.refs_0_), channel_id=1, source_target_pairs={{0,16},{8,24},{16,0},{24,8},{1,17},{9,25},{17,1},{25,9},{2,18},{10... | collective-permute-start | bytes 221192 | tf_op jit(solution)/shard_map/ppermute | solution.py:447
  40.2 1.3 %collective-permute-start.13 = (bf16[144,256]{1,0:T(8,128)(2,1)S(1)}, bf16[144,256]{1,0:T(8,128)(2,1)S(1)}, u32[]{:S(2)}, u32[]{:S(2)}) collective-permute-start(bf16[144,256]{1,0:T(8,128)(2,1)S(1)} %collective-permute-done.10.refs_0_.refs_2_), channel_id=1, source_target_pairs={{0,8},{8,0},{16,24},{24,16},{1,9},{9,1},{17,25},{25,17},{2,10},{10... | collective-permute-start | bytes 221192 | tf_op jit(solution)/shard_map/ppermute | solution.py:447

commit v7 on v6

--- a/solution.py
+++ b/solution.py
@@ -626,6 +626,9 @@
     for path in paths[1:]:
         if path not in depths:
             depths[path] = swap_tm(depths[path[:-1]], path[-1])
+    held = lax.optimization_barrier((arrived, *[depths[path] for path in paths[1:]]))
+    arrived = held[0]
+    depths.update(zip(paths[1:], held[1:]))
     pre_grad = call(
         grad_kernel,
         jax.ShapeDtypeStruct((width + 16, rows), BF16),

time: 42.8 us -> 42.7 us (level)
  no operation moved by 1% of the time
where the time goes in v7:
time: 42.7 us; the launch traced here: 42.5 us
  starting transfers between devices  16.2 us (38%)
  waiting for transfers between devices  12.5 us (29%)
  Pallas kernels  12.3 us (29%)
  between operations  0.99 us (2%)
    ppermute x5, starting transfers between devices, across(): return lax.ppermute(value, ('tm', 'vox'), pairs)  11 us
    pallas_call x10, Pallas kernels, call(): pl.pallas_call(body, out_shape=outs, in_specs=[spec for spec, _ in ins],...  10.1 us
    ppermute x5, waiting for transfers between devices, across(): return lax.ppermute(value, ('tm', 'vox'), pairs)  8.98 us
    ppermute x10, starting transfers between devices, swap_tm(): lax.ppermute(value, 'tm', [(i, i ^ 1 << bit) for i in range(tm_count)])  5.25 us
    ppermute x10, waiting for transfers between devices, swap_tm(): lax.ppermute(value, 'tm', [(i, i ^ 1 << bit) for i in range(tm_count)])  3.52 us
    pallas_call x1, Pallas kernels, shards(): pl.pallas_call(functools.partial(last_kernel, len(others), len(groups[2])...  1.17 us
    pallas_call x1, Pallas kernels, shards(): pl.pallas_call(functools.partial(pack_kernel, rows, blocks), out_shape=(p...  1.05 us
  transfers between devices with their start and end apart: 15, of which 6 were waited for; matrix products, arithmetic and copies ran while one was open for 1% of the time, Pallas kernels for 24%

profile of v7, /device:TPU:0, one launch (start us, length us, event | category | flops | bytes accessed | tf_op | source)
XLA Modules:
  0.0 42.5 jit_solution(11966505267432080709)
XLA Ops:
  0.7 1.0 %shard_map.121 = (bf16[64,1024]{1,0:T(8,128)(2,1)S(1)}, s32[8,128]{1,0:T(8,128)S(1)}, s32[24,128]{1,0:T(8,128)S(1)}) custom-call(s32[5]{0:T(128)} %subject_ref.1, s32[5]{0:T(128)} %live_hbm.1, s32[8]{0:T(128)} %lengths_hbm.1, bf16[256,1024]{1,0:T(8,128)(2,1)} %clip_ref.5, bf16[256,640]{1,0:T(8,128)(2,1)} %bold_ref.3), custom_call_target="tpu_custom_call" | custom-call | flops 6899999744 | bytes 1000000 | tf_op jit(solution)/shard_map/pallas_call | solution.py:470
  1.7 0.5 %collective-permute-start = (bf16[64,1024]{1,0:T(8,128)(2,1)S(1)}, bf16[64,1024]{1,0:T(8,128)(2,1)S(1)}, u32[]{:S(2)}, u32[]{:S(2)}) collective-permute-start(bf16[64,1024]{1,0:T(8,128)(2,1)S(1)} %get-tuple-element.35), channel_id=1, source_target_pairs={{0,8},{8,0},{16,24},{24,16},{1,9},{9,1},{17,25},{25,17},{2,10},{10... | collective-permute-start | bytes 393224 | tf_op jit(solution)/shard_map/ppermute | solution.py:447
  2.2 0.7 %collective-permute-start.1 = (bf16[64,1024]{1,0:T(8,128)(2,1)S(1)}, bf16[64,1024]{1,0:T(8,128)(2,1)S(1)}, u32[]{:S(2)}, u32[]{:S(2)}) collective-permute-start(bf16[64,1024]{1,0:T(8,128)(2,1)S(1)} %get-tuple-element.35), channel_id=1, source_target_pairs={{8,16},{9,17},{10,18},{11,19},{12,20},{13,21},{14,22},{15,23},{16,... | collective-permute-start | bytes 393224 | tf_op jit(solution)/shard_map/ppermute | solution.py:456
  2.9 4.4 %collective-permute-start.2 = (s32[8,128]{1,0:T(8,128)S(1)}, s32[8,128]{1,0:T(8,128)S(1)}, u32[]{:S(2)}, u32[]{:S(2)}) collective-permute-start(s32[8,128]{1,0:T(8,128)S(1)} %get-tuple-element.41), channel_id=1, source_target_pairs={{0,1},{1,0},{2,3},{3,2},{4,5},{5,4},{6,7},{7,6},{9,10},{10,9},{11,... | collective-permute-start | bytes 12296 | tf_op jit(solution)/shard_map/ppermute | solution.py:456
  7.4 0.1 constant_dynamic-slice_fusion.1.point_ref
  7.5 0.6 %shard_map.122 = (bf16[256,1024]{1,0:T(8,128)(2,1)S(1)}, bf16[288,1024]{1,0:T(8,128)(2,1)S(1)}) custom-call(s32[24,128]{1,0:T(8,128)S(1)} %get-tuple-element.36.facts_ref, bf16[256,1024]{1,0:T(8,128)(2,1)S(1)} %copy-done.1, bf16[64,1024]{1,0:T(8,128)(2,1)S(1)} %collective-permute-done.near_ref, bf16[64,1024]{1,0:T(8,128)(2,1)S(1)} %collective-permute-done.1.far_ref, ...), custom_call_target="tpu_custom_call" | custom-call | flops 115000000 | bytes 100000 | tf_op jit(solution)/shard_map/pallas_call | solution.py:23
  8.1 3.6 %collective-permute-start.5 = (bf16[256,1024]{1,0:T(8,128)(2,1)S(1)}, bf16[256,1024]{1,0:T(8,128)(2,1)S(1)}, u32[]{:S(2)}, u32[]{:S(2)}) collective-permute-start(bf16[256,1024]{1,0:T(8,128)(2,1)S(1)} %get-tuple-element.47.depth_ref.refs_2_), channel_id=1, source_target_pairs={{0,16},{8,24},{16,0},{24,8},{1,17},{9,25},{17,1},{25,9},{2,18},{10... | collective-permute-start | bytes 1572872 | tf_op jit(solution)/shard_map/ppermute | solution.py:447
  11.7 2.1 %shard_map.123 = (bf16[288,1024]{1,0:T(8,128)(2,1)S(1)}, bf16[1024,640]{1,0:T(8,128)(2,1)S(1)}, f32[5,288,128]{2,1,0:T(8,128)S(1)}) custom-call(bf16[256,1024]{1,0:T(8,128)(2,1)S(1)} %copy-done.1, bf16[64,1024]{1,0:T(8,128)(2,1)S(1)} %collective-permute-done.near_ref, bf16[64,1024]{1,0:T(8,128)(2,1)S(1)} %collective-permute-done.1.far_ref, ...), custom_call_target="tpu_custom_call" | custom-call | flops 1150000000 | bytes 1000000 | tf_op jit(solution)/shard_map/pallas_call | solution.py:23
  13.8 0.6 %collective-permute-start.3 = (s32[8,128]{1,0:T(8,128)S(1)}, s32[8,128]{1,0:T(8,128)S(1)}, u32[]{:S(2)}, u32[]{:S(2)}) collective-permute-start(s32[8,128]{1,0:T(8,128)S(1)} %collective-permute-done.2.mine_ref), channel_id=1, source_target_pairs={{0,8},{8,0},{16,24},{24,16},{1,9},{9,1},{17,25},{25,17},{2,10},{10... | collective-permute-start | bytes 12296 | tf_op jit(solution)/shard_map/ppermute | solution.py:447
  14.3 1.6 %shard_map.124.misfit_ref = f32[5,272,128]{2,1,0:T(8,128)S(1)} custom-call(s32[24,128]{1,0:T(8,128)S(1)} %get-tuple-element.36.facts_ref, f32[5,288,128]{2,1,0:T(8,128)S(1)} %get-tuple-element.43.response_ref, f32[16,640]{1,0:T(8,128)S(1)} %copy-done.6, bf16[256,640]{1,0:T(8,128)(2,1)S(1)} %copy-done.5, bf16[64,1024]{1,0:T(8,128)(2,1)S(1)} %collective-permute-done.near_ref, ...), custom_call_target="tpu_custom_call" | custom-call | flops 1724999936 | bytes 1500000 | tf_op jit(solution)/shard_map/pallas_call | solution.py:23
  16.0 2.0 %shard_map.125 = (bf16[256,640]{1,0:T(8,128)(2,1)S(1)}, bf16[528,256]{1,0:T(8,128)(2,1)S(1)}, f32[8,128]{1,0:T(8,128)S(1)}) custom-call(s32[24,128]{1,0:T(8,128)S(1)} %get-tuple-element.36.facts_ref, s32[8,128]{1,0:T(8,128)S(1)} %collective-permute-done.2.mine_ref, s32[8,128]{1,0:T(8,128)S(1)} %collective-permute-done.3.twin_ref, ...), custom_call_target="tpu_custom_call" | custom-call | flops 2875000064 | bytes 2500000 | tf_op jit(solution)/shard_map/pallas_call | solution.py:23
  17.9 1.6 %collective-permute-start.4 = (bf16[528,256]{1,0:T(8,128)(2,1)S(1)}, bf16[528,256]{1,0:T(8,128)(2,1)S(1)}, u32[]{:S(2)}, u32[]{:S(2)}) collective-permute-start(bf16[528,256]{1,0:T(8,128)(2,1)S(1)} %get-tuple-element.46), channel_id=1, source_target_pairs={{0,1},{1,0},{2,3},{3,2},{4,5},{5,4},{6,7},{7,6},{8,10},{9,11},{10,... | collective-permute-start | bytes 811016 | tf_op jit(solution)/shard_map/ppermute | solution.py:456
  19.5 0.4 shard_map.127.slope_ref
  19.9 1.1 %shard_map.126 = (f32[512,256]{1,0:T(8,128)S(1)}, bf16[512,640]{1,0:T(8,128)(2,1)S(1)}, f32[512,640]{1,0:T(8,128)S(1)}) custom-call(bf16[288,1024]{1,0:T(8,128)(2,1)S(1)} %get-tuple-element.38.core_ref, bf16[1024,640]{1,0:T(8,128)(2,1)S(1)} %get-tuple-element.39.effective_ref, bf16[256,640]{1,0:T(8,128)(2,1)S(1)} %get-tuple-element.44.half_ref), custom_call_target="tpu_custom_call" | custom-call | flops 1264999936 | bytes 1100000 | tf_op jit(solution)/shard_map/pallas_call | solution.py:23
  21.0 0.1 collective-permute-start.8
  21.1 3.4 %collective-permute-done.4 = bf16[528,256]{1,0:T(8,128)(2,1)S(1)} collective-permute-done((bf16[528,256]{1,0:T(8,128)(2,1)S(1)}, bf16[528,256]{1,0:T(8,128)(2,1)S(1)}, u32[]{:S(2)}, u32[]{:S(2)}) %collective-permute-start.4) | collective-permute-done | bytes 270368 | tf_op jit(solution)/shard_map/ppermute | solution.py:456
  24.5 0.1 convert_add_fusion.1
  24.6 1.6 %collective-permute-start.7 = (bf16[272,256]{1,0:T(8,128)(2,1)S(1)}, bf16[272,256]{1,0:T(8,128)(2,1)S(1)}, u32[]{:S(2)}, u32[]{:S(2)}) collective-permute-start(bf16[272,256]{1,0:T(8,128)(2,1)S(1)} %pad_maximum_fusion), channel_id=1, source_target_pairs={{0,2},{1,3},{2,0},{3,1},{4,6},{5,7},{6,4},{7,5},{8,9},{9,8},{10,11... | collective-permute-start | bytes 417800 | tf_op jit(solution)/shard_map/ppermute | solution.py:456
  26.3 0.1 convert_add_fusion
  26.5 0.4 collective-permute-start.13
  26.9 2.9 %collective-permute-done.7 = bf16[272,256]{1,0:T(8,128)(2,1)S(1)} collective-permute-done((bf16[272,256]{1,0:T(8,128)(2,1)S(1)}, bf16[272,256]{1,0:T(8,128)(2,1)S(1)}, u32[]{:S(2)}, u32[]{:S(2)}) %collective-permute-start.7) | collective-permute-done | bytes 139296 | tf_op jit(solution)/shard_map/ppermute | solution.py:456
  29.9 2.6 %collective-permute-start.9 = (bf16[144,256]{1,0:T(8,128)(2,1)S(1)}, bf16[144,256]{1,0:T(8,128)(2,1)S(1)}, u32[]{:S(2)}, u32[]{:S(2)}) collective-permute-start(bf16[144,256]{1,0:T(8,128)(2,1)S(1)} %pad_maximum_fusion.1), channel_id=1, source_target_pairs={{0,4},{1,5},{2,6},{3,7},{4,0},{5,1},{6,2},{7,3},{8,12},{9,13},{10,... | collective-permute-start | bytes 221192 | tf_op jit(solution)/shard_map/ppermute | solution.py:456
  32.5 2.7 %collective-permute-done.9.arrived_ref = bf16[144,256]{1,0:T(8,128)(2,1)S(1)} collective-permute-done((bf16[144,256]{1,0:T(8,128)(2,1)S(1)}, bf16[144,256]{1,0:T(8,128)(2,1)S(1)}, u32[]{:S(2)}, u32[]{:S(2)}) %collective-permute-start.9) | collective-permute-done | bytes 73760 | tf_op jit(solution)/shard_map/ppermute | solution.py:456
  35.3 0.1 collective-permute-start.12
  35.3 0.1 collective-permute-start.11
  35.4 1.2 %collective-permute-done.13.arrived_ref = bf16[256,640]{1,0:T(8,128)(2,1)S(1)} collective-permute-done((bf16[256,640]{1,0:T(8,128)(2,1)S(1)}, bf16[256,640]{1,0:T(8,128)(2,1)S(1)}, u32[]{:S(2)}, u32[]{:S(2)}) %collective-permute-start.13) | collective-permute-done | bytes 327712 | tf_op jit(solution)/shard_map/ppermute | solution.py:447
  36.7 1.8 %shard_map.130 = f32[256,640]{1,0:T(8,128)} custom-call(s32[5]{0:T(128)S(1)} %copy-done.7, f32[256,640]{1,0:T(8,128)S(1)} %slice.67.keep_ref, bf16[256,640]{1,0:T(8,128)(2,1)S(1)} %collective-permute-done.13.arrived_ref, f32[16,256]{1,0:T(8,128)S(1)} %constant_dynamic-slice_fusion.gains_ref), custom_call_target="tpu_custom_call" | custom-call | flops 4600000000 | bytes 4000000 | tf_op jit(solution)/shard_map/pallas_call | solution.py:23
  38.5 0.3 shard_map.129.before_ref
  38.8 1.2 %collective-permute-done.11.refs_0_.refs_2_ = bf16[144,256]{1,0:T(8,128)(2,1)S(1)} collective-permute-done((bf16[144,256]{1,0:T(8,128)(2,1)S(1)}, bf16[144,256]{1,0:T(8,128)(2,1)S(1)}, u32[]{:S(2)}, u32[]{:S(2)}) %collective-permute-start.11) | collective-permute-done | bytes 73760 | tf_op jit(solution)/shard_map/ppermute | solution.py:447
  40.0 0.2 shard_map.131.total_ref
  40.3 1.0 %collective-permute-done.14.refs_3_ = bf16[144,256]{1,0:T(8,128)(2,1)S(1)} collective-permute-done((bf16[144,256]{1,0:T(8,128)(2,1)S(1)}, bf16[144,256]{1,0:T(8,128)(2,1)S(1)}, u32[]{:S(2)}, u32[]{:S(2)}) %collective-permute-start.14) | collective-permute-done | bytes 73760 | tf_op jit(solution)/shard_map/ppermute | solution.py:447
  41.3 1.2 %shard_map.132 = (f32[1024,128]{1,0:T(8,128)}, f32[1,1]{1,0:T(1,128)}) custom-call(f32[128,1024]{1,0:T(8,128)S(1)} %shard_map.131.total_ref, bf16[144,256]{1,0:T(8,128)(2,1)S(1)} %shard_map.128.refs_0_, bf16[144,256]{1,0:T(8,128)(2,1)S(1)} %collective-permute-done.12.refs_1_, bf16[144,256]{1,0:T(8,128)(2,1)S(1)} %collective-permute-done.11.refs_0_.refs_2_, ...), custom_call_target="tpu_custom_call" | custom-call | flops 1150000000 | bytes 1000000 | tf_op jit(solution)/shard_map/pallas_call | solution.py:671
  (46 shorter events, 0.3 us)
Async XLA Ops:
  0.6 6.9 %copy-start.1 = (bf16[256,1024]{1,0:T(8,128)(2,1)S(1)}, bf16[256,1024]{1,0:T(8,128)(2,1)}, u32[]{:S(2)}) copy-start(bf16[256,1024]{1,0:T(8,128)(2,1)} %clip_ref.5) | copy-start | bytes 1572868
  0.6 6.7 %copy-start = (bf16[1024,1024]{1,0:T(8,128)(2,1)S(1)}, bf16[1024,1024]{1,0:T(8,128)(2,1)}, u32[]{:S(2)}) copy-start(bf16[1024,1024]{1,0:T(8,128)(2,1)} %point_ref.1) | copy-start | bytes 6291460
  0.7 6.9 %copy-start.4 = (f32[3,1024]{1,0:T(4,128)S(1)}, f32[3,1024]{1,0:T(4,128)}, u32[]{:S(2)}) copy-start(f32[3,1024]{1,0:T(4,128)} %taps_ref.1) | copy-start | bytes 36868
  1.7 10.0 %copy-start.3 = (f32[16,1024]{1,0:T(8,128)S(1)}, f32[16,1024]{1,0:T(8,128)}, u32[]{:S(2)}) copy-start(f32[16,1024]{1,0:T(8,128)} %gains_ref.1) | copy-start | bytes 196612
  1.7 5.8 %collective-permute-start = (bf16[64,1024]{1,0:T(8,128)(2,1)S(1)}, bf16[64,1024]{1,0:T(8,128)(2,1)S(1)}, u32[]{:S(2)}, u32[]{:S(2)}) collective-permute-start(bf16[64,1024]{1,0:T(8,128)(2,1)S(1)} %get-tuple-element.35), channel_id=1, source_target_pairs={{0,8},{8,0},{16,24},{24,16},{1,9},{9,1},{17,25},{25,17},{2,10},{10... | collective-permute-start | bytes 393224 | tf_op jit(solution)/shard_map/ppermute | solution.py:447
  2.2 5.2 %collective-permute-start.1 = (bf16[64,1024]{1,0:T(8,128)(2,1)S(1)}, bf16[64,1024]{1,0:T(8,128)(2,1)S(1)}, u32[]{:S(2)}, u32[]{:S(2)}) collective-permute-start(bf16[64,1024]{1,0:T(8,128)(2,1)S(1)} %get-tuple-element.35), channel_id=1, source_target_pairs={{8,16},{9,17},{10,18},{11,19},{12,20},{13,21},{14,22},{15,23},{16,... | collective-permute-start | bytes 393224 | tf_op jit(solution)/shard_map/ppermute | solution.py:456
  2.9 10.9 %collective-permute-start.2 = (s32[8,128]{1,0:T(8,128)S(1)}, s32[8,128]{1,0:T(8,128)S(1)}, u32[]{:S(2)}, u32[]{:S(2)}) collective-permute-start(s32[8,128]{1,0:T(8,128)S(1)} %get-tuple-element.41), channel_id=1, source_target_pairs={{0,1},{1,0},{2,3},{3,2},{4,5},{5,4},{6,7},{7,6},{9,10},{10,9},{11,... | collective-permute-start | bytes 12296 | tf_op jit(solution)/shard_map/ppermute | solution.py:456
  7.4 4.3 %copy-start.2 = (bf16[1024,640]{1,0:T(8,128)(2,1)S(1)}, bf16[1024,640]{1,0:T(8,128)(2,1)}, u32[]{:S(2)}) copy-start(bf16[1024,640]{1,0:T(8,128)(2,1)} %weight_ref.1) | copy-start | bytes 3932164
  8.1 16.4 %collective-permute-start.5 = (bf16[256,1024]{1,0:T(8,128)(2,1)S(1)}, bf16[256,1024]{1,0:T(8,128)(2,1)S(1)}, u32[]{:S(2)}, u32[]{:S(2)}) collective-permute-start(bf16[256,1024]{1,0:T(8,128)(2,1)S(1)} %get-tuple-element.47.depth_ref.refs_2_), channel_id=1, source_target_pairs={{0,16},{8,24},{16,0},{24,8},{1,17},{9,25},{17,1},{25,9},{2,18},{10... | collective-permute-start | bytes 1572872 | tf_op jit(solution)/shard_map/ppermute | solution.py:447
  11.7 12.8 %collective-permute-start.6 = (bf16[256,1024]{1,0:T(8,128)(2,1)S(1)}, bf16[256,1024]{1,0:T(8,128)(2,1)S(1)}, u32[]{:S(2)}, u32[]{:S(2)}) collective-permute-start(bf16[256,1024]{1,0:T(8,128)(2,1)S(1)} %get-tuple-element.47.depth_ref.refs_2_), channel_id=1, source_target_pairs={{0,8},{8,0},{16,24},{24,16},{1,9},{9,1},{17,25},{25,17},{2,10},{10... | collective-permute-start | bytes 1572872 | tf_op jit(solution)/shard_map/ppermute | solution.py:447
  11.7 2.7 %copy-start.5 = (bf16[256,640]{1,0:T(8,128)(2,1)S(1)}, bf16[256,640]{1,0:T(8,128)(2,1)}, u32[]{:S(2)}) copy-start(bf16[256,640]{1,0:T(8,128)(2,1)} %bold_ref.3) | copy-start | bytes 983044
  11.7 2.6 %copy-start.6 = (f32[16,640]{1,0:T(8,128)S(1)}, f32[16,640]{1,0:T(8,128)}, u32[]{:S(2)}) copy-start(f32[16,640]{1,0:T(8,128)} %hrf_ref.3) | copy-start | bytes 122884
  13.8 2.2 %collective-permute-start.3 = (s32[8,128]{1,0:T(8,128)S(1)}, s32[8,128]{1,0:T(8,128)S(1)}, u32[]{:S(2)}, u32[]{:S(2)}) collective-permute-start(s32[8,128]{1,0:T(8,128)S(1)} %collective-permute-done.2.mine_ref), channel_id=1, source_target_pairs={{0,8},{8,0},{16,24},{24,16},{1,9},{9,1},{17,25},{25,17},{2,10},{10... | collective-permute-start | bytes 12296 | tf_op jit(solution)/shard_map/ppermute | solution.py:447
  17.9 6.5 %collective-permute-start.4 = (bf16[528,256]{1,0:T(8,128)(2,1)S(1)}, bf16[528,256]{1,0:T(8,128)(2,1)S(1)}, u32[]{:S(2)}, u32[]{:S(2)}) collective-permute-start(bf16[528,256]{1,0:T(8,128)(2,1)S(1)} %get-tuple-element.46), channel_id=1, source_target_pairs={{0,1},{1,0},{2,3},{3,2},{4,5},{5,4},{6,7},{7,6},{8,10},{9,11},{10,... | collective-permute-start | bytes 811016 | tf_op jit(solution)/shard_map/ppermute | solution.py:456
  21.0 5.2 %collective-permute-start.8 = (bf16[512,640]{1,0:T(8,128)(2,1)S(1)}, bf16[512,640]{1,0:T(8,128)(2,1)S(1)}, u32[]{:S(2)}, u32[]{:S(2)}) collective-permute-start(bf16[512,640]{1,0:T(8,128)(2,1)S(1)} %get-tuple-element.51), channel_id=1, source_target_pairs={{0,8},{8,0},{16,24},{24,16},{1,9},{9,1},{17,25},{25,17},{2,10},{10... | collective-permute-start | bytes 1966088 | tf_op jit(solution)/shard_map/ppermute | solution.py:447
  24.6 5.1 %collective-permute-start.7 = (bf16[272,256]{1,0:T(8,128)(2,1)S(1)}, bf16[272,256]{1,0:T(8,128)(2,1)S(1)}, u32[]{:S(2)}, u32[]{:S(2)}) collective-permute-start(bf16[272,256]{1,0:T(8,128)(2,1)S(1)} %pad_maximum_fusion), channel_id=1, source_target_pairs={{0,2},{1,3},{2,0},{3,1},{4,6},{5,7},{6,4},{7,5},{8,9},{9,8},{10,11... | collective-permute-start | bytes 417800 | tf_op jit(solution)/shard_map/ppermute | solution.py:456
  26.3 9.0 %collective-permute-start.10 = (bf16[256,1024]{1,0:T(8,128)(2,1)S(1)}, bf16[256,1024]{1,0:T(8,128)(2,1)S(1)}, u32[]{:S(2)}, u32[]{:S(2)}) collective-permute-start(bf16[256,1024]{1,0:T(8,128)(2,1)S(1)} %collective-permute-done.5.refs_1_), channel_id=1, source_target_pairs={{0,8},{8,0},{16,24},{24,16},{1,9},{9,1},{17,25},{25,17},{2,10},{10... | collective-permute-start | bytes 1572872 | tf_op jit(solution)/shard_map/ppermute | solution.py:447
  26.5 10.2 %copy-start.7 = (s32[5]{0:T(128)S(1)}, s32[5]{0:T(128)}, u32[]{:S(2)}) copy-start(s32[5]{0:T(128)} %subject_ref.1) | copy-start | bytes 64
  26.5 10.2 %collective-permute-start.13 = (bf16[256,640]{1,0:T(8,128)(2,1)S(1)}, bf16[256,640]{1,0:T(8,128)(2,1)S(1)}, u32[]{:S(2)}, u32[]{:S(2)}) collective-permute-start(bf16[256,640]{1,0:T(8,128)(2,1)S(1)} %slice.89), channel_id=1, source_target_pairs={{0,16},{8,24},{16,0},{24,8},{1,17},{9,25},{17,1},{25,9},{2,18},{10... | collective-permute-start | bytes 983048 | tf_op jit(solution)/shard_map/ppermute | solution.py:447
  29.9 5.4 %collective-permute-start.9 = (bf16[144,256]{1,0:T(8,128)(2,1)S(1)}, bf16[144,256]{1,0:T(8,128)(2,1)S(1)}, u32[]{:S(2)}, u32[]{:S(2)}) collective-permute-start(bf16[144,256]{1,0:T(8,128)(2,1)S(1)} %pad_maximum_fusion.1), channel_id=1, source_target_pairs={{0,4},{1,5},{2,6},{3,7},{4,0},{5,1},{6,2},{7,3},{8,12},{9,13},{10,... | collective-permute-start | bytes 221192 | tf_op jit(solution)/shard_map/ppermute | solution.py:456
  35.3 3.2 %collective-permute-start.12 = (bf16[144,256]{1,0:T(8,128)(2,1)S(1)}, bf16[144,256]{1,0:T(8,128)(2,1)S(1)}, u32[]{:S(2)}, u32[]{:S(2)}) collective-permute-start(bf16[144,256]{1,0:T(8,128)(2,1)S(1)} %shard_map.128.refs_0_), channel_id=1, source_target_pairs={{0,8},{8,0},{16,24},{24,16},{1,9},{9,1},{17,25},{25,17},{2,10},{10... | collective-permute-start | bytes 221192 | tf_op jit(solution)/shard_map/ppermute | solution.py:447
  35.3 4.7 %collective-permute-start.11 = (bf16[144,256]{1,0:T(8,128)(2,1)S(1)}, bf16[144,256]{1,0:T(8,128)(2,1)S(1)}, u32[]{:S(2)}, u32[]{:S(2)}) collective-permute-start(bf16[144,256]{1,0:T(8,128)(2,1)S(1)} %shard_map.128.refs_0_), channel_id=1, source_target_pairs={{0,16},{8,24},{16,0},{24,8},{1,17},{9,25},{17,1},{25,9},{2,18},{10... | collective-permute-start | bytes 221192 | tf_op jit(solution)/shard_map/ppermute | solution.py:447
  40.0 1.3 %collective-permute-start.14 = (bf16[144,256]{1,0:T(8,128)(2,1)S(1)}, bf16[144,256]{1,0:T(8,128)(2,1)S(1)}, u32[]{:S(2)}, u32[]{:S(2)}) collective-permute-start(bf16[144,256]{1,0:T(8,128)(2,1)S(1)} %collective-permute-done.11.refs_0_.refs_2_), channel_id=1, source_target_pairs={{0,8},{8,0},{16,24},{24,16},{1,9},{9,1},{17,25},{25,17},{2,10},{10... | collective-permute-start | bytes 221192 | tf_op jit(solution)/shard_map/ppermute | solution.py:447
